TPU v7x, 32 devices: a whole 2x2x4 slice. The times are simulated.
32 devices in a mesh: ctx: 8 (over y, x, core), tp: 4 (over z).
Axes of the slice: x: 2, y: 2, z: 4, core: 2. Of those that a mesh axis runs over, the one named last changes fastest.
Arguments:
- gate_inner: bfloat16 [4096, 8192], P('ctx', 'tp'), may hold values from -6 to 6
- gate_outer: bfloat16 [4096, 8192], P('ctx', 'tp'), may hold values from -6 to 6
- hyena_value: bfloat16 [4096, 8192], P('ctx', 'tp'), may hold values from -6 to 6
- decay_rate: float32 [512, 16], P('tp'), may hold values from 1.2207031e-05 to 0.07
- residue: float32 [512, 16], P('tp'), may hold values from -1 to 1
- skip_gain: float32 [8192], P('tp'), may hold values from 0.5 to 1.5
- filter_index: int32 [512], P('tp'), may hold values from 0 to 511
- query_rows: bfloat16 [4096, 8192], P('ctx', 'tp'), may hold values from -8 to 8
- key_rows: bfloat16 [4096, 8192], P('ctx', 'tp'), may hold values from -8 to 8
- value_rows: bfloat16 [4096, 8192], P('ctx', 'tp'), may hold values from -6 to 6
Outputs:
- hyena_output: bfloat16 [4096, 8192], P('ctx', 'tp')
- attention_output: bfloat16 [4096, 8192], P('ctx', 'tp')
All inputs are finite; a program needn't handle non-finite values.
Results may differ from a plain program's by a relative error of at most 0.012.
Values may be sent and summed in bfloat16 or wider, within the bound.
No kernel may reach another device: no remote copies, remote signals or barrier semaphores. Data moves between devices by JAX's collectives and lax.ppermute only.
A program may use at most 192 MiB of HBM per device.

v0:
```python
import functools
import math

import jax
import jax.numpy as jnp
from jax import lax
from jax.experimental import pallas as pl
from jax.experimental.pallas import tpu as pltpu
from jax.sharding import PartitionSpec as P

HEAD_DIM = 128
GROUP = 16
LANES = 128
CHUNK = 128
TILE_GROUPS = LANES // GROUP
STEP_TILES = 4

floor_score = -1e30
LOG2E = 1.4426950408889634


F32 = jnp.float32
BF16 = jnp.bfloat16
LAST = (((1,), (1,)), ((), ()))
FIRST = (((0,), (0,)), ((), ()))
PLAIN = (((1,), (0,)), ((), ()))


def mxu(a, b, dims):
    return lax.dot_general(a, b, dims, preferred_element_type=F32)


def halves(a):
    high = a.astype(BF16)
    return high, (a - high.astype(F32)).astype(BF16)


def iota(shape, axis):
    return lax.broadcasted_iota(jnp.int32, shape, axis)


def same_group():
    rows, cols = iota((LANES, LANES), 0), iota((LANES, LANES), 1)
    return (rows // GROUP) == (cols // GROUP)


def carried_pieces(gate_ref, value_ref, lanes):
    rows = gate_ref.shape[0]
    carried = (gate_ref[:, lanes].astype(F32) * value_ref[:, lanes].astype(F32)).astype(BF16)
    return [carried[b * CHUNK : (b + 1) * CHUNK] for b in range(rows // CHUNK)]


def chunk_states(pieces, rate, step, mask):
    ends = jnp.concatenate(halves(jnp.exp((step - CHUNK) * rate)), axis=1)
    full = mxu(jnp.concatenate(pieces, axis=1), ends, FIRST)
    full = full[:, :LANES] + full[:, LANES:]
    return [
        jnp.where(mask, full[b * LANES : (b + 1) * LANES], 0.0) for b in range(len(pieces))
    ]


def spread_states(states, shrinking):
    state_high, state_low = halves(jnp.concatenate(states, axis=0))
    return mxu(
        jnp.concatenate(shrinking, axis=1),
        jnp.concatenate([state_high, state_high], axis=1),
        LAST,
    ) + mxu(shrinking[0], state_low, LAST)


def local_kernel(gate_ref, outer_ref, value_ref, rate_ref, residue_ref, skip_ref, out_ref, state_ref):
    cols = gate_ref.shape[1]
    step = iota((CHUNK, LANES), 0).astype(F32)
    lane_group = iota((CHUNK, LANES), 1) // GROUP
    zero = jnp.zeros((), BF16)
    shape = (CHUNK, TILE_GROUPS * CHUNK)
    causal = iota(shape, 0) >= iota(shape, 1) % CHUNK
    mask = same_group()
    pick = (iota((GROUP, LANES), 1) % GROUP == iota((GROUP, LANES), 0)).astype(BF16)

    def spread(a):
        return jnp.concatenate(
            [jnp.where(lane_group == g, a, zero) for g in range(TILE_GROUPS)], axis=0
        )

    for w in range(cols // LANES):
        lanes = slice(w * LANES, (w + 1) * LANES)
        rate, residue, skip = rate_ref[w], residue_ref[w], skip_ref[w]
        grown_high, grown_low = halves(jnp.exp((step - CHUNK // 2) * rate))
        shrunk = halves(residue * jnp.exp((CHUNK // 2 - step) * rate))
        from_start = halves(residue * jnp.exp(-step * rate))
        decay = jnp.exp(-CHUNK * rate)
        spread_high = spread(grown_high)
        taps = mxu(
            jnp.concatenate(shrunk, axis=1),
            jnp.concatenate([spread_high, spread_high], axis=1),
            LAST,
        ) + mxu(shrunk[0], spread(grown_low), LAST)
        toeplitz = jnp.where(causal, taps, 0.0).astype(BF16)
        pieces = carried_pieces(gate_ref, value_ref, lanes)
        blocks = jnp.concatenate(
            [
                jnp.concatenate(
                    [jnp.where(lane_group == g, piece, zero) for piece in pieces], axis=1
                )
                for g in range(TILE_GROUPS)
            ],
            axis=0,
        )
        inside = mxu(toeplitz, blocks, PLAIN)
        fresh = chunk_states(pieces, rate, step, mask)
        states = [fresh[0]]
        for more in fresh[1:]:
            states.append(states[-1] * decay + more)
        state_ref[w] = mxu(pick, states[-1].astype(BF16), PLAIN).astype(BF16)
        earlier = spread_states(states[:-1], from_start) if len(pieces) > 1 else None
        for b, piece in enumerate(pieces):
            convolved = inside[:, b * LANES : (b + 1) * LANES] + skip * piece.astype(F32)
            if b:
                convolved += earlier[:, (b - 1) * LANES : b * LANES]
            gate = outer_ref[b * CHUNK : (b + 1) * CHUNK, lanes].astype(F32)
            out_ref[b * CHUNK : (b + 1) * CHUNK, lanes] = gate * convolved


def remote_kernel(part_ref, outer_ref, rate_ref, residue_ref, state_ref, out_ref):
    rows, cols = outer_ref.shape
    chunks = rows // CHUNK
    step = iota((CHUNK, LANES), 0).astype(F32)
    mask = same_group()
    pick = (iota((LANES, GROUP), 0) % GROUP == iota((LANES, GROUP), 1)).astype(BF16)
    for w in range(cols // LANES):
        lanes = slice(w * LANES, (w + 1) * LANES)
        rate, residue = rate_ref[w], residue_ref[w]
        decay = jnp.exp(-CHUNK * rate)
        states = [jnp.where(mask, mxu(pick, state_ref[w], PLAIN), 0.0)]
        while len(states) < chunks:
            states.append(states[-1] * decay)
        earlier = spread_states(states, halves(residue * jnp.exp(-step * rate)))
        for b in range(chunks):
            rows_now = slice(b * CHUNK, (b + 1) * CHUNK)
            gate = outer_ref[rows_now, lanes].astype(F32)
            out_ref[rows_now, lanes] = (
                part_ref[rows_now, lanes] + gate * earlier[:, b * LANES : (b + 1) * LANES]
            ).astype(BF16)


def after(value, *earlier):
    return lax.optimization_barrier((value,) + earlier)[0]


def gathered_modes(decay_rate, residue, filter_index, tiles, tp_size, gate):
    modes = jnp.concatenate([decay_rate, residue], axis=1)
    if gate is not None:
        modes = after(modes, gate)
    filters, width = modes.shape
    if tp_size <= 4:
        place = lax.axis_index("tp")
        others = [modes] + [
            lax.ppermute(modes, "tp", [(i, (i + shift) % tp_size) for i in range(tp_size)])
            for shift in range(1, tp_size)
        ]
        bank = jnp.concatenate(others, axis=0)
        owner = filter_index // filters
        wanted = (place - owner) % tp_size * filters + filter_index % filters
    else:
        bank = lax.all_gather(modes, "tp", axis=0, tiled=True)
        wanted = filter_index
    chooser = (wanted[:, None] == jnp.arange(bank.shape[0], dtype=jnp.int32)[None, :]).astype(F32)
    local = jnp.dot(chooser, bank, precision=lax.Precision.HIGHEST)
    poles = width // 2
    return (
        local[:, :poles].reshape(tiles, 1, LANES),
        local[:, poles:].reshape(tiles, 1, LANES),
    )


def hyena_specs(row_count, tiles):
    group = math.gcd(tiles, STEP_TILES)
    return (
        (tiles // group,),
        pl.BlockSpec((row_count, group * LANES), lambda i: (0, i)),
        pl.BlockSpec((group, 1, LANES), lambda i: (i, 0, 0)),
        pl.BlockSpec((group, GROUP, LANES), lambda i: (i, 0, 0)),
    )


def local_part(gate_inner, gate_outer, hyena_value, rate, residue, skip_gain):
    row_count, chan_count = gate_inner.shape
    tiles = chan_count // LANES
    grid, wide, row, small = hyena_specs(row_count, tiles)
    return pl.pallas_call(
        local_kernel,
        grid=grid,
        in_specs=[wide, wide, wide, row, row, row],
        out_specs=[wide, small],
        out_shape=[
            jax.ShapeDtypeStruct((row_count, chan_count), F32),
            jax.ShapeDtypeStruct((tiles, GROUP, LANES), BF16),
        ],
        cost_estimate=pl.CostEstimate(
            flops=2 * row_count * chan_count * LANES * 16,
            bytes_accessed=10 * row_count * chan_count,
            transcendentals=row_count * chan_count,
        ),
        name="local_part",
    )(gate_inner, gate_outer, hyena_value, rate, residue, skip_gain.reshape(tiles, 1, LANES))


def remote_part(part, gate_outer, rate, residue, incoming):
    row_count, chan_count = gate_outer.shape
    tiles = chan_count // LANES
    grid, wide, row, small = hyena_specs(row_count, tiles)
    return pl.pallas_call(
        remote_kernel,
        grid=grid,
        in_specs=[wide, wide, row, row, small],
        out_specs=wide,
        out_shape=jax.ShapeDtypeStruct((row_count, chan_count), BF16),
        cost_estimate=pl.CostEstimate(
            flops=2 * row_count * chan_count * LANES * 3,
            bytes_accessed=8 * row_count * chan_count,
            transcendentals=row_count * chan_count // 4,
        ),
        name="remote_part",
    )(part, gate_outer, rate, residue, incoming)


def shifted(a, by, ctx_size):
    return lax.ppermute(a.astype(BF16), "ctx", [(i, i + by) for i in range(ctx_size - by)])


def scan_join(value, moved, base, rate, rows):
    for k, more in enumerate(moved, 1):
        value = value + more.astype(F32) * jnp.exp(-rate * float(rows * base * k))
    return value


def hyena_plain(gate_inner, gate_outer, hyena_value, modes, skip_gain, ctx_size):
    rate, residue = modes
    rows = gate_inner.shape[0]
    part, state = local_part(gate_inner, gate_outer, hyena_value, rate, residue, skip_gain)
    incoming = shifted(state, 1, ctx_size).astype(F32)
    base = 1
    while base < ctx_size - 1:
        incoming = scan_join(incoming, [shifted(incoming, base, ctx_size)], base, rate, rows)
        base *= 2
    return remote_part(part, gate_outer, rate, residue, incoming.astype(BF16))


def pack_kernel(place_ref, q_ref, k_ref, v_ref, *refs, spots, heads, head):
    outs, (buf, sems, out_sems) = refs[: len(spots)], refs[len(spots) :]
    place = place_ref[0]
    reads = []
    for n, r in enumerate(spots):
        column = pl.multiple_of(((place ^ r) * heads + head) * HEAD_DIM, HEAD_DIM)
        for j, source in enumerate((q_ref, k_ref, v_ref)):
            reads.append(
                pltpu.make_async_copy(
                    source.at[:, pl.ds(column, HEAD_DIM)],
                    buf.at[n, :, pl.ds(j * HEAD_DIM, HEAD_DIM)],
                    sems.at[n, j],
                )
            )
            reads[-1].start()
    writes = []
    for n in range(len(spots)):
        for j in range(3):
            reads[3 * n + j].wait()
        writes.append(pltpu.make_async_copy(buf.at[n], outs[n], out_sems.at[n]))
        writes[-1].start()
    for write in writes:
        write.wait()


def pack(place, arrays, spots, heads, head):
    rows = arrays[0].shape[0]
    shape = (rows, 3 * HEAD_DIM)
    return pl.pallas_call(
        functools.partial(pack_kernel, spots=spots, heads=heads, head=head),
        in_specs=[pl.BlockSpec(memory_space=pltpu.SMEM)]
        + [pl.BlockSpec(memory_space=pl.ANY)] * 3,
        out_specs=[pl.BlockSpec(memory_space=pl.ANY)] * len(spots),
        out_shape=[jax.ShapeDtypeStruct(shape, BF16)] * len(spots),
        scratch_shapes=[
            pltpu.VMEM((len(spots),) + shape, BF16),
            pltpu.SemaphoreType.DMA((len(spots), 3)),
            pltpu.SemaphoreType.DMA((len(spots),)),
        ],
        cost_estimate=pl.CostEstimate(
            flops=0, bytes_accessed=4 * len(spots) * rows * 3 * HEAD_DIM, transcendentals=0
        ),
        name="pack",
    )(place, *arrays)


def flash_kernel(place_ref, *refs, blocks):
    sources, outs = refs[:blocks], refs[blocks : 2 * blocks]
    q_buf, k_buf, v_buf, vt_buf, o_buf, s_buf, m_buf, l_buf, acc_buf, sems = refs[2 * blocks :]
    rows = sources[0].shape[0]
    place = place_ref[0]
    copies = []
    for r in range(blocks):
        spot = pl.ds(pl.multiple_of((place ^ r) * rows, rows), rows)
        for j, target in enumerate((q_buf, k_buf, v_buf)):
            copies.append(
                pltpu.make_async_copy(
                    sources[r].at[:, pl.ds(j * HEAD_DIM, HEAD_DIM)], target.at[spot], sems.at[r, j]
                )
            )
            copies[-1].start()
    for copy in copies:
        copy.wait()
    for j in range(blocks):
        vt_buf[:, j * rows : (j + 1) * rows] = v_buf[j * rows : (j + 1) * rows, :].T
    scale = LOG2E / math.sqrt(HEAD_DIM)

    def score(i, j):
        keys = slice(j * rows, (j + 1) * rows)
        scores = mxu(k_buf[keys, :], q_buf[i * rows : (i + 1) * rows, :], LAST)
        if i == j:
            shape = (rows, rows)
            scores = jnp.where(iota(shape, 1) >= iota(shape, 0), scores, floor_score)
        s_buf[i % 2, keys, :] = scores
        m_buf[i % 2] = jnp.maximum(
            m_buf[i % 2], jnp.max(scores.reshape(rows // 8, 8, rows), axis=0)
        )

    def weigh(i, j, top):
        keys = slice(j * rows, (j + 1) * rows)
        weights = jnp.exp2(s_buf[i % 2, keys, :] * scale - top)
        l_buf[...] += jnp.sum(weights.reshape(rows // 8, 8, rows), axis=0)
        acc_buf[...] += mxu(vt_buf[:, keys], weights.astype(BF16), PLAIN)

    m_buf[...] = jnp.full(m_buf.shape, floor_score, F32)
    score(0, 0)
    for i in range(blocks):
        top = jnp.max(m_buf[i % 2], axis=0, keepdims=True) * scale
        m_buf[(i + 1) % 2] = jnp.full((8, rows), floor_score, F32)
        acc_buf[...] = jnp.zeros(acc_buf.shape, F32)
        l_buf[...] = jnp.zeros(l_buf.shape, F32)
        for j in range(i + 2):
            if j <= i:
                weigh(i, j, top)
            if i + 1 < blocks:
                score(i + 1, j)
        total = jnp.sum(l_buf[...], axis=0, keepdims=True)
        o_buf[i * rows : (i + 1) * rows, :] = (acc_buf[...] / total).T.astype(BF16)
    writes = []
    for r in range(blocks):
        spot = pl.ds(pl.multiple_of((place ^ r) * rows, rows), rows)
        writes.append(pltpu.make_async_copy(o_buf.at[spot], outs[r], sems.at[r, 0]))
        writes[-1].start()
    for write in writes:
        write.wait()


def flash(place, sources):
    blocks, rows = len(sources), sources[0].shape[0]
    total = blocks * rows
    pairs = total * (total + rows) // 2
    return pl.pallas_call(
        functools.partial(flash_kernel, blocks=blocks),
        in_specs=[pl.BlockSpec(memory_space=pltpu.SMEM)]
        + [pl.BlockSpec(memory_space=pl.ANY)] * blocks,
        out_specs=[pl.BlockSpec(memory_space=pl.ANY)] * blocks,
        out_shape=[jax.ShapeDtypeStruct((rows, HEAD_DIM), BF16)] * blocks,
        scratch_shapes=[
            pltpu.VMEM((total, HEAD_DIM), BF16),
            pltpu.VMEM((total, HEAD_DIM), BF16),
            pltpu.VMEM((total, HEAD_DIM), BF16),
            pltpu.VMEM((HEAD_DIM, total), BF16),
            pltpu.VMEM((total, HEAD_DIM), BF16),
            pltpu.VMEM((2, total, rows), F32),
            pltpu.VMEM((2, 8, rows), F32),
            pltpu.VMEM((8, rows), F32),
            pltpu.VMEM((HEAD_DIM, rows), F32),
            pltpu.SemaphoreType.DMA((blocks, 3)),
        ],
        compiler_params=pltpu.CompilerParams(vmem_limit_bytes=48 << 20),
        cost_estimate=pl.CostEstimate(
            flops=8 * pairs * HEAD_DIM, bytes_accessed=8 * total * HEAD_DIM, transcendentals=pairs
        ),
        name="flash",
    )(place, *sources)


def join_kernel(place_ref, *refs, blocks, heads):
    parts, out_ref = refs[: blocks * heads], refs[blocks * heads]
    sems = refs[blocks * heads + 1]
    place = place_ref[0]
    copies = []
    for r in range(blocks):
        for h in range(heads):
            column = pl.multiple_of(((place ^ r) * heads + h) * HEAD_DIM, HEAD_DIM)
            copies.append(
                pltpu.make_async_copy(
                    parts[r * heads + h], out_ref.at[:, pl.ds(column, HEAD_DIM)], sems.at[r, h]
                )
            )
            copies[-1].start()
    for copy in copies:
        copy.wait()


def exchange_body(
    gate_inner,
    gate_outer,
    hyena_value,
    decay_rate,
    residue,
    skip_gain,
    filter_index,
    query_rows,
    key_rows,
    value_rows,
    mesh,
):
    ctx_size, tp_size = mesh.shape["ctx"], mesh.shape["tp"]
    row_count, width_cols = query_rows.shape
    heads = width_cols // HEAD_DIM // ctx_size
    place = lax.axis_index("ctx")
    where = place.astype(jnp.int32).reshape(1)
    tiles = gate_inner.shape[1] // LANES

    def swap(a, r):
        return lax.ppermute(a, "ctx", [(i, i ^ r) for i in range(ctx_size)])

    order = sorted(range(1, ctx_size), key=lambda r: (-bin(r >> 1).count("1"), r)) + [0]
    span = math.isqrt(ctx_size - 1) + (math.isqrt(ctx_size - 1) ** 2 < ctx_size - 1)
    got, backs = [], []
    sent = query_rows
    for h in range(heads):
        if h == 1:
            rate, local_residue = gathered_modes(
                decay_rate, residue, filter_index, tiles, tp_size, sent
            )
            part, state = local_part(
                gate_inner, gate_outer, hyena_value, rate, local_residue, skip_gain
            )
            near = [shifted(state, k, ctx_size) for k in range(1, span + 1)]
            sent = state
        packed = pack(where, (after(query_rows, sent), key_rows, value_rows), order, heads, h)
        sent = packed[0]
        mine = [None] * ctx_size
        for piece, r in zip(packed, order):
            mine[r] = swap(piece, r) if r else piece
        got.append(mine)
    for h in range(heads):
        results = flash(where, got[h])
        if h == 0:
            near = lax.optimization_barrier(tuple(near) + (results[0],))[:-1]
            incoming = scan_join(near[0].astype(F32), near[1:], 1, rate, row_count)
            far = [
                shifted(incoming, span * k, ctx_size)
                for k in range(1, span + 1)
                if span * k < ctx_size
            ]
        backs.append([swap(a, r) if r else a for r, a in enumerate(results)])
    far = lax.optimization_barrier(tuple(far) + (results[0],))[:-1]
    incoming = scan_join(incoming, far, span, rate, row_count).astype(BF16)
    hyena_output = remote_part(part, gate_outer, rate, local_residue, incoming)
    parts = [backs[h][r] for r in range(ctx_size) for h in range(heads)]
    parts[0] = after(parts[0], hyena_output)
    attention_output = pl.pallas_call(
        functools.partial(join_kernel, blocks=ctx_size, heads=heads),
        in_specs=[pl.BlockSpec(memory_space=pltpu.SMEM)]
        + [pl.BlockSpec(memory_space=pltpu.VMEM)] * len(parts),
        out_specs=pl.BlockSpec(memory_space=pl.ANY),
        out_shape=jax.ShapeDtypeStruct((row_count, width_cols), BF16),
        scratch_shapes=[pltpu.SemaphoreType.DMA((ctx_size, heads))],
        name="join",
    )(where, *parts)
    return (hyena_output, attention_output)


def row_steps(folded, members, handler, span_rows):
    total_rows = members[0].shape[0]
    block_count = total_rows // span_rows
    stacked = tuple(
        (member.reshape((block_count, span_rows) + member.shape[1:]) for member in members)
    )

    def advance(running, element):
        position, pieces = element
        return (handler(running, pieces, position * span_rows), None)

    folded, _ = lax.scan(advance, folded, (jnp.arange(block_count, dtype=jnp.int32), stacked))
    return folded


def gather_attention(query_rows, key_rows, value_rows):
    row_count, width_cols = query_rows.shape
    head_count = width_cols // HEAD_DIM
    queries = query_rows.reshape(row_count, head_count, HEAD_DIM)
    score_scale = 1.0 / math.sqrt(HEAD_DIM)
    own_rows = lax.axis_index("ctx") * row_count + jnp.arange(row_count, dtype=jnp.int32)

    def attend(folded, pieces, first_row):
        running_max, running_total, summed = folded
        block_rows = pieces[0].shape[0]
        keys_now = pieces[0].reshape(block_rows, head_count, HEAD_DIM)
        values_now = pieces[1].reshape(block_rows, head_count, HEAD_DIM)
        scores = (
            jnp.einsum("thd,shd->hts", queries, keys_now, preferred_element_type=jnp.float32)
            * score_scale
        )
        key_positions = first_row + jnp.arange(block_rows, dtype=jnp.int32)
        visible = own_rows[:, None] >= key_positions[None, :]
        masked = jnp.where(visible[None], scores, floor_score)
        newest = jnp.maximum(running_max, jnp.max(masked, axis=2))
        weights = jnp.where(visible[None], jnp.exp(scores - newest[:, :, None]), 0.0)
        factor = jnp.exp(running_max - newest)
        running_total = running_total * factor + jnp.sum(weights, axis=2)
        update = jnp.einsum(
            "hts,shd->thd",
            weights.astype(jnp.bfloat16),
            values_now,
            preferred_element_type=jnp.float32,
        )
        summed = summed * factor.T[:, :, None] + update
        return (newest, running_total, summed)

    initial = (
        jnp.full((head_count, row_count), floor_score, jnp.float32),
        jnp.zeros((head_count, row_count), jnp.float32),
        jnp.zeros((row_count, head_count, HEAD_DIM), jnp.float32),
    )
    _, running_total, summed = row_steps(
        initial,
        (
            lax.all_gather(key_rows, "ctx", axis=0, tiled=True),
            lax.all_gather(value_rows, "ctx", axis=0, tiled=True),
        ),
        attend,
        512,
    )
    result = summed / running_total.T[:, :, None]
    return result.reshape(row_count, width_cols).astype(jnp.bfloat16)


def solution(mesh):
    ctx_size, tp_size = mesh.shape["ctx"], mesh.shape["tp"]

    def body(
        gate_inner,
        gate_outer,
        hyena_value,
        decay_rate,
        residue,
        skip_gain,
        filter_index,
        query_rows,
        key_rows,
        value_rows,
    ):
        head_count = query_rows.shape[1] // HEAD_DIM
        if head_count % ctx_size == 0 and ctx_size & (ctx_size - 1) == 0 and ctx_size > 2:
            return exchange_body(
                gate_inner,
                gate_outer,
                hyena_value,
                decay_rate,
                residue,
                skip_gain,
                filter_index,
                query_rows,
                key_rows,
                value_rows,
                mesh,
            )
        attention_output = gather_attention(query_rows, key_rows, value_rows)
        tiles = gate_inner.shape[1] // LANES
        modes = gathered_modes(decay_rate, residue, filter_index, tiles, tp_size, None)
        hyena_output = hyena_plain(gate_inner, gate_outer, hyena_value, modes, skip_gain, ctx_size)
        return (hyena_output, attention_output)

    in_specs = (
        P("ctx", "tp"),
        P("ctx", "tp"),
        P("ctx", "tp"),
        P("tp", None),
        P("tp", None),
        P("tp"),
        P("tp"),
        P("ctx", "tp"),
        P("ctx", "tp"),
        P("ctx", "tp"),
    )
    out_specs = (P("ctx", "tp"), P("ctx", "tp"))
    return jax.shard_map(body, mesh=mesh, in_specs=in_specs, out_specs=out_specs, check_vma=False)
```

profile of v0, /device:TPU:0, one launch (start us, length us, event | category | flops | bytes accessed | tf_op | source)
XLA Modules:
  0.0 167.6 jit_solution(9173142805925033532)
XLA Ops:
  0.6 0.7 pad_maximum_fusion
  1.4 3.3 %pack.2 = (bf16[512,384]{1,0:T(8,128)(2,1)}, bf16[512,384]{1,0:T(8,128)(2,1)}, bf16[512,384]{1,0:T(8,128)(2,1)}, bf16[512,384]{1,0:T(8,128)(2,1)}, bf16[512,384]...) custom-call(s32[1]{0:T(128)} %bitcast.place_ref, ...), custom_call_target="tpu_custom_call" | custom-call | bytes 6291456 | tf_op jit(solution)/shard_map/pack/pallas_call | solution.py:278
  4.6 5.1 %collective-permute-start.2 = (f32[128,32]{0,1:T(8,128)S(1)}, f32[128,32]{0,1:T(8,128)S(1)}, u32[]{:S(2)}, u32[]{:S(2)}) collective-permute-start(f32[128,32]{0,1:T(8,128)S(1)} %pad_maximum_fusion), channel_id=1, source_target_pairs={{0,3},{1,0},{2,1},{3,2},{4,7},{5,4},{6,5},{7,6},{8,11},{9,8},{10,9... | collective-permute-start | bytes 49160 | tf_op jit(solution)/shard_map/ppermute | solution.py:159
  9.8 1.0 collective-permute-start
  10.8 1.5 collective-permute-start.7
  12.7 1.7 collective-permute-done.1
  14.4 1.5 collective-permute-start.9
  16.2 0.6 multiply_exponential_fusion.1
  17.0 0.7 reshape.64
  17.7 0.7 reshape.63
  18.4 15.8 %local_part.1 = (f32[512,2048]{1,0:T(8,128)}, bf16[16,16,128]{2,1,0:T(8,128)(2,1)}) custom-call(bf16[512,2048]{1,0:T(8,128)(2,1)} %gate_ref.1, bf16[512,2048]{1,0:T(8,128)(2,1)} %outer_ref.3, bf16[512,2048]{1,0:T(8,128)(2,1)} %value_ref.1, f32[16,1,128]{2,1,0:T(1,128)} %bitcast.8, f32[16,1,128]{2,1,0:T(1,128)} %bitcast.6, f32[16,1,128]{2,1,0:T(1,128)} %bitcast.10), custom_call_target="tpu_custom_call" | custom-call | flops 4294967296 | bytes 10485760 | tf_op jit(solution)/shard_map/local_part/pallas_call | solution.py:191
  34.3 1.3 collective-permute-start.5
  35.6 2.2 %collective-permute-done.5 = bf16[16,16,128]{2,1,0:T(8,128)(2,1)S(1)} collective-permute-done((bf16[16,16,128]{2,1,0:T(8,128)(2,1)}, bf16[16,16,128]{2,1,0:T(8,128)(2,1)S(1)}, u32[]{:S(2)}, u32[]{:S(2)}) %collective-permute-start.5) | collective-permute-done | bytes 65568 | tf_op jit(solution)/shard_map/ppermute | solution.py:229
  37.8 3.3 %collective-permute-start.4 = (bf16[16,16,128]{2,1,0:T(8,128)(2,1)}, bf16[16,16,128]{2,1,0:T(8,128)(2,1)S(1)}, u32[]{:S(2)}, u32[]{:S(2)}) collective-permute-start(bf16[16,16,128]{2,1,0:T(8,128)(2,1)} %get-tuple-element.49), channel_id=1, source_target_pairs={{0,8},{4,12},{8,16},{12,20},{16,24},{20,28},{1,9},{5,13},{9,17},{1... | collective-permute-start | bytes 196616 | tf_op jit(solution)/shard_map/ppermute | solution.py:229
  41.2 2.7 %collective-permute-done.4 = bf16[16,16,128]{2,1,0:T(8,128)(2,1)S(1)} collective-permute-done((bf16[16,16,128]{2,1,0:T(8,128)(2,1)}, bf16[16,16,128]{2,1,0:T(8,128)(2,1)S(1)}, u32[]{:S(2)}, u32[]{:S(2)}) %collective-permute-start.4) | collective-permute-done | bytes 65568 | tf_op jit(solution)/shard_map/ppermute | solution.py:229
  43.9 2.3 %collective-permute-start.3 = (bf16[16,16,128]{2,1,0:T(8,128)(2,1)}, bf16[16,16,128]{2,1,0:T(8,128)(2,1)S(1)}, u32[]{:S(2)}, u32[]{:S(2)}) collective-permute-start(bf16[16,16,128]{2,1,0:T(8,128)(2,1)} %get-tuple-element.49), channel_id=1, source_target_pairs={{0,4},{4,8},{8,12},{12,16},{16,20},{20,24},{24,28},{1,5},{5,9},{9,... | collective-permute-start | bytes 196616 | tf_op jit(solution)/shard_map/ppermute | solution.py:229
  46.2 0.9 collective-permute-done.3
  47.1 5.0 %collective-permute-start.10 = (bf16[512,384]{1,0:T(8,128)(2,1)}, bf16[512,384]{1,0:T(8,128)(2,1)S(1)}, u32[]{:S(2)}, u32[]{:S(2)}) collective-permute-start(bf16[512,384]{1,0:T(8,128)(2,1)} %get-tuple-element.55), channel_id=1, source_target_pairs={{0,20},{4,16},{8,28},{12,24},{16,4},{20,0},{24,12},{28,8},{1,21},{... | collective-permute-start | bytes 1179656 | tf_op jit(solution)/shard_map/ppermute | solution.py:426
  52.1 2.2 %collective-permute-start.12 = (bf16[512,384]{1,0:T(8,128)(2,1)}, bf16[512,384]{1,0:T(8,128)(2,1)S(1)}, u32[]{:S(2)}, u32[]{:S(2)}) collective-permute-start(bf16[512,384]{1,0:T(8,128)(2,1)} %get-tuple-element.56), channel_id=1, source_target_pairs={{0,28},{4,24},{8,20},{12,16},{16,12},{20,8},{24,4},{28,0},{1,29},{... | collective-permute-start | bytes 1179656 | tf_op jit(solution)/shard_map/ppermute | solution.py:426
  54.3 3.3 %pack.3 = (bf16[512,384]{1,0:T(8,128)(2,1)}, bf16[512,384]{1,0:T(8,128)(2,1)}, bf16[512,384]{1,0:T(8,128)(2,1)}, bf16[512,384]{1,0:T(8,128)(2,1)}, bf16[512,384]...) custom-call(s32[1]{0:T(128)} %bitcast.place_ref, ...), custom_call_target="tpu_custom_call" | custom-call | bytes 6291456 | tf_op jit(solution)/shard_map/pack/pallas_call | solution.py:278
  57.6 4.1 %collective-permute-start.11 = (bf16[512,384]{1,0:T(8,128)(2,1)}, bf16[512,384]{1,0:T(8,128)(2,1)}, u32[]{:S(2)}, u32[]{:S(2)}) collective-permute-start(bf16[512,384]{1,0:T(8,128)(2,1)} %get-tuple-element.46), channel_id=1, source_target_pairs={{0,24},{4,28},{8,16},{12,20},{16,8},{20,12},{24,0},{28,4},{1,25},{... | collective-permute-start | bytes 1179656 | tf_op jit(solution)/shard_map/ppermute | solution.py:426
  61.8 0.7 copy.18
  62.5 0.9 exp.45
  63.4 0.7 copy.19
  64.1 0.9 exp.47
  65.0 12.1 %collective-permute-done.10.refs_5_ = bf16[512,384]{1,0:T(8,128)(2,1)S(1)} collective-permute-done((bf16[512,384]{1,0:T(8,128)(2,1)}, bf16[512,384]{1,0:T(8,128)(2,1)S(1)}, u32[]{:S(2)}, u32[]{:S(2)}) %collective-permute-start.10) | collective-permute-done | bytes 393248 | tf_op jit(solution)/shard_map/ppermute | solution.py:426
  77.1 4.1 %collective-permute-start.17 = (bf16[512,384]{1,0:T(8,128)(2,1)}, bf16[512,384]{1,0:T(8,128)(2,1)S(1)}, u32[]{:S(2)}, u32[]{:S(2)}) collective-permute-start(bf16[512,384]{1,0:T(8,128)(2,1)} %get-tuple-element.65), channel_id=1, source_target_pairs={{0,12},{4,8},{8,4},{12,0},{16,28},{20,24},{24,20},{28,16},{1,13},{... | collective-permute-start | bytes 1179656 | tf_op jit(solution)/shard_map/ppermute | solution.py:426
  81.9 2.2 %collective-permute-start.20 = (bf16[512,384]{1,0:T(8,128)(2,1)}, bf16[512,384]{1,0:T(8,128)(2,1)S(1)}, u32[]{:S(2)}, u32[]{:S(2)}) collective-permute-start(bf16[512,384]{1,0:T(8,128)(2,1)} %get-tuple-element.68), channel_id=1, source_target_pairs={{0,24},{4,28},{8,16},{12,20},{16,8},{20,12},{24,0},{28,4},{1,25},{... | collective-permute-start | bytes 1179656 | tf_op jit(solution)/shard_map/ppermute | solution.py:426
  84.1 1.6 collective-permute-start.21
  85.6 15.9 %flash.2 = (bf16[512,128]{1,0:T(8,128)(2,1)S(1)}, bf16[512,128]{1,0:T(8,128)(2,1)S(1)}, bf16[512,128]{1,0:T(8,128)(2,1)S(1)}, bf16[512,128]{1,0:T(8,128)(2,1)S(1...) custom-call(s32[1]{0:T(128)} %bitcast.place_ref, ...), custom_call_target="tpu_custom_call" | custom-call | flops 9663676416 | bytes 4194304 | tf_op jit(solution)/shard_map/flash/pallas_call | solution.py:361
  102.3 2.3 %collective-permute-start.14 = (bf16[16,16,128]{2,1,0:T(8,128)(2,1)S(1)}, bf16[16,16,128]{2,1,0:T(8,128)(2,1)S(1)}, u32[]{:S(2)}, u32[]{:S(2)}) collective-permute-start(bf16[16,16,128]{2,1,0:T(8,128)(2,1)S(1)} %fusion.2), channel_id=1, source_target_pairs={{0,24},{4,28},{1,25},{5,29},{2,26},{6,30},{3,27},{7,31}} | collective-permute-start | bytes 196616 | tf_op jit(solution)/shard_map/ppermute | solution.py:229
  104.5 5.7 %collective-permute-done.18.refs_4_ = bf16[512,384]{1,0:T(8,128)(2,1)S(1)} collective-permute-done((bf16[512,384]{1,0:T(8,128)(2,1)}, bf16[512,384]{1,0:T(8,128)(2,1)S(1)}, u32[]{:S(2)}, u32[]{:S(2)}) %collective-permute-start.18) | collective-permute-done | bytes 393248 | tf_op jit(solution)/shard_map/ppermute | solution.py:426
  110.3 1.7 %collective-permute-start.13 = (bf16[16,16,128]{2,1,0:T(8,128)(2,1)S(1)}, bf16[16,16,128]{2,1,0:T(8,128)(2,1)S(1)}, u32[]{:S(2)}, u32[]{:S(2)}) collective-permute-start(bf16[16,16,128]{2,1,0:T(8,128)(2,1)S(1)} %fusion.2), channel_id=1, source_target_pairs={{0,12},{4,16},{8,20},{12,24},{16,28},{1,13},{5,17},{9,21},{13,25},... | collective-permute-start | bytes 196616 | tf_op jit(solution)/shard_map/ppermute | solution.py:229
  112.0 5.0 %collective-permute-done.19.refs_5_ = bf16[512,384]{1,0:T(8,128)(2,1)S(1)} collective-permute-done((bf16[512,384]{1,0:T(8,128)(2,1)}, bf16[512,384]{1,0:T(8,128)(2,1)S(1)}, u32[]{:S(2)}, u32[]{:S(2)}) %collective-permute-start.19) | collective-permute-done | bytes 393248 | tf_op jit(solution)/shard_map/ppermute | solution.py:426
  117.1 1.6 collective-permute-start.24
  118.9 2.4 %collective-permute-start.28 = (bf16[512,128]{1,0:T(8,128)(2,1)S(1)}, bf16[512,128]{1,0:T(8,128)(2,1)S(1)}, u32[]{:S(2)}, u32[]{:S(2)}) collective-permute-start(bf16[512,128]{1,0:T(8,128)(2,1)S(1)} %get-tuple-element.80), channel_id=1, source_target_pairs={{0,16},{4,20},{8,24},{12,28},{16,0},{20,4},{24,8},{28,12},{1,17},{... | collective-permute-start | bytes 393224 | tf_op jit(solution)/shard_map/ppermute | solution.py:426
  121.3 14.8 %flash.3 = (bf16[512,128]{1,0:T(8,128)(2,1)S(1)}, bf16[512,128]{1,0:T(8,128)(2,1)S(1)}, bf16[512,128]{1,0:T(8,128)(2,1)S(1)}, bf16[512,128]{1,0:T(8,128)(2,1)S(1...) custom-call(s32[1]{0:T(128)} %bitcast.place_ref, ...), custom_call_target="tpu_custom_call" | custom-call | flops 9663676416 | bytes 4194304 | tf_op jit(solution)/shard_map/flash/pallas_call | solution.py:361
  136.1 0.7 copy-done.1
  136.8 2.6 %collective-permute-start.32 = (bf16[512,128]{1,0:T(8,128)(2,1)}, bf16[512,128]{1,0:T(8,128)(2,1)S(1)}, u32[]{:S(2)}, u32[]{:S(2)}) collective-permute-start(bf16[512,128]{1,0:T(8,128)(2,1)} %get-tuple-element.84), channel_id=1, source_target_pairs={{0,24},{4,28},{8,16},{12,20},{16,8},{20,12},{24,0},{28,4},{1,25},{... | collective-permute-start | bytes 393224 | tf_op jit(solution)/shard_map/ppermute | solution.py:426
  139.9 1.6 collective-permute-start.25
  141.9 6.2 %collective-permute-done.30.refs_10_ = bf16[512,128]{1,0:T(8,128)(2,1)S(1)} collective-permute-done((bf16[512,128]{1,0:T(8,128)(2,1)}, bf16[512,128]{1,0:T(8,128)(2,1)S(1)}, u32[]{:S(2)}, u32[]{:S(2)}) %collective-permute-start.30) | collective-permute-done | bytes 131104 | tf_op jit(solution)/shard_map/ppermute | solution.py:426
  148.1 1.6 collective-permute-start.27
  149.7 1.5 collective-permute-start.31
  151.7 2.4 %collective-permute-start.35 = (bf16[512,128]{1,0:T(8,128)(2,1)S(1)}, bf16[512,128]{1,0:T(8,128)(2,1)S(1)}, u32[]{:S(2)}, u32[]{:S(2)}) collective-permute-start(bf16[512,128]{1,0:T(8,128)(2,1)S(1)} %get-tuple-element.87), channel_id=1, source_target_pairs={{0,28},{4,24},{8,20},{12,16},{16,12},{20,8},{24,4},{28,0},{1,29},{... | collective-permute-start | bytes 393224 | tf_op jit(solution)/shard_map/ppermute | solution.py:426
  154.1 0.7 add_convert_fusion.state_ref
  154.8 7.8 %remote_part.1 = bf16[512,2048]{1,0:T(8,128)(2,1)} custom-call(f32[512,2048]{1,0:T(8,128)} %get-tuple-element.48.part_ref, bf16[512,2048]{1,0:T(8,128)(2,1)} %outer_ref.3, f32[16,1,128]{2,1,0:T(1,128)} %bitcast.9, f32[16,1,128]{2,1,0:T(1,128)} %bitcast.7, bf16[16,16,128]{2,1,0:T(8,128)(2,1)} %add_convert_fusion.state_ref), custom_call_target="tpu_custom_call" | custom-call | flops 805306368 | bytes 8388608 | tf_op jit(solution)/shard_map/remote_part/pallas_call | solution.py:213
  163.7 0.6 copy-done.26
  164.3 3.0 %join.1 = bf16[512,2048]{1,0:T(8,128)(2,1)} custom-call(s32[1]{0:T(128)} %bitcast.place_ref, bf16[512,128]{1,0:T(8,128)(2,1)} %copy-done, bf16[512,128]{1,0:T(8,128)(2,1)} %copy-done.1, bf16[512,128]{1,0:T(8,128)(2,1)} %copy-done.13, bf16[512,128]{1,0:T(8,128)(2,1)} %copy-done.20, bf16[512,128]{1,0:T(8,128)(2,1)} %copy-done.14, bf16[512,128]{1,0:T(8,128)(2,1)} %copy-done.21, ...), custom_call_target="tpu_custom_call" | custom-call | tf_op jit(solution)/shard_map/join/pallas_call | solution.py:464
  (109 shorter events, 5.1 us)
Async XLA Ops:
  4.6 7.7 %collective-permute-start.2 = (f32[128,32]{0,1:T(8,128)S(1)}, f32[128,32]{0,1:T(8,128)S(1)}, u32[]{:S(2)}, u32[]{:S(2)}) collective-permute-start(f32[128,32]{0,1:T(8,128)S(1)} %pad_maximum_fusion), channel_id=1, source_target_pairs={{0,3},{1,0},{2,1},{3,2},{4,7},{5,4},{6,5},{7,6},{8,11},{9,8},{10,9... | collective-permute-start | bytes 49160 | tf_op jit(solution)/shard_map/ppermute | solution.py:159
  9.8 4.6 %collective-permute-start.1 = (f32[128,32]{0,1:T(8,128)S(1)}, f32[128,32]{0,1:T(8,128)S(1)}, u32[]{:S(2)}, u32[]{:S(2)}) collective-permute-start(f32[128,32]{0,1:T(8,128)S(1)} %pad_maximum_fusion), channel_id=1, source_target_pairs={{0,2},{1,3},{2,0},{3,1},{4,6},{5,7},{6,4},{7,5},{8,10},{9,11},{10,... | collective-permute-start | bytes 49160 | tf_op jit(solution)/shard_map/ppermute | solution.py:159
  9.8 6.2 %collective-permute-start = (f32[128,32]{0,1:T(8,128)S(1)}, f32[128,32]{0,1:T(8,128)S(1)}, u32[]{:S(2)}, u32[]{:S(2)}) collective-permute-start(f32[128,32]{0,1:T(8,128)S(1)} %pad_maximum_fusion), channel_id=1, source_target_pairs={{0,1},{1,2},{2,3},{3,0},{4,5},{5,6},{6,7},{7,4},{8,9},{9,10},{10,1... | collective-permute-start | bytes 49160 | tf_op jit(solution)/shard_map/ppermute | solution.py:159
  10.8 41.3 %collective-permute-start.6 = (bf16[512,384]{1,0:T(8,128)(2,1)}, bf16[512,384]{1,0:T(8,128)(2,1)S(1)}, u32[]{:S(2)}, u32[]{:S(2)}) collective-permute-start(bf16[512,384]{1,0:T(8,128)(2,1)} %get-tuple-element.51), channel_id=1, source_target_pairs={{0,4},{4,0},{8,12},{12,8},{16,20},{20,16},{24,28},{28,24},{1,5},{5... | collective-permute-start | bytes 1179656 | tf_op jit(solution)/shard_map/ppermute | solution.py:426
  10.8 46.8 %collective-permute-start.7 = (bf16[512,384]{1,0:T(8,128)(2,1)}, bf16[512,384]{1,0:T(8,128)(2,1)S(1)}, u32[]{:S(2)}, u32[]{:S(2)}) collective-permute-start(bf16[512,384]{1,0:T(8,128)(2,1)} %get-tuple-element.52), channel_id=1, source_target_pairs={{0,8},{4,12},{8,0},{12,4},{16,24},{20,28},{24,16},{28,20},{1,9},{5... | collective-permute-start | bytes 1179656 | tf_op jit(solution)/shard_map/ppermute | solution.py:426
  12.3 49.4 %collective-permute-start.8 = (bf16[512,384]{1,0:T(8,128)(2,1)}, bf16[512,384]{1,0:T(8,128)(2,1)S(1)}, u32[]{:S(2)}, u32[]{:S(2)}) collective-permute-start(bf16[512,384]{1,0:T(8,128)(2,1)} %get-tuple-element.53), channel_id=1, source_target_pairs={{0,12},{4,8},{8,4},{12,0},{16,28},{20,24},{24,20},{28,16},{1,13},{... | collective-permute-start | bytes 1179656 | tf_op jit(solution)/shard_map/ppermute | solution.py:426
  14.4 47.3 %collective-permute-start.9 = (bf16[512,384]{1,0:T(8,128)(2,1)}, bf16[512,384]{1,0:T(8,128)(2,1)S(1)}, u32[]{:S(2)}, u32[]{:S(2)}) collective-permute-start(bf16[512,384]{1,0:T(8,128)(2,1)} %get-tuple-element.54), channel_id=1, source_target_pairs={{0,16},{4,20},{8,24},{12,28},{16,0},{20,4},{24,8},{28,12},{1,17},{... | collective-permute-start | bytes 1179656 | tf_op jit(solution)/shard_map/ppermute | solution.py:426
  34.3 3.5 %collective-permute-start.5 = (bf16[16,16,128]{2,1,0:T(8,128)(2,1)}, bf16[16,16,128]{2,1,0:T(8,128)(2,1)S(1)}, u32[]{:S(2)}, u32[]{:S(2)}) collective-permute-start(bf16[16,16,128]{2,1,0:T(8,128)(2,1)} %get-tuple-element.49), channel_id=1, source_target_pairs={{0,12},{4,16},{8,20},{12,24},{16,28},{1,13},{5,17},{9,21},{13,25},... | collective-permute-start | bytes 196616 | tf_op jit(solution)/shard_map/ppermute | solution.py:229
  37.8 6.0 %collective-permute-start.4 = (bf16[16,16,128]{2,1,0:T(8,128)(2,1)}, bf16[16,16,128]{2,1,0:T(8,128)(2,1)S(1)}, u32[]{:S(2)}, u32[]{:S(2)}) collective-permute-start(bf16[16,16,128]{2,1,0:T(8,128)(2,1)} %get-tuple-element.49), channel_id=1, source_target_pairs={{0,8},{4,12},{8,16},{12,20},{16,24},{20,28},{1,9},{5,13},{9,17},{1... | collective-permute-start | bytes 196616 | tf_op jit(solution)/shard_map/ppermute | solution.py:229
  43.9 3.2 %collective-permute-start.3 = (bf16[16,16,128]{2,1,0:T(8,128)(2,1)}, bf16[16,16,128]{2,1,0:T(8,128)(2,1)S(1)}, u32[]{:S(2)}, u32[]{:S(2)}) collective-permute-start(bf16[16,16,128]{2,1,0:T(8,128)(2,1)} %get-tuple-element.49), channel_id=1, source_target_pairs={{0,4},{4,8},{8,12},{12,16},{16,20},{20,24},{24,28},{1,5},{5,9},{9,... | collective-permute-start | bytes 196616 | tf_op jit(solution)/shard_map/ppermute | solution.py:229
  47.1 30.0 %collective-permute-start.10 = (bf16[512,384]{1,0:T(8,128)(2,1)}, bf16[512,384]{1,0:T(8,128)(2,1)S(1)}, u32[]{:S(2)}, u32[]{:S(2)}) collective-permute-start(bf16[512,384]{1,0:T(8,128)(2,1)} %get-tuple-element.55), channel_id=1, source_target_pairs={{0,20},{4,16},{8,28},{12,24},{16,4},{20,0},{24,12},{28,8},{1,21},{... | collective-permute-start | bytes 1179656 | tf_op jit(solution)/shard_map/ppermute | solution.py:426
  52.1 33.5 %copy-start.2 = (bf16[512,384]{1,0:T(8,128)(2,1)S(1)}, bf16[512,384]{1,0:T(8,128)(2,1)}, u32[]{:S(2)}) copy-start(bf16[512,384]{1,0:T(8,128)(2,1)} %get-tuple-element.50.refs_0_) | copy-start | bytes 1179652
  52.1 29.1 %collective-permute-start.12 = (bf16[512,384]{1,0:T(8,128)(2,1)}, bf16[512,384]{1,0:T(8,128)(2,1)S(1)}, u32[]{:S(2)}, u32[]{:S(2)}) collective-permute-start(bf16[512,384]{1,0:T(8,128)(2,1)} %get-tuple-element.56), channel_id=1, source_target_pairs={{0,28},{4,24},{8,20},{12,16},{16,12},{20,8},{24,4},{28,0},{1,29},{... | collective-permute-start | bytes 1179656 | tf_op jit(solution)/shard_map/ppermute | solution.py:426
  57.6 23.7 %collective-permute-start.11 = (bf16[512,384]{1,0:T(8,128)(2,1)}, bf16[512,384]{1,0:T(8,128)(2,1)}, u32[]{:S(2)}, u32[]{:S(2)}) collective-permute-start(bf16[512,384]{1,0:T(8,128)(2,1)} %get-tuple-element.46), channel_id=1, source_target_pairs={{0,24},{4,28},{8,16},{12,20},{16,8},{20,12},{24,0},{28,4},{1,25},{... | collective-permute-start | bytes 1179656 | tf_op jit(solution)/shard_map/ppermute | solution.py:426
  61.7 20.2 %collective-permute-start.15 = (bf16[512,384]{1,0:T(8,128)(2,1)}, bf16[512,384]{1,0:T(8,128)(2,1)S(1)}, u32[]{:S(2)}, u32[]{:S(2)}) collective-permute-start(bf16[512,384]{1,0:T(8,128)(2,1)} %get-tuple-element.63), channel_id=1, source_target_pairs={{0,4},{4,0},{8,12},{12,8},{16,20},{20,16},{24,28},{28,24},{1,5},{5... | collective-permute-start | bytes 1179656 | tf_op jit(solution)/shard_map/ppermute | solution.py:426
  61.7 22.4 %collective-permute-start.16 = (bf16[512,384]{1,0:T(8,128)(2,1)}, bf16[512,384]{1,0:T(8,128)(2,1)S(1)}, u32[]{:S(2)}, u32[]{:S(2)}) collective-permute-start(bf16[512,384]{1,0:T(8,128)(2,1)} %get-tuple-element.64), channel_id=1, source_target_pairs={{0,8},{4,12},{8,0},{12,4},{16,24},{20,28},{24,16},{28,20},{1,9},{5... | collective-permute-start | bytes 1179656 | tf_op jit(solution)/shard_map/ppermute | solution.py:426
  77.1 25.1 %collective-permute-start.17 = (bf16[512,384]{1,0:T(8,128)(2,1)}, bf16[512,384]{1,0:T(8,128)(2,1)S(1)}, u32[]{:S(2)}, u32[]{:S(2)}) collective-permute-start(bf16[512,384]{1,0:T(8,128)(2,1)} %get-tuple-element.65), channel_id=1, source_target_pairs={{0,12},{4,8},{8,4},{12,0},{16,28},{20,24},{24,20},{28,16},{1,13},{... | collective-permute-start | bytes 1179656 | tf_op jit(solution)/shard_map/ppermute | solution.py:426
  81.2 29.1 %collective-permute-start.18 = (bf16[512,384]{1,0:T(8,128)(2,1)}, bf16[512,384]{1,0:T(8,128)(2,1)S(1)}, u32[]{:S(2)}, u32[]{:S(2)}) collective-permute-start(bf16[512,384]{1,0:T(8,128)(2,1)} %get-tuple-element.66), channel_id=1, source_target_pairs={{0,16},{4,20},{8,24},{12,28},{16,0},{20,4},{24,8},{28,12},{1,17},{... | collective-permute-start | bytes 1179656 | tf_op jit(solution)/shard_map/ppermute | solution.py:426
  81.2 35.8 %collective-permute-start.19 = (bf16[512,384]{1,0:T(8,128)(2,1)}, bf16[512,384]{1,0:T(8,128)(2,1)S(1)}, u32[]{:S(2)}, u32[]{:S(2)}) collective-permute-start(bf16[512,384]{1,0:T(8,128)(2,1)} %get-tuple-element.67), channel_id=1, source_target_pairs={{0,20},{4,16},{8,28},{12,24},{16,4},{20,0},{24,12},{28,8},{1,21},{... | collective-permute-start | bytes 1179656 | tf_op jit(solution)/shard_map/ppermute | solution.py:426
  81.9 35.3 %collective-permute-start.20 = (bf16[512,384]{1,0:T(8,128)(2,1)}, bf16[512,384]{1,0:T(8,128)(2,1)S(1)}, u32[]{:S(2)}, u32[]{:S(2)}) collective-permute-start(bf16[512,384]{1,0:T(8,128)(2,1)} %get-tuple-element.68), channel_id=1, source_target_pairs={{0,24},{4,28},{8,16},{12,20},{16,8},{20,12},{24,0},{28,4},{1,25},{... | collective-permute-start | bytes 1179656 | tf_op jit(solution)/shard_map/ppermute | solution.py:426
  84.1 34.6 %collective-permute-start.21 = (bf16[512,384]{1,0:T(8,128)(2,1)}, bf16[512,384]{1,0:T(8,128)(2,1)S(1)}, u32[]{:S(2)}, u32[]{:S(2)}) collective-permute-start(bf16[512,384]{1,0:T(8,128)(2,1)} %get-tuple-element.69), channel_id=1, source_target_pairs={{0,28},{4,24},{8,20},{12,16},{16,12},{20,8},{24,4},{28,0},{1,29},{... | collective-permute-start | bytes 1179656 | tf_op jit(solution)/shard_map/ppermute | solution.py:426
  85.6 16.6 %copy-start.11 = (bf16[16,16,128]{2,1,0:T(8,128)(2,1)S(1)}, bf16[16,16,128]{2,1,0:T(8,128)(2,1)}, u32[]{:S(2)}) copy-start(bf16[16,16,128]{2,1,0:T(8,128)(2,1)} %copy-done.10) | copy-start | bytes 196612
  85.6 35.6 %copy-start.3 = (bf16[512,384]{1,0:T(8,128)(2,1)S(1)}, bf16[512,384]{1,0:T(8,128)(2,1)}, u32[]{:S(2)}) copy-start(bf16[512,384]{1,0:T(8,128)(2,1)} %get-tuple-element.62.refs_0_) | copy-start | bytes 1179652
  102.3 16.6 %collective-permute-start.14 = (bf16[16,16,128]{2,1,0:T(8,128)(2,1)S(1)}, bf16[16,16,128]{2,1,0:T(8,128)(2,1)S(1)}, u32[]{:S(2)}, u32[]{:S(2)}) collective-permute-start(bf16[16,16,128]{2,1,0:T(8,128)(2,1)S(1)} %fusion.2), channel_id=1, source_target_pairs={{0,24},{4,28},{1,25},{5,29},{2,26},{6,30},{3,27},{7,31}} | collective-permute-start | bytes 196616 | tf_op jit(solution)/shard_map/ppermute | solution.py:229
  110.3 26.5 %collective-permute-start.13 = (bf16[16,16,128]{2,1,0:T(8,128)(2,1)S(1)}, bf16[16,16,128]{2,1,0:T(8,128)(2,1)S(1)}, u32[]{:S(2)}, u32[]{:S(2)}) collective-permute-start(bf16[16,16,128]{2,1,0:T(8,128)(2,1)S(1)} %fusion.2), channel_id=1, source_target_pairs={{0,12},{4,16},{8,20},{12,24},{16,28},{1,13},{5,17},{9,21},{13,25},... | collective-permute-start | bytes 196616 | tf_op jit(solution)/shard_map/ppermute | solution.py:229
  117.0 19.8 %collective-permute-start.22 = (bf16[512,128]{1,0:T(8,128)(2,1)S(1)}, bf16[512,128]{1,0:T(8,128)(2,1)S(1)}, u32[]{:S(2)}, u32[]{:S(2)}) collective-permute-start(bf16[512,128]{1,0:T(8,128)(2,1)S(1)} %get-tuple-element.74), channel_id=1, source_target_pairs={{0,4},{4,0},{8,12},{12,8},{16,20},{20,16},{24,28},{28,24},{1,5},{5... | collective-permute-start | bytes 393224 | tf_op jit(solution)/shard_map/ppermute | solution.py:426
  117.1 22.3 %collective-permute-start.24 = (bf16[512,128]{1,0:T(8,128)(2,1)S(1)}, bf16[512,128]{1,0:T(8,128)(2,1)S(1)}, u32[]{:S(2)}, u32[]{:S(2)}) collective-permute-start(bf16[512,128]{1,0:T(8,128)(2,1)S(1)} %get-tuple-element.76), channel_id=1, source_target_pairs={{0,8},{4,12},{8,0},{12,4},{16,24},{20,28},{24,16},{28,20},{1,9},{5... | collective-permute-start | bytes 393224 | tf_op jit(solution)/shard_map/ppermute | solution.py:426
  118.7 20.9 %collective-permute-start.26 = (bf16[512,128]{1,0:T(8,128)(2,1)S(1)}, bf16[512,128]{1,0:T(8,128)(2,1)S(1)}, u32[]{:S(2)}, u32[]{:S(2)}) collective-permute-start(bf16[512,128]{1,0:T(8,128)(2,1)S(1)} %get-tuple-element.78), channel_id=1, source_target_pairs={{0,12},{4,8},{8,4},{12,0},{16,28},{20,24},{24,20},{28,16},{1,13},{... | collective-permute-start | bytes 393224 | tf_op jit(solution)/shard_map/ppermute | solution.py:426
  118.9 21.0 %collective-permute-start.28 = (bf16[512,128]{1,0:T(8,128)(2,1)S(1)}, bf16[512,128]{1,0:T(8,128)(2,1)S(1)}, u32[]{:S(2)}, u32[]{:S(2)}) collective-permute-start(bf16[512,128]{1,0:T(8,128)(2,1)S(1)} %get-tuple-element.80), channel_id=1, source_target_pairs={{0,16},{4,20},{8,24},{12,28},{16,0},{20,4},{24,8},{28,12},{1,17},{... | collective-permute-start | bytes 393224 | tf_op jit(solution)/shard_map/ppermute | solution.py:426
  121.3 20.2 %copy-start.28 = (f32[128,16]{0,1:T(8,128)S(1)}, f32[128,16]{0,1:T(8,128)}, u32[]{:S(2)}) copy-start(f32[128,16]{0,1:T(8,128)} %get-tuple-element.88) | copy-start | bytes 24580
  121.3 20.4 %copy-start.27 = (f32[128,16]{0,1:T(8,128)S(1)}, f32[128,16]{0,1:T(8,128)}, u32[]{:S(2)}) copy-start(f32[128,16]{0,1:T(8,128)} %get-tuple-element.90) | copy-start | bytes 24580
  121.3 32.8 %copy-start.6 = (bf16[16,16,128]{2,1,0:T(8,128)(2,1)S(1)}, bf16[16,16,128]{2,1,0:T(8,128)(2,1)}, u32[]{:S(2)}) copy-start(bf16[16,16,128]{2,1,0:T(8,128)(2,1)} %copy-done.4) | copy-start | bytes 196612
  121.3 32.8 %copy-start.9 = (bf16[16,16,128]{2,1,0:T(8,128)(2,1)S(1)}, bf16[16,16,128]{2,1,0:T(8,128)(2,1)}, u32[]{:S(2)}) copy-start(bf16[16,16,128]{2,1,0:T(8,128)(2,1)} %copy-done.7) | copy-start | bytes 196612
  121.3 32.8 %copy-start.12 = (bf16[16,16,128]{2,1,0:T(8,128)(2,1)S(1)}, bf16[16,16,128]{2,1,0:T(8,128)(2,1)}, u32[]{:S(2)}) copy-start(bf16[16,16,128]{2,1,0:T(8,128)(2,1)} %copy-done.10) | copy-start | bytes 196612
  136.8 11.3 %collective-permute-start.30 = (bf16[512,128]{1,0:T(8,128)(2,1)}, bf16[512,128]{1,0:T(8,128)(2,1)S(1)}, u32[]{:S(2)}, u32[]{:S(2)}) collective-permute-start(bf16[512,128]{1,0:T(8,128)(2,1)} %get-tuple-element.82), channel_id=1, source_target_pairs={{0,20},{4,16},{8,28},{12,24},{16,4},{20,0},{24,12},{28,8},{1,21},{... | collective-permute-start | bytes 393224 | tf_op jit(solution)/shard_map/ppermute | solution.py:426
  136.8 25.8 %copy-start.13 = (bf16[512,128]{1,0:T(8,128)(2,1)}, bf16[512,128]{1,0:T(8,128)(2,1)S(1)}, u32[]{:S(2)}) copy-start(bf16[512,128]{1,0:T(8,128)(2,1)S(1)} %collective-permute-done.22.refs_2_) | copy-start | bytes 393220
  136.8 12.9 %collective-permute-start.32 = (bf16[512,128]{1,0:T(8,128)(2,1)}, bf16[512,128]{1,0:T(8,128)(2,1)S(1)}, u32[]{:S(2)}, u32[]{:S(2)}) collective-permute-start(bf16[512,128]{1,0:T(8,128)(2,1)} %get-tuple-element.84), channel_id=1, source_target_pairs={{0,24},{4,28},{8,16},{12,20},{16,8},{20,12},{24,0},{28,4},{1,25},{... | collective-permute-start | bytes 393224 | tf_op jit(solution)/shard_map/ppermute | solution.py:426
  139.4 23.2 %copy-start.14 = (bf16[512,128]{1,0:T(8,128)(2,1)}, bf16[512,128]{1,0:T(8,128)(2,1)S(1)}, u32[]{:S(2)}) copy-start(bf16[512,128]{1,0:T(8,128)(2,1)S(1)} %collective-permute-done.24.refs_4_) | copy-start | bytes 393220
  139.4 10.3 %collective-permute-start.34 = (bf16[512,128]{1,0:T(8,128)(2,1)}, bf16[512,128]{1,0:T(8,128)(2,1)S(1)}, u32[]{:S(2)}, u32[]{:S(2)}) collective-permute-start(bf16[512,128]{1,0:T(8,128)(2,1)} %get-tuple-element.86), channel_id=1, source_target_pairs={{0,28},{4,24},{8,20},{12,16},{16,12},{20,8},{24,4},{28,0},{1,29},{... | collective-permute-start | bytes 393224 | tf_op jit(solution)/shard_map/ppermute | solution.py:426
  139.6 23.0 %copy-start.15 = (bf16[512,128]{1,0:T(8,128)(2,1)}, bf16[512,128]{1,0:T(8,128)(2,1)S(1)}, u32[]{:S(2)}) copy-start(bf16[512,128]{1,0:T(8,128)(2,1)S(1)} %collective-permute-done.26.refs_6_) | copy-start | bytes 393220
  139.6 11.6 %collective-permute-start.23 = (bf16[512,128]{1,0:T(8,128)(2,1)S(1)}, bf16[512,128]{1,0:T(8,128)(2,1)S(1)}, u32[]{:S(2)}, u32[]{:S(2)}) collective-permute-start(bf16[512,128]{1,0:T(8,128)(2,1)S(1)} %get-tuple-element.75), channel_id=1, source_target_pairs={{0,4},{4,0},{8,12},{12,8},{16,20},{20,16},{24,28},{28,24},{1,5},{5... | collective-permute-start | bytes 393224 | tf_op jit(solution)/shard_map/ppermute | solution.py:426
  139.9 22.7 %copy-start.16 = (bf16[512,128]{1,0:T(8,128)(2,1)}, bf16[512,128]{1,0:T(8,128)(2,1)S(1)}, u32[]{:S(2)}) copy-start(bf16[512,128]{1,0:T(8,128)(2,1)S(1)} %collective-permute-done.28.refs_8_) | copy-start | bytes 393220
  139.9 11.8 %collective-permute-start.25 = (bf16[512,128]{1,0:T(8,128)(2,1)S(1)}, bf16[512,128]{1,0:T(8,128)(2,1)S(1)}, u32[]{:S(2)}, u32[]{:S(2)}) collective-permute-start(bf16[512,128]{1,0:T(8,128)(2,1)S(1)} %get-tuple-element.77), channel_id=1, source_target_pairs={{0,8},{4,12},{8,0},{12,4},{16,24},{20,28},{24,16},{28,20},{1,9},{5... | collective-permute-start | bytes 393224 | tf_op jit(solution)/shard_map/ppermute | solution.py:426
  148.1 14.6 %collective-permute-start.27 = (bf16[512,128]{1,0:T(8,128)(2,1)S(1)}, bf16[512,128]{1,0:T(8,128)(2,1)S(1)}, u32[]{:S(2)}, u32[]{:S(2)}) collective-permute-start(bf16[512,128]{1,0:T(8,128)(2,1)S(1)} %get-tuple-element.79), channel_id=1, source_target_pairs={{0,12},{4,8},{8,4},{12,0},{16,28},{20,24},{24,20},{28,16},{1,13},{... | collective-permute-start | bytes 393224 | tf_op jit(solution)/shard_map/ppermute | solution.py:426
  149.7 13.0 %collective-permute-start.29 = (bf16[512,128]{1,0:T(8,128)(2,1)S(1)}, bf16[512,128]{1,0:T(8,128)(2,1)S(1)}, u32[]{:S(2)}, u32[]{:S(2)}) collective-permute-start(bf16[512,128]{1,0:T(8,128)(2,1)S(1)} %get-tuple-element.81), channel_id=1, source_target_pairs={{0,16},{4,20},{8,24},{12,28},{16,0},{20,4},{24,8},{28,12},{1,17},{... | collective-permute-start | bytes 393224 | tf_op jit(solution)/shard_map/ppermute | solution.py:426
  149.7 13.2 %collective-permute-start.31 = (bf16[512,128]{1,0:T(8,128)(2,1)S(1)}, bf16[512,128]{1,0:T(8,128)(2,1)S(1)}, u32[]{:S(2)}, u32[]{:S(2)}) collective-permute-start(bf16[512,128]{1,0:T(8,128)(2,1)S(1)} %get-tuple-element.83), channel_id=1, source_target_pairs={{0,20},{4,16},{8,28},{12,24},{16,4},{20,0},{24,12},{28,8},{1,21},{... | collective-permute-start | bytes 393224 | tf_op jit(solution)/shard_map/ppermute | solution.py:426
  151.3 11.7 %collective-permute-start.33 = (bf16[512,128]{1,0:T(8,128)(2,1)S(1)}, bf16[512,128]{1,0:T(8,128)(2,1)S(1)}, u32[]{:S(2)}, u32[]{:S(2)}) collective-permute-start(bf16[512,128]{1,0:T(8,128)(2,1)S(1)} %get-tuple-element.85), channel_id=1, source_target_pairs={{0,24},{4,28},{8,16},{12,20},{16,8},{20,12},{24,0},{28,4},{1,25},{... | collective-permute-start | bytes 393224 | tf_op jit(solution)/shard_map/ppermute | solution.py:426
  151.7 11.3 %collective-permute-start.35 = (bf16[512,128]{1,0:T(8,128)(2,1)S(1)}, bf16[512,128]{1,0:T(8,128)(2,1)S(1)}, u32[]{:S(2)}, u32[]{:S(2)}) collective-permute-start(bf16[512,128]{1,0:T(8,128)(2,1)S(1)} %get-tuple-element.87), channel_id=1, source_target_pairs={{0,28},{4,24},{8,20},{12,16},{16,12},{20,8},{24,4},{28,0},{1,29},{... | collective-permute-start | bytes 393224 | tf_op jit(solution)/shard_map/ppermute | solution.py:426
  (18 other events, 138.9 us)
where the time goes:
time: 168 us
  Pallas kernels  63.9 us (38%)
  starting transfers between devices  55.3 us (33%)
  waiting for transfers between devices  36.9 us (22%)
  local copies, waits for them, and re-layouts  7.91 us (5%)
  other arithmetic  2.12 us (1%)
    ppermute x28, starting transfers between devices, swap(): return lax.ppermute(a, 'ctx', [(i, i ^ r) for i in range(ctx_size)])  38.2 us
    pallas_call x2, Pallas kernels, flash(): pl.pallas_call(functools.partial(flash_kernel, blocks=blocks), in_specs=[...  30.7 us
    ppermute x28, waiting for transfers between devices, swap(): return lax.ppermute(a, 'ctx', [(i, i ^ r) for i in range(ctx_size)])  29.4 us
    pallas_call x1, Pallas kernels, local_part(): pl.pallas_call(local_kernel, grid=grid, in_specs=[wide, wide, wide, row,...  15.8 us
    ppermute x5, starting transfers between devices, shifted(): lax.ppermute(a.astype(BF16), 'ctx', [(i, i + by) for i in range(ctx_size...  11 us
    pallas_call x1, Pallas kernels, remote_part(): pl.pallas_call(remote_kernel, grid=grid, in_specs=[wide, wide, row, row,...  7.77 us
    pallas_call x2, Pallas kernels, pack(): pl.pallas_call(functools.partial(pack_kernel, spots=spots, heads=heads, h...  6.53 us
    ppermute x3, starting transfers between devices, gathered_modes(): lax.ppermute(modes, 'tp', [(i, (i + shift) % tp_size) for i in range(tp_s...  6.14 us
  transfers between devices with their start and end apart: 36, of which 9 were waited for; matrix products, arithmetic and copies ran while one was open for 4% of the time, Pallas kernels for 34%

commit v1 on v0

--- a/solution.py
+++ b/solution.py
@@ -14,6 +14,7 @@
 CHUNK = 128
 TILE_GROUPS = LANES // GROUP
 STEP_TILES = 4
+SPAN = 4
 
 floor_score = -1e30
 LOG2E = 1.4426950408889634
@@ -122,26 +123,57 @@
             out_ref[b * CHUNK : (b + 1) * CHUNK, lanes] = gate * convolved
 
 
-def remote_kernel(part_ref, outer_ref, rate_ref, residue_ref, state_ref, out_ref):
+def gather_kernel(place_ref, rate_ref, *refs):
+    nears, (before_ref, total_ref) = refs[:SPAN], refs[SPAN:]
+    spot = place_ref[0] % SPAN
+    rows = place_ref[1].astype(F32)
+    rate = rate_ref[...]
+    before = jnp.zeros(before_ref.shape, F32)
+    total = jnp.zeros(before_ref.shape, F32)
+    for r, near in enumerate(nears):
+        value = near[...].astype(F32)
+        j = spot ^ r
+        ahead = jnp.maximum(spot - 1 - j, 0).astype(F32) * rows
+        faded = value * jnp.exp(-rate * ahead)
+        before += jnp.where(j < spot, faded, 0.0)
+        total += value * jnp.exp(-rate * ((SPAN - 1 - j).astype(F32) * rows))
+    before_ref[...] = before
+    total_ref[...] = total.astype(BF16)
+
+
+def gather_states(where, rate, nears):
+    shape = nears[0].shape
+    return pl.pallas_call(
+        gather_kernel,
+        in_specs=[pl.BlockSpec(memory_space=pltpu.SMEM)]
+        + [pl.BlockSpec(memory_space=pltpu.VMEM)] * (1 + SPAN),
+        out_specs=[pl.BlockSpec(memory_space=pltpu.VMEM)] * 2,
+        out_shape=[jax.ShapeDtypeStruct(shape, F32), jax.ShapeDtypeStruct(shape, BF16)],
+        name="gather_states",
+    )(where, rate, *nears)
+
+
+def remote_kernel(
+    place_ref, part_ref, outer_ref, rate_ref, residue_ref, before_ref, other_ref, out_ref
+):
     rows, cols = outer_ref.shape
-    chunks = rows // CHUNK
-    step = iota((CHUNK, LANES), 0).astype(F32)
+    step = iota((rows, LANES), 0).astype(F32)
     mask = same_group()
     pick = (iota((LANES, GROUP), 0) % GROUP == iota((LANES, GROUP), 1)).astype(BF16)
+    spot = (place_ref[0] % SPAN).astype(F32) * rows
+    upper = place_ref[0] >= SPAN
     for w in range(cols // LANES):
         lanes = slice(w * LANES, (w + 1) * LANES)
-        rate, residue = rate_ref[w], residue_ref[w]
-        decay = jnp.exp(-CHUNK * rate)
-        states = [jnp.where(mask, mxu(pick, state_ref[w], PLAIN), 0.0)]
-        while len(states) < chunks:
-            states.append(states[-1] * decay)
-        earlier = spread_states(states, halves(residue * jnp.exp(-step * rate)))
-        for b in range(chunks):
-            rows_now = slice(b * CHUNK, (b + 1) * CHUNK)
-            gate = outer_ref[rows_now, lanes].astype(F32)
-            out_ref[rows_now, lanes] = (
-                part_ref[rows_now, lanes] + gate * earlier[:, b * LANES : (b + 1) * LANES]
-            ).astype(BF16)
+        rate = rate_ref[w]
+        faded = other_ref[w].astype(F32) * jnp.exp(-rate * spot)
+        incoming = (before_ref[w] + jnp.where(upper, faded, 0.0)).astype(BF16)
+        state = jnp.where(mask, mxu(pick, incoming, PLAIN), 0.0).astype(BF16)
+        shrinking = halves(residue_ref[w] * jnp.exp(-step * rate))
+        earlier = mxu(
+            jnp.concatenate(shrinking, axis=1), jnp.concatenate([state, state], axis=1), LAST
+        )
+        gate = outer_ref[:, lanes].astype(F32)
+        out_ref[:, lanes] = (part_ref[:, lanes] + gate * earlier).astype(BF16)
 
 
 def after(value, *earlier):
@@ -206,14 +238,14 @@
     )(gate_inner, gate_outer, hyena_value, rate, residue, skip_gain.reshape(tiles, 1, LANES))
 
 
-def remote_part(part, gate_outer, rate, residue, incoming):
+def remote_part(where, part, gate_outer, rate, residue, before, other):
     row_count, chan_count = gate_outer.shape
     tiles = chan_count // LANES
     grid, wide, row, small = hyena_specs(row_count, tiles)
     return pl.pallas_call(
         remote_kernel,
         grid=grid,
-        in_specs=[wide, wide, row, row, small],
+        in_specs=[pl.BlockSpec(memory_space=pltpu.SMEM), wide, wide, row, row, small, small],
         out_specs=wide,
         out_shape=jax.ShapeDtypeStruct((row_count, chan_count), BF16),
         cost_estimate=pl.CostEstimate(
@@ -222,7 +254,7 @@
             transcendentals=row_count * chan_count // 4,
         ),
         name="remote_part",
-    )(part, gate_outer, rate, residue, incoming)
+    )(where, part, gate_outer, rate, residue, before, other)
 
 
 def shifted(a, by, ctx_size):
@@ -244,7 +276,10 @@
     while base < ctx_size - 1:
         incoming = scan_join(incoming, [shifted(incoming, base, ctx_size)], base, rate, rows)
         base *= 2
-    return remote_part(part, gate_outer, rate, residue, incoming.astype(BF16))
+    where = jnp.zeros((1,), jnp.int32)
+    return remote_part(
+        where, part, gate_outer, rate, residue, incoming, jnp.zeros_like(state)
+    )
 
 
 def pack_kernel(place_ref, q_ref, k_ref, v_ref, *refs, spots, heads, head):
@@ -298,20 +333,24 @@
     q_buf, k_buf, v_buf, vt_buf, o_buf, s_buf, m_buf, l_buf, acc_buf, sems = refs[2 * blocks :]
     rows = sources[0].shape[0]
     place = place_ref[0]
-    copies = []
+    targets = (q_buf, k_buf, v_buf)
+
+    def fetch(r, block, j):
+        spot = pl.ds(pl.multiple_of(block * rows, rows), rows)
+        return pltpu.make_async_copy(
+            sources[r].at[:, pl.ds(j * HEAD_DIM, HEAD_DIM)], targets[j].at[spot], sems.at[block, j]
+        )
+
     for r in range(blocks):
-        spot = pl.ds(pl.multiple_of((place ^ r) * rows, rows), rows)
-        for j, target in enumerate((q_buf, k_buf, v_buf)):
-            copies.append(
-                pltpu.make_async_copy(
-                    sources[r].at[:, pl.ds(j * HEAD_DIM, HEAD_DIM)], target.at[spot], sems.at[r, j]
-                )
-            )
-            copies[-1].start()
-    for copy in copies:
-        copy.wait()
-    for j in range(blocks):
-        vt_buf[:, j * rows : (j + 1) * rows] = v_buf[j * rows : (j + 1) * rows, :].T
+        for j in range(3):
+            fetch(r, place ^ r, j).start()
+
+    def ready(block):
+        for j in range(3):
+            fetch(0, block, j).wait()
+        spot = slice(block * rows, (block + 1) * rows)
+        vt_buf[:, spot] = v_buf[spot, :].T
+
     scale = LOG2E / math.sqrt(HEAD_DIM)
 
     def score(i, j):
@@ -332,8 +371,11 @@
         acc_buf[...] += mxu(vt_buf[:, keys], weights.astype(BF16), PLAIN)
 
     m_buf[...] = jnp.full(m_buf.shape, floor_score, F32)
+    ready(0)
     score(0, 0)
     for i in range(blocks):
+        if i + 1 < blocks:
+            ready(i + 1)
         top = jnp.max(m_buf[i % 2], axis=0, keepdims=True) * scale
         m_buf[(i + 1) % 2] = jnp.full((8, rows), floor_score, F32)
         acc_buf[...] = jnp.zeros(acc_buf.shape, F32)
@@ -384,22 +426,47 @@
     )(place, *sources)
 
 
-def join_kernel(place_ref, *refs, blocks, heads):
-    parts, out_ref = refs[: blocks * heads], refs[blocks * heads]
-    sems = refs[blocks * heads + 1]
+def join_kernel(place_ref, *refs, blocks, heads, head):
+    parts, out_ref, buf, sems = refs[:blocks], refs[-3], refs[-2], refs[-1]
     place = place_ref[0]
-    copies = []
+    reads, writes = [], []
     for r in range(blocks):
-        for h in range(heads):
-            column = pl.multiple_of(((place ^ r) * heads + h) * HEAD_DIM, HEAD_DIM)
-            copies.append(
-                pltpu.make_async_copy(
-                    parts[r * heads + h], out_ref.at[:, pl.ds(column, HEAD_DIM)], sems.at[r, h]
-                )
+        reads.append(pltpu.make_async_copy(parts[r], buf.at[r], sems.at[0, r]))
+        reads[-1].start()
+    for r in range(blocks):
+        column = pl.multiple_of(((place ^ r) * heads + head) * HEAD_DIM, HEAD_DIM)
+        reads[r].wait()
+        writes.append(
+            pltpu.make_async_copy(
+                buf.at[r], out_ref.at[:, pl.ds(column, HEAD_DIM)], sems.at[1, r]
             )
-            copies[-1].start()
-    for copy in copies:
-        copy.wait()
+        )
+        writes[-1].start()
+    for write in writes:
+        write.wait()
+
+
+def join(place, parts, whole, heads, head):
+    blocks = len(parts)
+    rows = parts[0].shape[0]
+    fresh = whole is None
+    operands = tuple(parts) + (() if fresh else (whole,))
+    return pl.pallas_call(
+        functools.partial(join_kernel, blocks=blocks, heads=heads, head=head),
+        in_specs=[pl.BlockSpec(memory_space=pltpu.SMEM)]
+        + [pl.BlockSpec(memory_space=pl.ANY)] * len(operands),
+        out_specs=pl.BlockSpec(memory_space=pl.ANY),
+        out_shape=jax.ShapeDtypeStruct((rows, blocks * heads * HEAD_DIM), BF16),
+        scratch_shapes=[
+            pltpu.VMEM((blocks, rows, HEAD_DIM), BF16),
+            pltpu.SemaphoreType.DMA((2, blocks)),
+        ],
+        input_output_aliases={} if fresh else {len(operands): 0},
+        cost_estimate=pl.CostEstimate(
+            flops=0, bytes_accessed=4 * blocks * rows * HEAD_DIM, transcendentals=0
+        ),
+        name="join",
+    )(place, *operands)
 
 
 def exchange_body(
@@ -426,50 +493,40 @@
         return lax.ppermute(a, "ctx", [(i, i ^ r) for i in range(ctx_size)])
 
     order = sorted(range(1, ctx_size), key=lambda r: (-bin(r >> 1).count("1"), r)) + [0]
-    span = math.isqrt(ctx_size - 1) + (math.isqrt(ctx_size - 1) ** 2 < ctx_size - 1)
     got, backs = [], []
     sent = query_rows
     for h in range(heads):
-        if h == 1:
+        packed = pack(where, (after(query_rows, sent), key_rows, value_rows), order, heads, h)
+        sent = packed[0]
+        if h == 0:
             rate, local_residue = gathered_modes(
                 decay_rate, residue, filter_index, tiles, tp_size, sent
             )
-            part, state = local_part(
-                gate_inner, gate_outer, hyena_value, rate, local_residue, skip_gain
-            )
-            near = [shifted(state, k, ctx_size) for k in range(1, span + 1)]
-            sent = state
-        packed = pack(where, (after(query_rows, sent), key_rows, value_rows), order, heads, h)
-        sent = packed[0]
         mine = [None] * ctx_size
         for piece, r in zip(packed, order):
             mine[r] = swap(piece, r) if r else piece
         got.append(mine)
+    part, state = local_part(gate_inner, gate_outer, hyena_value, rate, local_residue, skip_gain)
+    near = [state] + [swap(state, r) for r in range(1, SPAN)]
+
     for h in range(heads):
+        if h == heads - 1:
+            near = lax.optimization_barrier(tuple(near) + (backs[-1][0],))[:-1]
+            before, total = gather_states(
+                jnp.stack([place.astype(jnp.int32), jnp.int32(row_count)]), rate, near
+            )
+            other = swap(total, SPAN)
         results = flash(where, got[h])
-        if h == 0:
-            near = lax.optimization_barrier(tuple(near) + (results[0],))[:-1]
-            incoming = scan_join(near[0].astype(F32), near[1:], 1, rate, row_count)
-            far = [
-                shifted(incoming, span * k, ctx_size)
-                for k in range(1, span + 1)
-                if span * k < ctx_size
-            ]
         backs.append([swap(a, r) if r else a for r, a in enumerate(results)])
-    far = lax.optimization_barrier(tuple(far) + (results[0],))[:-1]
-    incoming = scan_join(incoming, far, span, rate, row_count).astype(BF16)
-    hyena_output = remote_part(part, gate_outer, rate, local_residue, incoming)
-    parts = [backs[h][r] for r in range(ctx_size) for h in range(heads)]
-    parts[0] = after(parts[0], hyena_output)
-    attention_output = pl.pallas_call(
-        functools.partial(join_kernel, blocks=ctx_size, heads=heads),
-        in_specs=[pl.BlockSpec(memory_space=pltpu.SMEM)]
-        + [pl.BlockSpec(memory_space=pltpu.VMEM)] * len(parts),
-        out_specs=pl.BlockSpec(memory_space=pl.ANY),
-        out_shape=jax.ShapeDtypeStruct((row_count, width_cols), BF16),
-        scratch_shapes=[pltpu.SemaphoreType.DMA((ctx_size, heads))],
-        name="join",
-    )(where, *parts)
+    before = after(before, backs[-1][0])
+    hyena_output = remote_part(where, part, gate_outer, rate, local_residue, before, other)
+    attention_output = None
+    for h in range(heads):
+        attention_output = join(where, backs[h], attention_output, heads, h)
+        if h == heads - 2:
+            hyena_output, attention_output = lax.optimization_barrier(
+                (hyena_output, attention_output)
+            )
     return (hyena_output, attention_output)
 
 
@@ -554,7 +611,7 @@
         value_rows,
     ):
         head_count = query_rows.shape[1] // HEAD_DIM
-        if head_count % ctx_size == 0 and ctx_size & (ctx_size - 1) == 0 and ctx_size > 2:
+        if head_count % (2 * ctx_size) == 0 and ctx_size == 2 * SPAN:
             return exchange_body(
                 gate_inner,
                 gate_outer,

time: 168 us -> 158 us (0.940)
  starting transfers between devices: 55.3 us -> 37.2 us
  waiting for transfers between devices: 36.9 us -> 42.5 us
  local copies, waits for them, and re-layouts: 7.91 us -> 11.2 us
    ppermute x28 -> x32, waiting for transfers between devices: 29.4 us -> 40.8 us  [swap(): return lax.ppermute(a, 'ctx', [(i, i ^ r) for i in range(ctx_size)])]
    ppermute x5 -> x0, starting transfers between devices: 11 us -> none  [shifted(): lax.ppermute(a.astype(BF16), 'ctx', [(i, i + by) for i in range(ctx_size...]
    ppermute x28 -> x32, starting transfers between devices: 38.2 us -> 31.1 us  [swap(): return lax.ppermute(a, 'ctx', [(i, i ^ r) for i in range(ctx_size)])]
    unnamed x60 -> x72, local copies, waits for them, and re-layouts: 2.72 us -> 9.64 us
    ppermute x5 -> x0, waiting for transfers between devices: 5.82 us -> none  [shifted(): lax.ppermute(a.astype(BF16), 'ctx', [(i, i + by) for i in range(ctx_size...]
    exp x8 -> x0, local copies, waits for them, and re-layouts: 3.63 us -> none  [scan_join(): value = value + more.astype(F32) * jnp.exp(-rate * float(rows * base * k))]
    pallas_call x2, Pallas kernels: 30.7 us -> 28.3 us  [flash(): pl.pallas_call(functools.partial(flash_kernel, blocks=blocks), in_specs=[...]
    pallas_call x2 -> x4, Pallas kernels: 10.8 us -> 12.9 us  [the longest x1 6.99 us: remote_part(): pl.pallas_call(remote_kernel, grid=grid, in_specs=[pl.BlockSpec(memory_sp...]
  transfers between devices with their start and end apart: 36 -> 35, of which waited for: 9 -> 9; matrix products, arithmetic and copies ran while one was open for 4% -> 2% of each run, Pallas kernels for 34% -> 37%
where the time goes in v1:
time: 158 us; the launch traced here: 157 us
  Pallas kernels  63.7 us (40%)
  waiting for transfers between devices  42.5 us (27%)
  starting transfers between devices  37.2 us (24%)
  local copies, waits for them, and re-layouts  11.2 us (7%)
    ppermute x32, waiting for transfers between devices, swap(): return lax.ppermute(a, 'ctx', [(i, i ^ r) for i in range(ctx_size)])  40.8 us
    ppermute x32, starting transfers between devices, swap(): return lax.ppermute(a, 'ctx', [(i, i ^ r) for i in range(ctx_size)])  31.1 us
    pallas_call x2, Pallas kernels, flash(): pl.pallas_call(functools.partial(flash_kernel, blocks=blocks), in_specs=[...  28.3 us
    pallas_call x1, Pallas kernels, local_part(): pl.pallas_call(local_kernel, grid=grid, in_specs=[wide, wide, wide, row,...  16 us
    unnamed x72, local copies, waits for them, and re-layouts  9.64 us
    pallas_call x1, Pallas kernels, remote_part(): pl.pallas_call(remote_kernel, grid=grid, in_specs=[pl.BlockSpec(memory_sp...  6.99 us
    pallas_call x2, Pallas kernels, pack(): pl.pallas_call(functools.partial(pack_kernel, spots=spots, heads=heads, h...  6.5 us
    ppermute x3, starting transfers between devices, gathered_modes(): lax.ppermute(modes, 'tp', [(i, (i + shift) % tp_size) for i in range(tp_s...  6.14 us
  transfers between devices with their start and end apart: 35, of which 9 were waited for; matrix products, arithmetic and copies ran while one was open for 2% of the time, Pallas kernels for 37%

profile of v1, /device:TPU:0, one launch (start us, length us, event | category | flops | bytes accessed | tf_op | source)
XLA Modules:
  0.0 157.4 jit_solution(7682731201214181209)
XLA Ops:
  0.6 0.7 pad_maximum_fusion
  1.4 3.3 %pack.2 = (bf16[512,384]{1,0:T(8,128)(2,1)}, bf16[512,384]{1,0:T(8,128)(2,1)}, bf16[512,384]{1,0:T(8,128)(2,1)}, bf16[512,384]{1,0:T(8,128)(2,1)}, bf16[512,384]...) custom-call(s32[1]{0:T(128)} %bitcast.place_ref, ...), custom_call_target="tpu_custom_call" | custom-call | bytes 6291456 | tf_op jit(solution)/shard_map/pack/pallas_call | solution.py:313
  4.6 5.1 %collective-permute-start.2 = (f32[128,32]{0,1:T(8,128)S(1)}, f32[128,32]{0,1:T(8,128)S(1)}, u32[]{:S(2)}, u32[]{:S(2)}) collective-permute-start(f32[128,32]{0,1:T(8,128)S(1)} %pad_maximum_fusion), channel_id=1, source_target_pairs={{0,3},{1,0},{2,1},{3,2},{4,7},{5,4},{6,5},{7,6},{8,11},{9,8},{10,9... | collective-permute-start | bytes 49160 | tf_op jit(solution)/shard_map/ppermute | solution.py:191
  9.8 1.0 collective-permute-start
  10.8 1.5 collective-permute-start.7
  12.7 1.7 %collective-permute-done.1 = f32[128,32]{0,1:T(8,128)S(1)} collective-permute-done((f32[128,32]{0,1:T(8,128)S(1)}, f32[128,32]{0,1:T(8,128)S(1)}, u32[]{:S(2)}, u32[]{:S(2)}) %collective-permute-start.1) | collective-permute-done | bytes 16416 | tf_op jit(solution)/shard_map/ppermute | solution.py:191
  14.4 1.5 collective-permute-start.9
  16.3 0.7 reshape.19
  17.1 0.7 reshape.18
  17.8 16.0 %local_part.1 = (f32[512,2048]{1,0:T(8,128)}, bf16[16,16,128]{2,1,0:T(8,128)(2,1)}) custom-call(bf16[512,2048]{1,0:T(8,128)(2,1)} %gate_ref.1, bf16[512,2048]{1,0:T(8,128)(2,1)} %outer_ref.3, bf16[512,2048]{1,0:T(8,128)(2,1)} %value_ref.1, f32[16,1,128]{2,1,0:T(1,128)} %bitcast.7, f32[16,1,128]{2,1,0:T(1,128)} %bitcast.10, f32[16,1,128]{2,1,0:T(1,128)} %bitcast.12), custom_call_target="tpu_custom_call" | custom-call | flops 4294967296 | bytes 10485760 | tf_op jit(solution)/shard_map/local_part/pallas_call | solution.py:223
  33.8 4.6 %collective-permute-done.5.refs_3_ = bf16[16,16,128]{2,1,0:T(8,128)(2,1)S(1)} collective-permute-done((bf16[16,16,128]{2,1,0:T(8,128)(2,1)}, bf16[16,16,128]{2,1,0:T(8,128)(2,1)S(1)}, u32[]{:S(2)}, u32[]{:S(2)}) %collective-permute-start.5) | collective-permute-done | bytes 65568 | tf_op jit(solution)/shard_map/ppermute | solution.py:493
  38.4 0.8 collective-permute-start.4
  39.2 3.6 %collective-permute-done.4.refs_2_ = bf16[16,16,128]{2,1,0:T(8,128)(2,1)S(1)} collective-permute-done((bf16[16,16,128]{2,1,0:T(8,128)(2,1)}, bf16[16,16,128]{2,1,0:T(8,128)(2,1)S(1)}, u32[]{:S(2)}, u32[]{:S(2)}) %collective-permute-start.4) | collective-permute-done | bytes 65568 | tf_op jit(solution)/shard_map/ppermute | solution.py:493
  42.9 1.5 collective-permute-done.3.refs_1_
  44.3 0.7 collective-permute-start.10
  45.0 1.4 collective-permute-start.12
  46.4 3.2 %pack.3 = (bf16[512,384]{1,0:T(8,128)(2,1)}, bf16[512,384]{1,0:T(8,128)(2,1)}, bf16[512,384]{1,0:T(8,128)(2,1)}, bf16[512,384]{1,0:T(8,128)(2,1)}, bf16[512,384]...) custom-call(s32[1]{0:T(128)} %bitcast.place_ref, ...), custom_call_target="tpu_custom_call" | custom-call | bytes 6291456 | tf_op jit(solution)/shard_map/pack/pallas_call | solution.py:313
  49.7 1.6 %collective-permute-start.11 = (bf16[512,384]{1,0:T(8,128)(2,1)}, bf16[512,384]{1,0:T(8,128)(2,1)S(1)}, u32[]{:S(2)}, u32[]{:S(2)}) collective-permute-start(bf16[512,384]{1,0:T(8,128)(2,1)} %get-tuple-element.49), channel_id=1, source_target_pairs={{0,24},{4,28},{8,16},{12,20},{16,8},{20,12},{24,0},{28,4},{1,25},{... | collective-permute-start | bytes 1179656 | tf_op jit(solution)/shard_map/ppermute | solution.py:493
  51.3 0.9 collective-permute-start.14
  52.8 19.4 %collective-permute-done.10.refs_5_ = bf16[512,384]{1,0:T(8,128)(2,1)S(1)} collective-permute-done((bf16[512,384]{1,0:T(8,128)(2,1)S(1)}, bf16[512,384]{1,0:T(8,128)(2,1)S(1)}, u32[]{:S(2)}, u32[]{:S(2)}) %collective-permute-start.10) | collective-permute-done | bytes 393248 | tf_op jit(solution)/shard_map/ppermute | solution.py:493
  72.3 0.8 copy-done.4
  73.0 0.9 collective-permute-start.15
  73.9 0.9 collective-permute-start.16
  75.3 1.5 collective-permute-start.18
  76.9 1.4 collective-permute-start.19
  78.3 1.0 copy-done.5
  79.3 14.2 %flash.2 = (bf16[512,128]{1,0:T(8,128)(2,1)S(1)}, bf16[512,128]{1,0:T(8,128)(2,1)S(1)}, bf16[512,128]{1,0:T(8,128)(2,1)S(1)}, bf16[512,128]{1,0:T(8,128)(2,1)S(1...) custom-call(s32[1]{0:T(128)} %bitcast.place_ref, ...), custom_call_target="tpu_custom_call" | custom-call | flops 9663676416 | bytes 4194304 | tf_op jit(solution)/shard_map/flash/pallas_call | solution.py:403
  94.8 0.7 copy-done.8
  96.8 0.7 copy-done.13
  98.7 1.8 %gather_states.1 = (f32[16,16,128]{2,1,0:T(8,128)}, bf16[16,16,128]{2,1,0:T(8,128)(2,1)}) custom-call(s32[2]{0:T(128)} %pad_add_fusion.place_ref, f32[16,1,128]{2,1,0:T(1,128)} %bitcast.8, bf16[16,16,128]{2,1,0:T(8,128)(2,1)} %get-tuple-element.61.refs_0_, bf16[16,16,128]{2,1,0:T(8,128)(2,1)} %copy-done.33, bf16[16,16,128]{2,1,0:T(8,128)(2,1)} %copy-done.32, ...), custom_call_target="tpu_custom_call" | custom-call | tf_op jit(solution)/shard_map/gather_states/pallas_call | solution.py:146
  100.5 2.5 %collective-permute-done.16.refs_4_ = bf16[512,384]{1,0:T(8,128)(2,1)} collective-permute-done((bf16[512,384]{1,0:T(8,128)(2,1)}, bf16[512,384]{1,0:T(8,128)(2,1)}, u32[]{:S(2)}, u32[]{:S(2)}) %collective-permute-start.16) | collective-permute-done | bytes 393248 | tf_op jit(solution)/shard_map/ppermute | solution.py:493
  103.1 1.2 collective-permute-start.22
  104.3 5.4 %collective-permute-done.17.refs_5_ = bf16[512,384]{1,0:T(8,128)(2,1)} collective-permute-done((bf16[512,384]{1,0:T(8,128)(2,1)}, bf16[512,384]{1,0:T(8,128)(2,1)}, u32[]{:S(2)}, u32[]{:S(2)}) %collective-permute-start.17) | collective-permute-done | bytes 393248 | tf_op jit(solution)/shard_map/ppermute | solution.py:493
  109.7 1.5 collective-permute-start.23
  111.2 0.9 collective-permute-start.24
  112.1 1.1 collective-permute-start.20
  113.3 14.1 %flash.3 = (bf16[512,128]{1,0:T(8,128)(2,1)S(1)}, bf16[512,128]{1,0:T(8,128)(2,1)S(1)}, bf16[512,128]{1,0:T(8,128)(2,1)S(1)}, bf16[512,128]{1,0:T(8,128)(2,1)S(1...) custom-call(s32[1]{0:T(128)} %bitcast.place_ref, ...), custom_call_target="tpu_custom_call" | custom-call | flops 9663676416 | bytes 4194304 | tf_op jit(solution)/shard_map/flash/pallas_call | solution.py:403
  128.0 1.0 collective-permute-start.25
  129.0 1.7 %collective-permute-start.26 = (bf16[512,128]{1,0:T(8,128)(2,1)S(1)}, bf16[512,128]{1,0:T(8,128)(2,1)S(1)}, u32[]{:S(2)}, u32[]{:S(2)}) collective-permute-start(bf16[512,128]{1,0:T(8,128)(2,1)S(1)} %copy-done.9), channel_id=1, source_target_pairs={{0,24},{4,28},{8,16},{12,20},{16,8},{20,12},{24,0},{28,4},{1,25},{... | collective-permute-start | bytes 393224 | tf_op jit(solution)/shard_map/ppermute | solution.py:493
  130.7 1.8 %collective-permute-start.27 = (bf16[512,128]{1,0:T(8,128)(2,1)S(1)}, bf16[512,128]{1,0:T(8,128)(2,1)S(1)}, u32[]{:S(2)}, u32[]{:S(2)}) collective-permute-start(bf16[512,128]{1,0:T(8,128)(2,1)S(1)} %copy-done.7), channel_id=1, source_target_pairs={{0,28},{4,24},{8,20},{12,16},{16,12},{20,8},{24,4},{28,0},{1,29},{... | collective-permute-start | bytes 393224 | tf_op jit(solution)/shard_map/ppermute | solution.py:493
  133.2 1.1 collective-permute-start.29
  134.4 3.5 %collective-permute-done.25.refs_5_ = bf16[512,128]{1,0:T(8,128)(2,1)S(1)} collective-permute-done((bf16[512,128]{1,0:T(8,128)(2,1)S(1)}, bf16[512,128]{1,0:T(8,128)(2,1)S(1)}, u32[]{:S(2)}, u32[]{:S(2)}) %collective-permute-start.25) | collective-permute-done | bytes 131104 | tf_op jit(solution)/shard_map/ppermute | solution.py:493
  137.9 2.1 %collective-permute-start.30 = (bf16[512,128]{1,0:T(8,128)(2,1)S(1)}, bf16[512,128]{1,0:T(8,128)(2,1)S(1)}, u32[]{:S(2)}, u32[]{:S(2)}) collective-permute-start(bf16[512,128]{1,0:T(8,128)(2,1)S(1)} %get-tuple-element.88), channel_id=1, source_target_pairs={{0,12},{4,8},{8,4},{12,0},{16,28},{20,24},{24,20},{28,16},{1,13},{... | collective-permute-start | bytes 393224 | tf_op jit(solution)/shard_map/ppermute | solution.py:493
  140.0 1.3 collective-permute-start.31
  141.9 2.1 %collective-permute-start.33 = (bf16[512,128]{1,0:T(8,128)(2,1)S(1)}, bf16[512,128]{1,0:T(8,128)(2,1)S(1)}, u32[]{:S(2)}, u32[]{:S(2)}) collective-permute-start(bf16[512,128]{1,0:T(8,128)(2,1)S(1)} %get-tuple-element.91), channel_id=1, source_target_pairs={{0,24},{4,28},{8,16},{12,20},{16,8},{20,12},{24,0},{28,4},{1,25},{... | collective-permute-start | bytes 393224 | tf_op jit(solution)/shard_map/ppermute | solution.py:493
  144.4 7.0 %remote_part.1 = bf16[512,2048]{1,0:T(8,128)(2,1)} custom-call(s32[1]{0:T(128)} %bitcast.place_ref, f32[512,2048]{1,0:T(8,128)} %get-tuple-element.51.part_ref, bf16[512,2048]{1,0:T(8,128)(2,1)} %outer_ref.3, f32[16,1,128]{2,1,0:T(1,128)} %bitcast.9, f32[16,1,128]{2,1,0:T(1,128)} %bitcast.11, f32[16,16,128]{2,1,0:T(8,128)} %get-tuple-element.76.before_ref, ...), custom_call_target="tpu_custom_call" | custom-call | flops 805306368 | bytes 8388608 | tf_op jit(solution)/shard_map/remote_part/pallas_call | solution.py:245
  151.4 2.1 %join.2.refs_8_ = bf16[512,2048]{1,0:T(8,128)(2,1)} custom-call(s32[1]{0:T(128)} %bitcast.place_ref, bf16[512,128]{1,0:T(8,128)(2,1)} %copy-done.1, bf16[512,128]{1,0:T(8,128)(2,1)} %copy-done.23, bf16[512,128]{1,0:T(8,128)(2,1)} %copy-done.24, bf16[512,128]{1,0:T(8,128)(2,1)} %copy-done.25, bf16[512,128]{1,0:T(8,128)(2,1)} %copy-done.26, ...), custom_call_target="tpu_custom_call" | custom-call | bytes 2097152 | tf_op jit(solution)/shard_map/join/pallas_call | solution.py:454
  155.1 2.1 %join.3 = bf16[512,2048]{1,0:T(8,128)(2,1)} custom-call(s32[1]{0:T(128)} %bitcast.place_ref, bf16[512,128]{1,0:T(8,128)(2,1)} %copy-done, bf16[512,128]{1,0:T(8,128)(2,1)} %copy-done.16, bf16[512,128]{1,0:T(8,128)(2,1)} %copy-done.17, bf16[512,128]{1,0:T(8,128)(2,1)} %copy-done.18, bf16[512,128]{1,0:T(8,128)(2,1)} %copy-done.19, ...), custom_call_target="tpu_custom_call", output_to_operand_aliasing={{}: (9, {})} | custom-call | bytes 2097152 | tf_op jit(solution)/shard_map/join/pallas_call | solution.py:454
  (112 shorter events, 10.0 us)
Async XLA Ops:
  1.4 10.9 %copy-start.35 = (s32[128]{0:T(128)S(1)}, s32[128]{0:T(128)}, u32[]{:S(2)}) copy-start(s32[128]{0:T(128)} %param.16) | copy-start | bytes 1540
  4.6 7.7 %collective-permute-start.2 = (f32[128,32]{0,1:T(8,128)S(1)}, f32[128,32]{0,1:T(8,128)S(1)}, u32[]{:S(2)}, u32[]{:S(2)}) collective-permute-start(f32[128,32]{0,1:T(8,128)S(1)} %pad_maximum_fusion), channel_id=1, source_target_pairs={{0,3},{1,0},{2,1},{3,2},{4,7},{5,4},{6,5},{7,6},{8,11},{9,8},{10,9... | collective-permute-start | bytes 49160 | tf_op jit(solution)/shard_map/ppermute | solution.py:191
  9.8 4.6 %collective-permute-start.1 = (f32[128,32]{0,1:T(8,128)S(1)}, f32[128,32]{0,1:T(8,128)S(1)}, u32[]{:S(2)}, u32[]{:S(2)}) collective-permute-start(f32[128,32]{0,1:T(8,128)S(1)} %pad_maximum_fusion), channel_id=1, source_target_pairs={{0,2},{1,3},{2,0},{3,1},{4,6},{5,7},{6,4},{7,5},{8,10},{9,11},{10,... | collective-permute-start | bytes 49160 | tf_op jit(solution)/shard_map/ppermute | solution.py:191
  9.8 6.2 %collective-permute-start = (f32[128,32]{0,1:T(8,128)S(1)}, f32[128,32]{0,1:T(8,128)S(1)}, u32[]{:S(2)}, u32[]{:S(2)}) collective-permute-start(f32[128,32]{0,1:T(8,128)S(1)} %pad_maximum_fusion), channel_id=1, source_target_pairs={{0,1},{1,2},{2,3},{3,0},{4,5},{5,6},{6,7},{7,4},{8,9},{9,10},{10,1... | collective-permute-start | bytes 49160 | tf_op jit(solution)/shard_map/ppermute | solution.py:191
  10.8 34.2 %collective-permute-start.6 = (bf16[512,384]{1,0:T(8,128)(2,1)}, bf16[512,384]{1,0:T(8,128)(2,1)S(1)}, u32[]{:S(2)}, u32[]{:S(2)}) collective-permute-start(bf16[512,384]{1,0:T(8,128)(2,1)} %get-tuple-element.54), channel_id=1, source_target_pairs={{0,4},{4,0},{8,12},{12,8},{16,20},{20,16},{24,28},{28,24},{1,5},{5... | collective-permute-start | bytes 1179656 | tf_op jit(solution)/shard_map/ppermute | solution.py:493
  10.8 38.9 %collective-permute-start.7 = (bf16[512,384]{1,0:T(8,128)(2,1)}, bf16[512,384]{1,0:T(8,128)(2,1)S(1)}, u32[]{:S(2)}, u32[]{:S(2)}) collective-permute-start(bf16[512,384]{1,0:T(8,128)(2,1)} %get-tuple-element.55), channel_id=1, source_target_pairs={{0,8},{4,12},{8,0},{12,4},{16,24},{20,28},{24,16},{28,20},{1,9},{5... | collective-permute-start | bytes 1179656 | tf_op jit(solution)/shard_map/ppermute | solution.py:493
  12.3 39.0 %collective-permute-start.8 = (bf16[512,384]{1,0:T(8,128)(2,1)}, bf16[512,384]{1,0:T(8,128)(2,1)S(1)}, u32[]{:S(2)}, u32[]{:S(2)}) collective-permute-start(bf16[512,384]{1,0:T(8,128)(2,1)} %get-tuple-element.56), channel_id=1, source_target_pairs={{0,12},{4,8},{8,4},{12,0},{16,28},{20,24},{24,20},{28,16},{1,13},{... | collective-permute-start | bytes 1179656 | tf_op jit(solution)/shard_map/ppermute | solution.py:493
  14.4 36.9 %collective-permute-start.9 = (bf16[512,384]{1,0:T(8,128)(2,1)}, bf16[512,384]{1,0:T(8,128)(2,1)S(1)}, u32[]{:S(2)}, u32[]{:S(2)}) collective-permute-start(bf16[512,384]{1,0:T(8,128)(2,1)} %get-tuple-element.57), channel_id=1, source_target_pairs={{0,16},{4,20},{8,24},{12,28},{16,0},{20,4},{24,8},{28,12},{1,17},{... | collective-permute-start | bytes 1179656 | tf_op jit(solution)/shard_map/ppermute | solution.py:493
  17.8 26.5 %copy-start.34 = (bf16[512,384]{1,0:T(8,128)(2,1)S(1)}, bf16[512,384]{1,0:T(8,128)(2,1)}, u32[]{:S(2)}) copy-start(bf16[512,384]{1,0:T(8,128)(2,1)} %get-tuple-element.58) | copy-start | bytes 1179652
  33.8 4.6 %collective-permute-start.5 = (bf16[16,16,128]{2,1,0:T(8,128)(2,1)}, bf16[16,16,128]{2,1,0:T(8,128)(2,1)S(1)}, u32[]{:S(2)}, u32[]{:S(2)}) collective-permute-start(bf16[16,16,128]{2,1,0:T(8,128)(2,1)} %get-tuple-element.61.refs_0_), channel_id=1, source_target_pairs={{0,12},{4,8},{8,4},{12,0},{16,28},{20,24},{24,20},{28,16},{1,13},{... | collective-permute-start | bytes 196616 | tf_op jit(solution)/shard_map/ppermute | solution.py:493
  38.4 4.5 %collective-permute-start.4 = (bf16[16,16,128]{2,1,0:T(8,128)(2,1)}, bf16[16,16,128]{2,1,0:T(8,128)(2,1)S(1)}, u32[]{:S(2)}, u32[]{:S(2)}) collective-permute-start(bf16[16,16,128]{2,1,0:T(8,128)(2,1)} %get-tuple-element.61.refs_0_), channel_id=1, source_target_pairs={{0,8},{4,12},{8,0},{12,4},{16,24},{20,28},{24,16},{28,20},{1,9},{5... | collective-permute-start | bytes 196616 | tf_op jit(solution)/shard_map/ppermute | solution.py:493
  42.9 1.5 collective-permute-start.3
  44.3 27.9 %collective-permute-start.10 = (bf16[512,384]{1,0:T(8,128)(2,1)S(1)}, bf16[512,384]{1,0:T(8,128)(2,1)S(1)}, u32[]{:S(2)}, u32[]{:S(2)}) collective-permute-start(bf16[512,384]{1,0:T(8,128)(2,1)S(1)} %copy-done.34), channel_id=1, source_target_pairs={{0,20},{4,16},{8,28},{12,24},{16,4},{20,0},{24,12},{28,8},{1,21},{... | collective-permute-start | bytes 1179656 | tf_op jit(solution)/shard_map/ppermute | solution.py:493
  45.0 33.3 %copy-start.2 = (bf16[512,384]{1,0:T(8,128)(2,1)S(1)}, bf16[512,384]{1,0:T(8,128)(2,1)}, u32[]{:S(2)}) copy-start(bf16[512,384]{1,0:T(8,128)(2,1)} %get-tuple-element.53.refs_0_) | copy-start | bytes 1179652
  45.0 28.9 %collective-permute-start.12 = (bf16[512,384]{1,0:T(8,128)(2,1)}, bf16[512,384]{1,0:T(8,128)(2,1)}, u32[]{:S(2)}, u32[]{:S(2)}) collective-permute-start(bf16[512,384]{1,0:T(8,128)(2,1)} %get-tuple-element.59), channel_id=1, source_target_pairs={{0,28},{4,24},{8,20},{12,16},{16,12},{20,8},{24,4},{28,0},{1,29},{... | collective-permute-start | bytes 1179656 | tf_op jit(solution)/shard_map/ppermute | solution.py:493
  49.7 25.1 %collective-permute-start.11 = (bf16[512,384]{1,0:T(8,128)(2,1)}, bf16[512,384]{1,0:T(8,128)(2,1)S(1)}, u32[]{:S(2)}, u32[]{:S(2)}) collective-permute-start(bf16[512,384]{1,0:T(8,128)(2,1)} %get-tuple-element.49), channel_id=1, source_target_pairs={{0,24},{4,28},{8,16},{12,20},{16,8},{20,12},{24,0},{28,4},{1,25},{... | collective-permute-start | bytes 1179656 | tf_op jit(solution)/shard_map/ppermute | solution.py:493
  51.3 24.0 %collective-permute-start.13 = (bf16[512,384]{1,0:T(8,128)(2,1)}, bf16[512,384]{1,0:T(8,128)(2,1)S(1)}, u32[]{:S(2)}, u32[]{:S(2)}) collective-permute-start(bf16[512,384]{1,0:T(8,128)(2,1)} %get-tuple-element.68), channel_id=1, source_target_pairs={{0,4},{4,0},{8,12},{12,8},{16,20},{20,16},{24,28},{28,24},{1,5},{5... | collective-permute-start | bytes 1179656 | tf_op jit(solution)/shard_map/ppermute | solution.py:493
  51.3 25.5 %collective-permute-start.14 = (bf16[512,384]{1,0:T(8,128)(2,1)}, bf16[512,384]{1,0:T(8,128)(2,1)S(1)}, u32[]{:S(2)}, u32[]{:S(2)}) collective-permute-start(bf16[512,384]{1,0:T(8,128)(2,1)} %get-tuple-element.69), channel_id=1, source_target_pairs={{0,8},{4,12},{8,0},{12,4},{16,24},{20,28},{24,16},{28,20},{1,9},{5... | collective-permute-start | bytes 1179656 | tf_op jit(solution)/shard_map/ppermute | solution.py:493
  73.0 27.5 %collective-permute-start.15 = (bf16[512,384]{1,0:T(8,128)(2,1)}, bf16[512,384]{1,0:T(8,128)(2,1)S(1)}, u32[]{:S(2)}, u32[]{:S(2)}) collective-permute-start(bf16[512,384]{1,0:T(8,128)(2,1)} %get-tuple-element.70), channel_id=1, source_target_pairs={{0,12},{4,8},{8,4},{12,0},{16,28},{20,24},{24,20},{28,16},{1,13},{... | collective-permute-start | bytes 1179656 | tf_op jit(solution)/shard_map/ppermute | solution.py:493
  73.9 29.2 %collective-permute-start.16 = (bf16[512,384]{1,0:T(8,128)(2,1)}, bf16[512,384]{1,0:T(8,128)(2,1)}, u32[]{:S(2)}, u32[]{:S(2)}) collective-permute-start(bf16[512,384]{1,0:T(8,128)(2,1)} %get-tuple-element.71), channel_id=1, source_target_pairs={{0,16},{4,20},{8,24},{12,28},{16,0},{20,4},{24,8},{28,12},{1,17},{... | collective-permute-start | bytes 1179656 | tf_op jit(solution)/shard_map/ppermute | solution.py:493
  74.8 34.8 %collective-permute-start.17 = (bf16[512,384]{1,0:T(8,128)(2,1)}, bf16[512,384]{1,0:T(8,128)(2,1)}, u32[]{:S(2)}, u32[]{:S(2)}) collective-permute-start(bf16[512,384]{1,0:T(8,128)(2,1)} %get-tuple-element.72), channel_id=1, source_target_pairs={{0,20},{4,16},{8,28},{12,24},{16,4},{20,0},{24,12},{28,8},{1,21},{... | collective-permute-start | bytes 1179656 | tf_op jit(solution)/shard_map/ppermute | solution.py:493
  75.3 35.9 %collective-permute-start.18 = (bf16[512,384]{1,0:T(8,128)(2,1)}, bf16[512,384]{1,0:T(8,128)(2,1)}, u32[]{:S(2)}, u32[]{:S(2)}) collective-permute-start(bf16[512,384]{1,0:T(8,128)(2,1)} %get-tuple-element.73), channel_id=1, source_target_pairs={{0,24},{4,28},{8,16},{12,20},{16,8},{20,12},{24,0},{28,4},{1,25},{... | collective-permute-start | bytes 1179656 | tf_op jit(solution)/shard_map/ppermute | solution.py:493
  76.9 35.2 %collective-permute-start.19 = (bf16[512,384]{1,0:T(8,128)(2,1)}, bf16[512,384]{1,0:T(8,128)(2,1)}, u32[]{:S(2)}, u32[]{:S(2)}) collective-permute-start(bf16[512,384]{1,0:T(8,128)(2,1)} %get-tuple-element.74), channel_id=1, source_target_pairs={{0,28},{4,24},{8,20},{12,16},{16,12},{20,8},{24,4},{28,0},{1,29},{... | collective-permute-start | bytes 1179656 | tf_op jit(solution)/shard_map/ppermute | solution.py:493
  79.3 33.9 %copy-start.3 = (bf16[512,384]{1,0:T(8,128)(2,1)S(1)}, bf16[512,384]{1,0:T(8,128)(2,1)}, u32[]{:S(2)}) copy-start(bf16[512,384]{1,0:T(8,128)(2,1)} %get-tuple-element.67.refs_0_) | copy-start | bytes 1179652
  100.5 28.5 %collective-permute-start.21 = (bf16[512,128]{1,0:T(8,128)(2,1)}, bf16[512,128]{1,0:T(8,128)(2,1)S(1)}, u32[]{:S(2)}, u32[]{:S(2)}) collective-permute-start(bf16[512,128]{1,0:T(8,128)(2,1)} %copy-done.15), channel_id=1, source_target_pairs={{0,4},{4,0},{8,12},{12,8},{16,20},{20,16},{24,28},{28,24},{1,5},{5... | collective-permute-start | bytes 393224 | tf_op jit(solution)/shard_map/ppermute | solution.py:493
  103.1 27.6 %collective-permute-start.22 = (bf16[512,128]{1,0:T(8,128)(2,1)}, bf16[512,128]{1,0:T(8,128)(2,1)S(1)}, u32[]{:S(2)}, u32[]{:S(2)}) collective-permute-start(bf16[512,128]{1,0:T(8,128)(2,1)} %copy-done.14), channel_id=1, source_target_pairs={{0,8},{4,12},{8,0},{12,4},{16,24},{20,28},{24,16},{28,20},{1,9},{5... | collective-permute-start | bytes 393224 | tf_op jit(solution)/shard_map/ppermute | solution.py:493
  109.7 22.8 %collective-permute-start.23 = (bf16[512,128]{1,0:T(8,128)(2,1)}, bf16[512,128]{1,0:T(8,128)(2,1)S(1)}, u32[]{:S(2)}, u32[]{:S(2)}) collective-permute-start(bf16[512,128]{1,0:T(8,128)(2,1)} %copy-done.13), channel_id=1, source_target_pairs={{0,12},{4,8},{8,4},{12,0},{16,28},{20,24},{24,20},{28,16},{1,13},{... | collective-permute-start | bytes 393224 | tf_op jit(solution)/shard_map/ppermute | solution.py:493
  111.2 21.4 %collective-permute-start.24 = (bf16[512,128]{1,0:T(8,128)(2,1)}, bf16[512,128]{1,0:T(8,128)(2,1)S(1)}, u32[]{:S(2)}, u32[]{:S(2)}) collective-permute-start(bf16[512,128]{1,0:T(8,128)(2,1)} %copy-done.12), channel_id=1, source_target_pairs={{0,16},{4,20},{8,24},{12,28},{16,0},{20,4},{24,8},{28,12},{1,17},{... | collective-permute-start | bytes 393224 | tf_op jit(solution)/shard_map/ppermute | solution.py:493
  112.1 15.9 %collective-permute-start.20 = (bf16[16,16,128]{2,1,0:T(8,128)(2,1)}, bf16[16,16,128]{2,1,0:T(8,128)(2,1)S(1)}, u32[]{:S(2)}, u32[]{:S(2)}) collective-permute-start(bf16[16,16,128]{2,1,0:T(8,128)(2,1)} %get-tuple-element.77), channel_id=1, source_target_pairs={{0,16},{4,20},{8,24},{12,28},{16,0},{20,4},{24,8},{28,12},{1,17},{... | collective-permute-start | bytes 196616 | tf_op jit(solution)/shard_map/ppermute | solution.py:493
  113.2 14.8 %copy-start.11 = (bf16[512,128]{1,0:T(8,128)(2,1)S(1)}, bf16[512,128]{1,0:T(8,128)(2,1)}, u32[]{:S(2)}) copy-start(bf16[512,128]{1,0:T(8,128)(2,1)} %copy-done.10) | copy-start | bytes 393220
  113.2 15.8 %copy-start.9 = (bf16[512,128]{1,0:T(8,128)(2,1)S(1)}, bf16[512,128]{1,0:T(8,128)(2,1)}, u32[]{:S(2)}) copy-start(bf16[512,128]{1,0:T(8,128)(2,1)} %copy-done.8) | copy-start | bytes 393220
  113.2 17.4 %copy-start.7 = (bf16[512,128]{1,0:T(8,128)(2,1)S(1)}, bf16[512,128]{1,0:T(8,128)(2,1)}, u32[]{:S(2)}) copy-start(bf16[512,128]{1,0:T(8,128)(2,1)} %copy-done.6) | copy-start | bytes 393220
  128.0 9.9 %collective-permute-start.25 = (bf16[512,128]{1,0:T(8,128)(2,1)S(1)}, bf16[512,128]{1,0:T(8,128)(2,1)S(1)}, u32[]{:S(2)}, u32[]{:S(2)}) collective-permute-start(bf16[512,128]{1,0:T(8,128)(2,1)S(1)} %copy-done.11), channel_id=1, source_target_pairs={{0,20},{4,16},{8,28},{12,24},{16,4},{20,0},{24,12},{28,8},{1,21},{... | collective-permute-start | bytes 393224 | tf_op jit(solution)/shard_map/ppermute | solution.py:493
  129.0 22.4 %copy-start.23 = (bf16[512,128]{1,0:T(8,128)(2,1)}, bf16[512,128]{1,0:T(8,128)(2,1)S(1)}, u32[]{:S(2)}) copy-start(bf16[512,128]{1,0:T(8,128)(2,1)S(1)} %collective-permute-done.21.refs_1_) | copy-start | bytes 393220
  129.0 11.0 %collective-permute-start.26 = (bf16[512,128]{1,0:T(8,128)(2,1)S(1)}, bf16[512,128]{1,0:T(8,128)(2,1)S(1)}, u32[]{:S(2)}, u32[]{:S(2)}) collective-permute-start(bf16[512,128]{1,0:T(8,128)(2,1)S(1)} %copy-done.9), channel_id=1, source_target_pairs={{0,24},{4,28},{8,16},{12,20},{16,8},{20,12},{24,0},{28,4},{1,25},{... | collective-permute-start | bytes 393224 | tf_op jit(solution)/shard_map/ppermute | solution.py:493
  130.7 20.7 %copy-start.24 = (bf16[512,128]{1,0:T(8,128)(2,1)}, bf16[512,128]{1,0:T(8,128)(2,1)S(1)}, u32[]{:S(2)}) copy-start(bf16[512,128]{1,0:T(8,128)(2,1)S(1)} %collective-permute-done.22.refs_2_) | copy-start | bytes 393220
  130.7 10.6 %collective-permute-start.27 = (bf16[512,128]{1,0:T(8,128)(2,1)S(1)}, bf16[512,128]{1,0:T(8,128)(2,1)S(1)}, u32[]{:S(2)}, u32[]{:S(2)}) collective-permute-start(bf16[512,128]{1,0:T(8,128)(2,1)S(1)} %copy-done.7), channel_id=1, source_target_pairs={{0,28},{4,24},{8,20},{12,16},{16,12},{20,8},{24,4},{28,0},{1,29},{... | collective-permute-start | bytes 393224 | tf_op jit(solution)/shard_map/ppermute | solution.py:493
  132.5 18.9 %copy-start.25 = (bf16[512,128]{1,0:T(8,128)(2,1)}, bf16[512,128]{1,0:T(8,128)(2,1)S(1)}, u32[]{:S(2)}) copy-start(bf16[512,128]{1,0:T(8,128)(2,1)S(1)} %collective-permute-done.23.refs_3_) | copy-start | bytes 393220
  132.5 9.4 %collective-permute-start.28 = (bf16[512,128]{1,0:T(8,128)(2,1)S(1)}, bf16[512,128]{1,0:T(8,128)(2,1)S(1)}, u32[]{:S(2)}, u32[]{:S(2)}) collective-permute-start(bf16[512,128]{1,0:T(8,128)(2,1)S(1)} %get-tuple-element.86), channel_id=1, source_target_pairs={{0,4},{4,0},{8,12},{12,8},{16,20},{20,16},{24,28},{28,24},{1,5},{5... | collective-permute-start | bytes 393224 | tf_op jit(solution)/shard_map/ppermute | solution.py:493
  133.2 10.7 %collective-permute-start.29 = (bf16[512,128]{1,0:T(8,128)(2,1)S(1)}, bf16[512,128]{1,0:T(8,128)(2,1)S(1)}, u32[]{:S(2)}, u32[]{:S(2)}) collective-permute-start(bf16[512,128]{1,0:T(8,128)(2,1)S(1)} %get-tuple-element.87), channel_id=1, source_target_pairs={{0,8},{4,12},{8,0},{12,4},{16,24},{20,28},{24,16},{28,20},{1,9},{5... | collective-permute-start | bytes 393224 | tf_op jit(solution)/shard_map/ppermute | solution.py:493
  137.9 13.5 %copy-start.27 = (bf16[512,128]{1,0:T(8,128)(2,1)}, bf16[512,128]{1,0:T(8,128)(2,1)S(1)}, u32[]{:S(2)}) copy-start(bf16[512,128]{1,0:T(8,128)(2,1)S(1)} %collective-permute-done.25.refs_5_) | copy-start | bytes 393220
  137.9 15.7 %collective-permute-start.30 = (bf16[512,128]{1,0:T(8,128)(2,1)S(1)}, bf16[512,128]{1,0:T(8,128)(2,1)S(1)}, u32[]{:S(2)}, u32[]{:S(2)}) collective-permute-start(bf16[512,128]{1,0:T(8,128)(2,1)S(1)} %get-tuple-element.88), channel_id=1, source_target_pairs={{0,12},{4,8},{8,4},{12,0},{16,28},{20,24},{24,20},{28,16},{1,13},{... | collective-permute-start | bytes 393224 | tf_op jit(solution)/shard_map/ppermute | solution.py:493
  140.0 11.4 %copy-start.28 = (bf16[512,128]{1,0:T(8,128)(2,1)}, bf16[512,128]{1,0:T(8,128)(2,1)S(1)}, u32[]{:S(2)}) copy-start(bf16[512,128]{1,0:T(8,128)(2,1)S(1)} %collective-permute-done.26.refs_6_) | copy-start | bytes 393220
  140.0 13.6 %collective-permute-start.31 = (bf16[512,128]{1,0:T(8,128)(2,1)S(1)}, bf16[512,128]{1,0:T(8,128)(2,1)S(1)}, u32[]{:S(2)}, u32[]{:S(2)}) collective-permute-start(bf16[512,128]{1,0:T(8,128)(2,1)S(1)} %get-tuple-element.89), channel_id=1, source_target_pairs={{0,16},{4,20},{8,24},{12,28},{16,0},{20,4},{24,8},{28,12},{1,17},{... | collective-permute-start | bytes 393224 | tf_op jit(solution)/shard_map/ppermute | solution.py:493
  141.3 10.1 %copy-start.29 = (bf16[512,128]{1,0:T(8,128)(2,1)}, bf16[512,128]{1,0:T(8,128)(2,1)S(1)}, u32[]{:S(2)}) copy-start(bf16[512,128]{1,0:T(8,128)(2,1)S(1)} %collective-permute-done.27.refs_7_) | copy-start | bytes 393220
  141.3 12.4 %collective-permute-start.32 = (bf16[512,128]{1,0:T(8,128)(2,1)S(1)}, bf16[512,128]{1,0:T(8,128)(2,1)S(1)}, u32[]{:S(2)}, u32[]{:S(2)}) collective-permute-start(bf16[512,128]{1,0:T(8,128)(2,1)S(1)} %get-tuple-element.90), channel_id=1, source_target_pairs={{0,20},{4,16},{8,28},{12,24},{16,4},{20,0},{24,12},{28,8},{1,21},{... | collective-permute-start | bytes 393224 | tf_op jit(solution)/shard_map/ppermute | solution.py:493
  141.9 11.9 %collective-permute-start.33 = (bf16[512,128]{1,0:T(8,128)(2,1)S(1)}, bf16[512,128]{1,0:T(8,128)(2,1)S(1)}, u32[]{:S(2)}, u32[]{:S(2)}) collective-permute-start(bf16[512,128]{1,0:T(8,128)(2,1)S(1)} %get-tuple-element.91), channel_id=1, source_target_pairs={{0,24},{4,28},{8,16},{12,20},{16,8},{20,12},{24,0},{28,4},{1,25},{... | collective-permute-start | bytes 393224 | tf_op jit(solution)/shard_map/ppermute | solution.py:493
  143.9 9.8 %collective-permute-start.34 = (bf16[512,128]{1,0:T(8,128)(2,1)S(1)}, bf16[512,128]{1,0:T(8,128)(2,1)S(1)}, u32[]{:S(2)}, u32[]{:S(2)}) collective-permute-start(bf16[512,128]{1,0:T(8,128)(2,1)S(1)} %get-tuple-element.92), channel_id=1, source_target_pairs={{0,28},{4,24},{8,20},{12,16},{16,12},{20,8},{24,4},{28,0},{1,29},{... | collective-permute-start | bytes 393224 | tf_op jit(solution)/shard_map/ppermute | solution.py:493
  (23 other events, 42.6 us)

commit v2 on v1

--- a/solution.py
+++ b/solution.py
@@ -15,6 +15,8 @@
 TILE_GROUPS = LANES // GROUP
 STEP_TILES = 4
 SPAN = 4
+SENDS = (6, 7, 4, 2, 5, 3, 1)
+WHOLE_VMEM = pltpu.CompilerParams(vmem_limit_bytes=63 << 20)
 
 floor_score = -1e30
 LOG2E = 1.4426950408889634
@@ -149,6 +151,7 @@
         + [pl.BlockSpec(memory_space=pltpu.VMEM)] * (1 + SPAN),
         out_specs=[pl.BlockSpec(memory_space=pltpu.VMEM)] * 2,
         out_shape=[jax.ShapeDtypeStruct(shape, F32), jax.ShapeDtypeStruct(shape, BF16)],
+        compiler_params=WHOLE_VMEM,
         name="gather_states",
     )(where, rate, *nears)
 
@@ -157,7 +160,7 @@
     place_ref, part_ref, outer_ref, rate_ref, residue_ref, before_ref, other_ref, out_ref
 ):
     rows, cols = outer_ref.shape
-    step = iota((rows, LANES), 0).astype(F32)
+    step = iota((CHUNK, LANES), 0).astype(F32)
     mask = same_group()
     pick = (iota((LANES, GROUP), 0) % GROUP == iota((LANES, GROUP), 1)).astype(BF16)
     spot = (place_ref[0] % SPAN).astype(F32) * rows
@@ -168,10 +171,11 @@
         faded = other_ref[w].astype(F32) * jnp.exp(-rate * spot)
         incoming = (before_ref[w] + jnp.where(upper, faded, 0.0)).astype(BF16)
         state = jnp.where(mask, mxu(pick, incoming, PLAIN), 0.0).astype(BF16)
-        shrinking = halves(residue_ref[w] * jnp.exp(-step * rate))
-        earlier = mxu(
-            jnp.concatenate(shrinking, axis=1), jnp.concatenate([state, state], axis=1), LAST
-        )
+        decay = jnp.exp(-CHUNK * rate)
+        shrinking = [residue_ref[w] * jnp.exp(-step * rate)]
+        while len(shrinking) < rows // CHUNK:
+            shrinking.append(shrinking[-1] * decay)
+        earlier = mxu(jnp.concatenate(shrinking, axis=0).astype(BF16), state, LAST)
         gate = outer_ref[:, lanes].astype(F32)
         out_ref[:, lanes] = (part_ref[:, lanes] + gate * earlier).astype(BF16)
 
@@ -206,8 +210,8 @@
     )
 
 
-def hyena_specs(row_count, tiles):
-    group = math.gcd(tiles, STEP_TILES)
+def hyena_specs(row_count, tiles, most=STEP_TILES):
+    group = math.gcd(tiles, most)
     return (
         (tiles // group,),
         pl.BlockSpec((row_count, group * LANES), lambda i: (0, i)),
@@ -234,6 +238,7 @@
             bytes_accessed=10 * row_count * chan_count,
             transcendentals=row_count * chan_count,
         ),
+        compiler_params=WHOLE_VMEM,
         name="local_part",
     )(gate_inner, gate_outer, hyena_value, rate, residue, skip_gain.reshape(tiles, 1, LANES))
 
@@ -241,7 +246,7 @@
 def remote_part(where, part, gate_outer, rate, residue, before, other):
     row_count, chan_count = gate_outer.shape
     tiles = chan_count // LANES
-    grid, wide, row, small = hyena_specs(row_count, tiles)
+    grid, wide, row, small = hyena_specs(row_count, tiles, 4)
     return pl.pallas_call(
         remote_kernel,
         grid=grid,
@@ -253,6 +258,7 @@
             bytes_accessed=8 * row_count * chan_count,
             transcendentals=row_count * chan_count // 4,
         ),
+        compiler_params=WHOLE_VMEM,
         name="remote_part",
     )(where, part, gate_outer, rate, residue, before, other)
 
@@ -324,6 +330,7 @@
         cost_estimate=pl.CostEstimate(
             flops=0, bytes_accessed=4 * len(spots) * rows * 3 * HEAD_DIM, transcendentals=0
         ),
+        compiler_params=WHOLE_VMEM,
         name="pack",
     )(place, *arrays)
 
@@ -353,22 +360,40 @@
 
     scale = LOG2E / math.sqrt(HEAD_DIM)
 
+    half = rows // 2
+
+    def score_part(i, keys, first, masked):
+        queries = slice(i * rows + first, (i + 1) * rows)
+        scores = mxu(k_buf[keys, :], q_buf[queries, :], LAST)
+        shape = scores.shape
+        if masked:
+            scores = jnp.where(iota(shape, 1) >= iota(shape, 0), scores, floor_score)
+        s_buf[i % 2, keys, first:] = scores
+        m_buf[i % 2, :, first:] = jnp.maximum(
+            m_buf[i % 2, :, first:], jnp.max(scores.reshape(shape[0] // 8, 8, shape[1]), axis=0)
+        )
+
+    def weigh_part(i, keys, first, top):
+        weights = jnp.exp2(s_buf[i % 2, keys, first:] * scale - top[:, first:])
+        shape = weights.shape
+        l_buf[:, first:] += jnp.sum(weights.reshape(shape[0] // 8, 8, shape[1]), axis=0)
+        acc_buf[:, first:] += mxu(vt_buf[:, keys], weights.astype(BF16), PLAIN)
+
+    def spans(i, j):
+        if i != j:
+            return [(slice(j * rows, (j + 1) * rows), 0)]
+        return [
+            (slice(j * rows, j * rows + half), 0),
+            (slice(j * rows + half, (j + 1) * rows), half),
+        ]
+
     def score(i, j):
-        keys = slice(j * rows, (j + 1) * rows)
-        scores = mxu(k_buf[keys, :], q_buf[i * rows : (i + 1) * rows, :], LAST)
-        if i == j:
-            shape = (rows, rows)
-            scores = jnp.where(iota(shape, 1) >= iota(shape, 0), scores, floor_score)
-        s_buf[i % 2, keys, :] = scores
-        m_buf[i % 2] = jnp.maximum(
-            m_buf[i % 2], jnp.max(scores.reshape(rows // 8, 8, rows), axis=0)
-        )
+        for keys, first in spans(i, j):
+            score_part(i, keys, first, i == j)
 
     def weigh(i, j, top):
-        keys = slice(j * rows, (j + 1) * rows)
-        weights = jnp.exp2(s_buf[i % 2, keys, :] * scale - top)
-        l_buf[...] += jnp.sum(weights.reshape(rows // 8, 8, rows), axis=0)
-        acc_buf[...] += mxu(vt_buf[:, keys], weights.astype(BF16), PLAIN)
+        for keys, first in spans(i, j):
+            weigh_part(i, keys, first, top)
 
     m_buf[...] = jnp.full(m_buf.shape, floor_score, F32)
     ready(0)
@@ -418,7 +443,7 @@
             pltpu.VMEM((HEAD_DIM, rows), F32),
             pltpu.SemaphoreType.DMA((blocks, 3)),
         ],
-        compiler_params=pltpu.CompilerParams(vmem_limit_bytes=48 << 20),
+        compiler_params=WHOLE_VMEM,
         cost_estimate=pl.CostEstimate(
             flops=8 * pairs * HEAD_DIM, bytes_accessed=8 * total * HEAD_DIM, transcendentals=pairs
         ),
@@ -426,47 +451,45 @@
     )(place, *sources)
 
 
-def join_kernel(place_ref, *refs, blocks, heads, head):
-    parts, out_ref, buf, sems = refs[:blocks], refs[-3], refs[-2], refs[-1]
+def join_kernel(place_ref, *refs, blocks, heads):
+    count = blocks * heads
+    parts, out_ref, buf, sems = refs[:count], refs[-3], refs[-2], refs[-1]
     place = place_ref[0]
     reads, writes = [], []
-    for r in range(blocks):
-        reads.append(pltpu.make_async_copy(parts[r], buf.at[r], sems.at[0, r]))
+    for n in range(count):
+        reads.append(pltpu.make_async_copy(parts[n], buf.at[n], sems.at[0, n]))
         reads[-1].start()
-    for r in range(blocks):
-        column = pl.multiple_of(((place ^ r) * heads + head) * HEAD_DIM, HEAD_DIM)
-        reads[r].wait()
+    for n in range(count):
+        column = pl.multiple_of(((place ^ (n % blocks)) * heads + n // blocks) * HEAD_DIM, HEAD_DIM)
+        reads[n].wait()
         writes.append(
-            pltpu.make_async_copy(
-                buf.at[r], out_ref.at[:, pl.ds(column, HEAD_DIM)], sems.at[1, r]
-            )
+            pltpu.make_async_copy(buf.at[n], out_ref.at[:, pl.ds(column, HEAD_DIM)], sems.at[1, n])
         )
         writes[-1].start()
     for write in writes:
         write.wait()
 
 
-def join(place, parts, whole, heads, head):
-    blocks = len(parts)
+def join(place, backs):
+    heads, blocks = len(backs), len(backs[0])
+    parts = [a for back in backs for a in back]
     rows = parts[0].shape[0]
-    fresh = whole is None
-    operands = tuple(parts) + (() if fresh else (whole,))
     return pl.pallas_call(
-        functools.partial(join_kernel, blocks=blocks, heads=heads, head=head),
+        functools.partial(join_kernel, blocks=blocks, heads=heads),
         in_specs=[pl.BlockSpec(memory_space=pltpu.SMEM)]
-        + [pl.BlockSpec(memory_space=pl.ANY)] * len(operands),
+        + [pl.BlockSpec(memory_space=pl.ANY)] * len(parts),
         out_specs=pl.BlockSpec(memory_space=pl.ANY),
         out_shape=jax.ShapeDtypeStruct((rows, blocks * heads * HEAD_DIM), BF16),
         scratch_shapes=[
-            pltpu.VMEM((blocks, rows, HEAD_DIM), BF16),
-            pltpu.SemaphoreType.DMA((2, blocks)),
+            pltpu.VMEM((len(parts), rows, HEAD_DIM), BF16),
+            pltpu.SemaphoreType.DMA((2, len(parts))),
         ],
-        input_output_aliases={} if fresh else {len(operands): 0},
+        compiler_params=WHOLE_VMEM,
         cost_estimate=pl.CostEstimate(
-            flops=0, bytes_accessed=4 * blocks * rows * HEAD_DIM, transcendentals=0
+            flops=0, bytes_accessed=4 * len(parts) * rows * HEAD_DIM, transcendentals=0
         ),
         name="join",
-    )(place, *operands)
+    )(place, *parts)
 
 
 def exchange_body(
@@ -492,42 +515,42 @@
     def swap(a, r):
         return lax.ppermute(a, "ctx", [(i, i ^ r) for i in range(ctx_size)])
 
-    order = sorted(range(1, ctx_size), key=lambda r: (-bin(r >> 1).count("1"), r)) + [0]
+    order = list(SENDS) + [0]
     got, backs = [], []
     sent = query_rows
+    lead = 2
     for h in range(heads):
-        packed = pack(where, (after(query_rows, sent), key_rows, value_rows), order, heads, h)
-        sent = packed[0]
+        mine = [None] * ctx_size
+        pieces = [order[:lead], order[lead:]] if h == 0 else [order]
+        for some in pieces:
+            packed = pack(where, (after(query_rows, sent), key_rows, value_rows), some, heads, h)
+            sent = packed[0]
+            for piece, r in zip(packed, some):
+                mine[r] = swap(piece, r) if r else piece
         if h == 0:
             rate, local_residue = gathered_modes(
                 decay_rate, residue, filter_index, tiles, tp_size, sent
             )
-        mine = [None] * ctx_size
-        for piece, r in zip(packed, order):
-            mine[r] = swap(piece, r) if r else piece
         got.append(mine)
     part, state = local_part(gate_inner, gate_outer, hyena_value, rate, local_residue, skip_gain)
     near = [state] + [swap(state, r) for r in range(1, SPAN)]
 
     for h in range(heads):
-        if h == heads - 1:
-            near = lax.optimization_barrier(tuple(near) + (backs[-1][0],))[:-1]
+        results = flash(where, got[h])
+        if h == heads - 2:
+            near = lax.optimization_barrier(tuple(near) + (results[0],))[:-1]
             before, total = gather_states(
                 jnp.stack([place.astype(jnp.int32), jnp.int32(row_count)]), rate, near
             )
             other = swap(total, SPAN)
-        results = flash(where, got[h])
-        backs.append([swap(a, r) if r else a for r, a in enumerate(results)])
+        back = list(results)
+        for r in SENDS:
+            back[r] = swap(results[r], r)
+        backs.append(back)
     before = after(before, backs[-1][0])
     hyena_output = remote_part(where, part, gate_outer, rate, local_residue, before, other)
-    attention_output = None
-    for h in range(heads):
-        attention_output = join(where, backs[h], attention_output, heads, h)
-        if h == heads - 2:
-            hyena_output, attention_output = lax.optimization_barrier(
-                (hyena_output, attention_output)
-            )
-    return (hyena_output, attention_output)
+    backs[-1][0] = after(backs[-1][0], hyena_output)
+    return (hyena_output, join(where, backs))
 
 
 def row_steps(folded, members, handler, span_rows):

time: 158 us -> 147 us (0.930)
  local copies, waits for them, and re-layouts: 11.2 us -> 2.41 us
  waiting for transfers between devices: 42.5 us -> 46.9 us
  starting transfers between devices: 37.2 us -> 33.4 us
  Pallas kernels: 63.7 us -> 61.7 us
    unnamed x72 -> x36, local copies, waits for them, and re-layouts: 9.64 us -> 0.81 us
    ppermute x32, waiting for transfers between devices: 40.8 us -> 43.2 us  [swap(): return lax.ppermute(a, 'ctx', [(i, i ^ r) for i in range(ctx_size)])]
    ppermute x32, starting transfers between devices: 31.1 us -> 28.7 us  [swap(): return lax.ppermute(a, 'ctx', [(i, i ^ r) for i in range(ctx_size)])]
    ppermute x3, waiting for transfers between devices: 1.67 us -> 3.7 us  [gathered_modes(): lax.ppermute(modes, 'tp', [(i, (i + shift) % tp_size) for i in range(tp_s...]
    pallas_call x2 -> x1, Pallas kernels: 4.17 us -> 2.57 us  [join(): pl.pallas_call(functools.partial(join_kernel, blocks=blocks, heads=heads)...]
    pallas_call x2 -> x3, Pallas kernels: 6.5 us -> 7.99 us  [pack(): pl.pallas_call(functools.partial(pack_kernel, spots=spots, heads=heads, h...]
  transfers between devices with their start and end apart: 35 -> 35, of which waited for: 9 -> 13; matrix products, arithmetic and copies ran while one was open for 2% -> 2% of each run, Pallas kernels for 37% -> 39%
where the time goes in v2:
time: 147 us; the launch traced here: 146 us
  Pallas kernels  61.7 us (42%)
  waiting for transfers between devices  46.9 us (32%)
  starting transfers between devices  33.4 us (23%)
  local copies, waits for them, and re-layouts  2.41 us (2%)
    ppermute x32, waiting for transfers between devices, swap(): return lax.ppermute(a, 'ctx', [(i, i ^ r) for i in range(ctx_size)])  43.2 us
    ppermute x32, starting transfers between devices, swap(): return lax.ppermute(a, 'ctx', [(i, i ^ r) for i in range(ctx_size)])  28.7 us
    pallas_call x2, Pallas kernels, flash(): pl.pallas_call(functools.partial(flash_kernel, blocks=blocks), in_specs=[...  27.2 us
    pallas_call x1, Pallas kernels, local_part(): pl.pallas_call(local_kernel, grid=grid, in_specs=[wide, wide, wide, row,...  15.9 us
    pallas_call x3, Pallas kernels, pack(): pl.pallas_call(functools.partial(pack_kernel, spots=spots, heads=heads, h...  7.99 us
    pallas_call x1, Pallas kernels, remote_part(): pl.pallas_call(remote_kernel, grid=grid, in_specs=[pl.BlockSpec(memory_sp...  6.37 us
    ppermute x3, starting transfers between devices, gathered_modes(): lax.ppermute(modes, 'tp', [(i, (i + shift) % tp_size) for i in range(tp_s...  4.67 us
    ppermute x3, waiting for transfers between devices, gathered_modes(): lax.ppermute(modes, 'tp', [(i, (i + shift) % tp_size) for i in range(tp_s...  3.7 us
  transfers between devices with their start and end apart: 35, of which 13 were waited for; matrix products, arithmetic and copies ran while one was open for 2% of the time, Pallas kernels for 39%

profile of v2, /device:TPU:0, one launch (start us, length us, event | category | flops | bytes accessed | tf_op | source)
XLA Modules:
  0.0 146.5 jit_solution(3050103895092004036)
XLA Ops:
  0.6 2.0 %pack.3 = (bf16[512,384]{1,0:T(8,128)(2,1)}, bf16[512,384]{1,0:T(8,128)(2,1)}) custom-call(s32[1]{0:T(128)} %bitcast.place_ref, bf16[512,2048]{1,0:T(8,128)(2,1)} %q_ref.2, bf16[512,2048]{1,0:T(8,128)(2,1)} %k_ref.5, bf16[512,2048]{1,0:T(8,128)(2,1)} %v_ref.5), custom_call_target="tpu_custom_call" | custom-call | bytes 1572864 | tf_op jit(solution)/shard_map/pack/pallas_call | solution.py:319
  2.7 4.0 %collective-permute-start.11 = (bf16[512,384]{1,0:T(8,128)(2,1)}, bf16[512,384]{1,0:T(8,128)(2,1)S(1)}, u32[]{:S(2)}, u32[]{:S(2)}) collective-permute-start(bf16[512,384]{1,0:T(8,128)(2,1)} %get-tuple-element.49), channel_id=1, source_target_pairs={{0,24},{4,28},{8,16},{12,20},{16,8},{20,12},{24,0},{28,4},{1,25},{... | collective-permute-start | bytes 1179656 | tf_op jit(solution)/shard_map/ppermute | solution.py:516
  6.7 2.7 %pack.4 = (bf16[512,384]{1,0:T(8,128)(2,1)}, bf16[512,384]{1,0:T(8,128)(2,1)}, bf16[512,384]{1,0:T(8,128)(2,1)}, bf16[512,384]{1,0:T(8,128)(2,1)}, bf16[512,384]{1,0:T(8,128)(2,1)}, /*index=5*/bf16[512,384]{1,0:T(8,128)(2,1)}) custom-call(s32[1]{0:T(128)} %bitcast.place_ref, bf16[512,2048]{1,0:T(8,128)(2,1)} %q_ref.2, bf16[512,2048]{1,0:T(8,128)(2,1)} %k_ref.5, ...), custom_call_target="tpu_custom_call" | custom-call | bytes 4718592 | tf_op jit(solution)/shard_map/pack/pallas_call | solution.py:319
  9.4 3.7 %collective-permute-start.2 = (f32[128,32]{0,1:T(8,128)S(1)}, f32[128,32]{0,1:T(8,128)S(1)}, u32[]{:S(2)}, u32[]{:S(2)}) collective-permute-start(f32[128,32]{0,1:T(8,128)S(1)} %pad_maximum_fusion), channel_id=1, source_target_pairs={{0,3},{1,0},{2,1},{3,2},{4,7},{5,4},{6,5},{7,6},{8,11},{9,8},{10,9... | collective-permute-start | bytes 49160 | tf_op jit(solution)/shard_map/ppermute | solution.py:195
  13.1 1.0 collective-permute-start
  14.8 2.9 %collective-permute-done.1 = f32[128,32]{0,1:T(8,128)S(1)} collective-permute-done((f32[128,32]{0,1:T(8,128)S(1)}, f32[128,32]{0,1:T(8,128)S(1)}, u32[]{:S(2)}, u32[]{:S(2)}) %collective-permute-start.1) | collective-permute-done | bytes 16416 | tf_op jit(solution)/shard_map/ppermute | solution.py:195
  17.7 0.5 collective-permute-start.7
  19.1 0.7 reshape.19
  19.9 0.7 reshape.18
  20.5 15.9 %local_part.1 = (f32[512,2048]{1,0:T(8,128)}, bf16[16,16,128]{2,1,0:T(8,128)(2,1)}) custom-call(bf16[512,2048]{1,0:T(8,128)(2,1)} %gate_ref.1, bf16[512,2048]{1,0:T(8,128)(2,1)} %outer_ref.3, bf16[512,2048]{1,0:T(8,128)(2,1)} %value_ref.1, f32[16,1,128]{2,1,0:T(1,128)} %bitcast.7, f32[16,1,128]{2,1,0:T(1,128)} %bitcast.10, f32[16,1,128]{2,1,0:T(1,128)} %bitcast.12), custom_call_target="tpu_custom_call" | custom-call | flops 4294967296 | bytes 10485760 | tf_op jit(solution)/shard_map/local_part/pallas_call | solution.py:227
  36.4 4.3 %collective-permute-done.5.refs_3_ = bf16[16,16,128]{2,1,0:T(8,128)(2,1)S(1)} collective-permute-done((bf16[16,16,128]{2,1,0:T(8,128)(2,1)}, bf16[16,16,128]{2,1,0:T(8,128)(2,1)S(1)}, u32[]{:S(2)}, u32[]{:S(2)}) %collective-permute-start.5) | collective-permute-done | bytes 65568 | tf_op jit(solution)/shard_map/ppermute | solution.py:516
  40.7 0.9 collective-permute-start.4
  41.6 3.6 %collective-permute-done.4.refs_2_ = bf16[16,16,128]{2,1,0:T(8,128)(2,1)S(1)} collective-permute-done((bf16[16,16,128]{2,1,0:T(8,128)(2,1)}, bf16[16,16,128]{2,1,0:T(8,128)(2,1)S(1)}, u32[]{:S(2)}, u32[]{:S(2)}) %collective-permute-start.4) | collective-permute-done | bytes 65568 | tf_op jit(solution)/shard_map/ppermute | solution.py:516
  45.2 1.5 collective-permute-done.3.refs_1_
  46.6 0.7 collective-permute-start.8
  47.8 3.2 %pack.5 = (bf16[512,384]{1,0:T(8,128)(2,1)}, bf16[512,384]{1,0:T(8,128)(2,1)}, bf16[512,384]{1,0:T(8,128)(2,1)}, bf16[512,384]{1,0:T(8,128)(2,1)}, bf16[512,384]...) custom-call(s32[1]{0:T(128)} %bitcast.place_ref, ...), custom_call_target="tpu_custom_call" | custom-call | bytes 6291456 | tf_op jit(solution)/shard_map/pack/pallas_call | solution.py:319
  51.1 1.6 %collective-permute-start.9 = (bf16[512,384]{1,0:T(8,128)(2,1)}, bf16[512,384]{1,0:T(8,128)(2,1)S(1)}, u32[]{:S(2)}, u32[]{:S(2)}) collective-permute-start(bf16[512,384]{1,0:T(8,128)(2,1)} %get-tuple-element.51), channel_id=1, source_target_pairs={{0,16},{4,20},{8,24},{12,28},{16,0},{20,4},{24,8},{28,12},{1,17},{... | collective-permute-start | bytes 1179656 | tf_op jit(solution)/shard_map/ppermute | solution.py:516
  52.7 1.2 collective-permute-start.14
  53.9 0.6 pad_add_fusion.place_ref
  54.5 3.5 %collective-permute-done.8.refs_3_ = bf16[512,384]{1,0:T(8,128)(2,1)} collective-permute-done((bf16[512,384]{1,0:T(8,128)(2,1)}, bf16[512,384]{1,0:T(8,128)(2,1)}, u32[]{:S(2)}, u32[]{:S(2)}) %collective-permute-start.8) | collective-permute-done | bytes 393248 | tf_op jit(solution)/shard_map/ppermute | solution.py:516
  58.0 1.3 collective-permute-start.15
  59.3 0.5 collective-permute-start.16
  59.8 8.0 %collective-permute-done.9.refs_4_ = bf16[512,384]{1,0:T(8,128)(2,1)S(1)} collective-permute-done((bf16[512,384]{1,0:T(8,128)(2,1)}, bf16[512,384]{1,0:T(8,128)(2,1)S(1)}, u32[]{:S(2)}, u32[]{:S(2)}) %collective-permute-start.9) | collective-permute-done | bytes 393248 | tf_op jit(solution)/shard_map/ppermute | solution.py:516
  67.9 0.7 copy-done.16
  68.6 1.1 collective-permute-start.18
  69.7 1.1 collective-permute-start.19
  70.8 13.7 %flash.2 = (bf16[512,128]{1,0:T(8,128)(2,1)}, bf16[512,128]{1,0:T(8,128)(2,1)}, bf16[512,128]{1,0:T(8,128)(2,1)}, bf16[512,128]{1,0:T(8,128)(2,1)}, bf16[512,128...) custom-call(s32[1]{0:T(128)} %bitcast.place_ref, ...), custom_call_target="tpu_custom_call" | custom-call | flops 9663676416 | bytes 4194304 | tf_op jit(solution)/shard_map/flash/pallas_call | solution.py:428
  84.5 1.8 %gather_states.1 = (f32[16,16,128]{2,1,0:T(8,128)}, bf16[16,16,128]{2,1,0:T(8,128)(2,1)}) custom-call(s32[2]{0:T(128)} %pad_add_fusion.place_ref, f32[16,1,128]{2,1,0:T(1,128)} %bitcast.8, bf16[16,16,128]{2,1,0:T(8,128)(2,1)} %get-tuple-element.62.refs_0_, bf16[16,16,128]{2,1,0:T(8,128)(2,1)} %copy-done.10, bf16[16,16,128]{2,1,0:T(8,128)(2,1)} %copy-done.9, ...), custom_call_target="tpu_custom_call" | custom-call | tf_op jit(solution)/shard_map/gather_states/pallas_call | solution.py:148
  86.3 1.0 collective-permute-start.21
  87.3 5.9 %collective-permute-done.16.refs_4_ = bf16[512,384]{1,0:T(8,128)(2,1)} collective-permute-done((bf16[512,384]{1,0:T(8,128)(2,1)}, bf16[512,384]{1,0:T(8,128)(2,1)}, u32[]{:S(2)}, u32[]{:S(2)}) %collective-permute-start.16) | collective-permute-done | bytes 393248 | tf_op jit(solution)/shard_map/ppermute | solution.py:516
  93.3 1.1 collective-permute-start.22
  94.4 6.2 %collective-permute-done.17.refs_5_ = bf16[512,384]{1,0:T(8,128)(2,1)} collective-permute-done((bf16[512,384]{1,0:T(8,128)(2,1)}, bf16[512,384]{1,0:T(8,128)(2,1)}, u32[]{:S(2)}, u32[]{:S(2)}) %collective-permute-start.17) | collective-permute-done | bytes 393248 | tf_op jit(solution)/shard_map/ppermute | solution.py:516
  100.6 1.1 collective-permute-start.23
  102.2 1.5 %collective-permute-start.20 = (bf16[16,16,128]{2,1,0:T(8,128)(2,1)}, bf16[16,16,128]{2,1,0:T(8,128)(2,1)S(1)}, u32[]{:S(2)}, u32[]{:S(2)}) collective-permute-start(bf16[16,16,128]{2,1,0:T(8,128)(2,1)} %get-tuple-element.78), channel_id=1, source_target_pairs={{0,16},{4,20},{8,24},{12,28},{16,0},{20,4},{24,8},{28,12},{1,17},{... | collective-permute-start | bytes 196616 | tf_op jit(solution)/shard_map/ppermute | solution.py:516
  103.8 13.5 %flash.3 = (bf16[512,128]{1,0:T(8,128)(2,1)}, bf16[512,128]{1,0:T(8,128)(2,1)}, bf16[512,128]{1,0:T(8,128)(2,1)}, bf16[512,128]{1,0:T(8,128)(2,1)}, bf16[512,128...) custom-call(s32[1]{0:T(128)} %bitcast.place_ref, ...), custom_call_target="tpu_custom_call" | custom-call | flops 9663676416 | bytes 4194304 | tf_op jit(solution)/shard_map/flash/pallas_call | solution.py:428
  117.7 1.6 %collective-permute-start.26 = (bf16[512,128]{1,0:T(8,128)(2,1)}, bf16[512,128]{1,0:T(8,128)(2,1)S(1)}, u32[]{:S(2)}, u32[]{:S(2)}) collective-permute-start(bf16[512,128]{1,0:T(8,128)(2,1)} %get-tuple-element.84), channel_id=1, source_target_pairs={{0,24},{4,28},{8,16},{12,20},{16,8},{20,12},{24,0},{28,4},{1,25},{... | collective-permute-start | bytes 393224 | tf_op jit(solution)/shard_map/ppermute | solution.py:516
  119.3 1.4 collective-permute-start.27
  120.7 1.2 collective-permute-start.29
  121.9 6.9 %collective-permute-done.25.refs_5_ = bf16[512,128]{1,0:T(8,128)(2,1)S(1)} collective-permute-done((bf16[512,128]{1,0:T(8,128)(2,1)}, bf16[512,128]{1,0:T(8,128)(2,1)S(1)}, u32[]{:S(2)}, u32[]{:S(2)}) %collective-permute-start.25) | collective-permute-done | bytes 131104 | tf_op jit(solution)/shard_map/ppermute | solution.py:516
  128.9 0.8 collective-permute-start.30
  129.7 1.0 collective-permute-start.31
  130.7 0.8 collective-permute-start.32
  131.5 1.3 collective-permute-start.33
  132.8 1.3 collective-permute-start.34
  134.1 6.4 %remote_part.1 = bf16[512,2048]{1,0:T(8,128)(2,1)} custom-call(s32[1]{0:T(128)} %bitcast.place_ref, f32[512,2048]{1,0:T(8,128)} %get-tuple-element.53.part_ref, bf16[512,2048]{1,0:T(8,128)(2,1)} %outer_ref.3, f32[16,1,128]{2,1,0:T(1,128)} %bitcast.9, f32[16,1,128]{2,1,0:T(1,128)} %bitcast.11, f32[16,16,128]{2,1,0:T(8,128)} %get-tuple-element.77.before_ref, ...), custom_call_target="tpu_custom_call" | custom-call | flops 805306368 | bytes 8388608 | tf_op jit(solution)/shard_map/remote_part/pallas_call | solution.py:250
  140.6 1.5 collective-permute-done.31.refs_12_
  142.0 1.7 %collective-permute-done.32.refs_13_ = bf16[512,128]{1,0:T(8,128)(2,1)} collective-permute-done((bf16[512,128]{1,0:T(8,128)(2,1)}, bf16[512,128]{1,0:T(8,128)(2,1)}, u32[]{:S(2)}, u32[]{:S(2)}) %collective-permute-start.32) | collective-permute-done | bytes 131104 | tf_op jit(solution)/shard_map/ppermute | solution.py:516
  143.7 2.6 %join.1 = bf16[512,2048]{1,0:T(8,128)(2,1)} custom-call(s32[1]{0:T(128)} %bitcast.place_ref, bf16[512,128]{1,0:T(8,128)(2,1)} %get-tuple-element.61.refs_0_, bf16[512,128]{1,0:T(8,128)(2,1)} %copy-done, bf16[512,128]{1,0:T(8,128)(2,1)} %copy-done.1, bf16[512,128]{1,0:T(8,128)(2,1)} %copy-done.2, bf16[512,128]{1,0:T(8,128)(2,1)} %copy-done.3, ...), custom_call_target="tpu_custom_call" | custom-call | bytes 4194304 | tf_op jit(solution)/shard_map/join/pallas_call | solution.py:477
  (76 shorter events, 3.1 us)
Async XLA Ops:
  2.7 6.7 %copy-start.11 = (f32[128,16]{0,1:T(8,128)S(1)}, f32[128,16]{0,1:T(8,128)}, u32[]{:S(2)}) copy-start(f32[128,16]{0,1:T(8,128)} %param.14) | copy-start | bytes 24580
  2.7 11.4 %copy-start.17 = (s32[128]{0:T(128)S(1)}, s32[128]{0:T(128)}, u32[]{:S(2)}) copy-start(s32[128]{0:T(128)} %param.16) | copy-start | bytes 1540
  2.7 48.3 %collective-permute-start.11 = (bf16[512,384]{1,0:T(8,128)(2,1)}, bf16[512,384]{1,0:T(8,128)(2,1)S(1)}, u32[]{:S(2)}, u32[]{:S(2)}) collective-permute-start(bf16[512,384]{1,0:T(8,128)(2,1)} %get-tuple-element.49), channel_id=1, source_target_pairs={{0,24},{4,28},{8,16},{12,20},{16,8},{20,12},{24,0},{28,4},{1,25},{... | collective-permute-start | bytes 1179656 | tf_op jit(solution)/shard_map/ppermute | solution.py:516
  9.4 5.1 %collective-permute-start.2 = (f32[128,32]{0,1:T(8,128)S(1)}, f32[128,32]{0,1:T(8,128)S(1)}, u32[]{:S(2)}, u32[]{:S(2)}) collective-permute-start(f32[128,32]{0,1:T(8,128)S(1)} %pad_maximum_fusion), channel_id=1, source_target_pairs={{0,3},{1,0},{2,1},{3,2},{4,7},{5,4},{6,5},{7,6},{8,11},{9,8},{10,9... | collective-permute-start | bytes 49160 | tf_op jit(solution)/shard_map/ppermute | solution.py:195
  13.1 4.6 %collective-permute-start.1 = (f32[128,32]{0,1:T(8,128)S(1)}, f32[128,32]{0,1:T(8,128)S(1)}, u32[]{:S(2)}, u32[]{:S(2)}) collective-permute-start(f32[128,32]{0,1:T(8,128)S(1)} %pad_maximum_fusion), channel_id=1, source_target_pairs={{0,2},{1,3},{2,0},{3,1},{4,6},{5,7},{6,4},{7,5},{8,10},{9,11},{10,... | collective-permute-start | bytes 49160 | tf_op jit(solution)/shard_map/ppermute | solution.py:195
  13.1 5.5 %collective-permute-start = (f32[128,32]{0,1:T(8,128)S(1)}, f32[128,32]{0,1:T(8,128)S(1)}, u32[]{:S(2)}, u32[]{:S(2)}) collective-permute-start(f32[128,32]{0,1:T(8,128)S(1)} %pad_maximum_fusion), channel_id=1, source_target_pairs={{0,1},{1,2},{2,3},{3,0},{4,5},{5,6},{6,7},{7,4},{8,9},{9,10},{10,1... | collective-permute-start | bytes 49160 | tf_op jit(solution)/shard_map/ppermute | solution.py:195
  14.1 33.2 %collective-permute-start.12 = (bf16[512,384]{1,0:T(8,128)(2,1)}, bf16[512,384]{1,0:T(8,128)(2,1)S(1)}, u32[]{:S(2)}, u32[]{:S(2)}) collective-permute-start(bf16[512,384]{1,0:T(8,128)(2,1)} %get-tuple-element.60), channel_id=1, source_target_pairs={{0,28},{4,24},{8,20},{12,16},{16,12},{20,8},{24,4},{28,0},{1,29},{... | collective-permute-start | bytes 1179656 | tf_op jit(solution)/shard_map/ppermute | solution.py:516
  14.5 38.1 %collective-permute-start.6 = (bf16[512,384]{1,0:T(8,128)(2,1)}, bf16[512,384]{1,0:T(8,128)(2,1)}, u32[]{:S(2)}, u32[]{:S(2)}) collective-permute-start(bf16[512,384]{1,0:T(8,128)(2,1)} %get-tuple-element.56), channel_id=1, source_target_pairs={{0,4},{4,0},{8,12},{12,8},{16,20},{20,16},{24,28},{28,24},{1,5},{5... | collective-permute-start | bytes 1179656 | tf_op jit(solution)/shard_map/ppermute | solution.py:516
  17.7 34.9 %collective-permute-start.7 = (bf16[512,384]{1,0:T(8,128)(2,1)}, bf16[512,384]{1,0:T(8,128)(2,1)}, u32[]{:S(2)}, u32[]{:S(2)}) collective-permute-start(bf16[512,384]{1,0:T(8,128)(2,1)} %get-tuple-element.57), channel_id=1, source_target_pairs={{0,8},{4,12},{8,0},{12,4},{16,24},{20,28},{24,16},{28,20},{1,9},{5... | collective-permute-start | bytes 1179656 | tf_op jit(solution)/shard_map/ppermute | solution.py:516
  36.4 4.3 %collective-permute-start.5 = (bf16[16,16,128]{2,1,0:T(8,128)(2,1)}, bf16[16,16,128]{2,1,0:T(8,128)(2,1)S(1)}, u32[]{:S(2)}, u32[]{:S(2)}) collective-permute-start(bf16[16,16,128]{2,1,0:T(8,128)(2,1)} %get-tuple-element.62.refs_0_), channel_id=1, source_target_pairs={{0,12},{4,8},{8,4},{12,0},{16,28},{20,24},{24,20},{28,16},{1,13},{... | collective-permute-start | bytes 196616 | tf_op jit(solution)/shard_map/ppermute | solution.py:516
  40.7 10.3 %copy-start.8 = (bf16[16,16,128]{2,1,0:T(8,128)(2,1)}, bf16[16,16,128]{2,1,0:T(8,128)(2,1)S(1)}, u32[]{:S(2)}) copy-start(bf16[16,16,128]{2,1,0:T(8,128)(2,1)S(1)} %collective-permute-done.5.refs_3_) | copy-start | bytes 196612
  40.7 4.5 %collective-permute-start.4 = (bf16[16,16,128]{2,1,0:T(8,128)(2,1)}, bf16[16,16,128]{2,1,0:T(8,128)(2,1)S(1)}, u32[]{:S(2)}, u32[]{:S(2)}) collective-permute-start(bf16[16,16,128]{2,1,0:T(8,128)(2,1)} %get-tuple-element.62.refs_0_), channel_id=1, source_target_pairs={{0,8},{4,12},{8,0},{12,4},{16,24},{20,28},{24,16},{28,20},{1,9},{5... | collective-permute-start | bytes 196616 | tf_op jit(solution)/shard_map/ppermute | solution.py:516
  45.2 1.5 %collective-permute-start.3 = (bf16[16,16,128]{2,1,0:T(8,128)(2,1)}, bf16[16,16,128]{2,1,0:T(8,128)(2,1)S(1)}, u32[]{:S(2)}, u32[]{:S(2)}) collective-permute-start(bf16[16,16,128]{2,1,0:T(8,128)(2,1)} %get-tuple-element.62.refs_0_), channel_id=1, source_target_pairs={{0,4},{4,0},{8,12},{12,8},{16,20},{20,16},{24,28},{28,24},{1,5},{5... | collective-permute-start | bytes 196616 | tf_op jit(solution)/shard_map/ppermute | solution.py:516
  46.6 11.4 %collective-permute-start.8 = (bf16[512,384]{1,0:T(8,128)(2,1)}, bf16[512,384]{1,0:T(8,128)(2,1)}, u32[]{:S(2)}, u32[]{:S(2)}) collective-permute-start(bf16[512,384]{1,0:T(8,128)(2,1)} %get-tuple-element.58), channel_id=1, source_target_pairs={{0,12},{4,8},{8,4},{12,0},{16,28},{20,24},{24,20},{28,16},{1,13},{... | collective-permute-start | bytes 1179656 | tf_op jit(solution)/shard_map/ppermute | solution.py:516
  47.3 12.0 %collective-permute-start.10 = (bf16[512,384]{1,0:T(8,128)(2,1)}, bf16[512,384]{1,0:T(8,128)(2,1)}, u32[]{:S(2)}, u32[]{:S(2)}) collective-permute-start(bf16[512,384]{1,0:T(8,128)(2,1)} %get-tuple-element.59), channel_id=1, source_target_pairs={{0,20},{4,16},{8,28},{12,24},{16,4},{20,0},{24,12},{28,8},{1,21},{... | collective-permute-start | bytes 1179656 | tf_op jit(solution)/shard_map/ppermute | solution.py:516
  51.1 19.8 %copy-start.13 = (bf16[512,384]{1,0:T(8,128)(2,1)}, bf16[512,384]{1,0:T(8,128)(2,1)S(1)}, u32[]{:S(2)}) copy-start(bf16[512,384]{1,0:T(8,128)(2,1)S(1)} %collective-permute-done.11.refs_6_) | copy-start | bytes 1179652
  51.1 16.8 %collective-permute-start.9 = (bf16[512,384]{1,0:T(8,128)(2,1)}, bf16[512,384]{1,0:T(8,128)(2,1)S(1)}, u32[]{:S(2)}, u32[]{:S(2)}) collective-permute-start(bf16[512,384]{1,0:T(8,128)(2,1)} %get-tuple-element.51), channel_id=1, source_target_pairs={{0,16},{4,20},{8,24},{12,28},{16,0},{20,4},{24,8},{28,12},{1,17},{... | collective-permute-start | bytes 1179656 | tf_op jit(solution)/shard_map/ppermute | solution.py:516
  52.7 15.2 %collective-permute-start.13 = (bf16[512,384]{1,0:T(8,128)(2,1)}, bf16[512,384]{1,0:T(8,128)(2,1)S(1)}, u32[]{:S(2)}, u32[]{:S(2)}) collective-permute-start(bf16[512,384]{1,0:T(8,128)(2,1)} %get-tuple-element.69), channel_id=1, source_target_pairs={{0,4},{4,0},{8,12},{12,8},{16,20},{20,16},{24,28},{28,24},{1,5},{5... | collective-permute-start | bytes 1179656 | tf_op jit(solution)/shard_map/ppermute | solution.py:516
  52.7 17.0 %collective-permute-start.14 = (bf16[512,384]{1,0:T(8,128)(2,1)}, bf16[512,384]{1,0:T(8,128)(2,1)}, u32[]{:S(2)}, u32[]{:S(2)}) collective-permute-start(bf16[512,384]{1,0:T(8,128)(2,1)} %get-tuple-element.70), channel_id=1, source_target_pairs={{0,8},{4,12},{8,0},{12,4},{16,24},{20,28},{24,16},{28,20},{1,9},{5... | collective-permute-start | bytes 1179656 | tf_op jit(solution)/shard_map/ppermute | solution.py:516
  58.0 28.3 %collective-permute-start.15 = (bf16[512,384]{1,0:T(8,128)(2,1)}, bf16[512,384]{1,0:T(8,128)(2,1)}, u32[]{:S(2)}, u32[]{:S(2)}) collective-permute-start(bf16[512,384]{1,0:T(8,128)(2,1)} %get-tuple-element.71), channel_id=1, source_target_pairs={{0,12},{4,8},{8,4},{12,0},{16,28},{20,24},{24,20},{28,16},{1,13},{... | collective-permute-start | bytes 1179656 | tf_op jit(solution)/shard_map/ppermute | solution.py:516
  59.3 33.9 %collective-permute-start.16 = (bf16[512,384]{1,0:T(8,128)(2,1)}, bf16[512,384]{1,0:T(8,128)(2,1)}, u32[]{:S(2)}, u32[]{:S(2)}) collective-permute-start(bf16[512,384]{1,0:T(8,128)(2,1)} %get-tuple-element.72), channel_id=1, source_target_pairs={{0,16},{4,20},{8,24},{12,28},{16,0},{20,4},{24,8},{28,12},{1,17},{... | collective-permute-start | bytes 1179656 | tf_op jit(solution)/shard_map/ppermute | solution.py:516
  67.9 32.8 %collective-permute-start.17 = (bf16[512,384]{1,0:T(8,128)(2,1)}, bf16[512,384]{1,0:T(8,128)(2,1)}, u32[]{:S(2)}, u32[]{:S(2)}) collective-permute-start(bf16[512,384]{1,0:T(8,128)(2,1)} %get-tuple-element.73), channel_id=1, source_target_pairs={{0,20},{4,16},{8,28},{12,24},{16,4},{20,0},{24,12},{28,8},{1,21},{... | collective-permute-start | bytes 1179656 | tf_op jit(solution)/shard_map/ppermute | solution.py:516
  68.6 15.9 %copy-start.15 = (bf16[512,384]{1,0:T(8,128)(2,1)}, bf16[512,384]{1,0:T(8,128)(2,1)S(1)}, u32[]{:S(2)}) copy-start(bf16[512,384]{1,0:T(8,128)(2,1)S(1)} %collective-permute-done.13.refs_1_) | copy-start | bytes 1179652
  68.6 33.1 %collective-permute-start.18 = (bf16[512,384]{1,0:T(8,128)(2,1)}, bf16[512,384]{1,0:T(8,128)(2,1)}, u32[]{:S(2)}, u32[]{:S(2)}) collective-permute-start(bf16[512,384]{1,0:T(8,128)(2,1)} %get-tuple-element.74), channel_id=1, source_target_pairs={{0,24},{4,28},{8,16},{12,20},{16,8},{20,12},{24,0},{28,4},{1,25},{... | collective-permute-start | bytes 1179656 | tf_op jit(solution)/shard_map/ppermute | solution.py:516
  69.7 32.5 %collective-permute-start.19 = (bf16[512,384]{1,0:T(8,128)(2,1)}, bf16[512,384]{1,0:T(8,128)(2,1)}, u32[]{:S(2)}, u32[]{:S(2)}) collective-permute-start(bf16[512,384]{1,0:T(8,128)(2,1)} %get-tuple-element.75), channel_id=1, source_target_pairs={{0,28},{4,24},{8,20},{12,16},{16,12},{20,8},{24,4},{28,0},{1,29},{... | collective-permute-start | bytes 1179656 | tf_op jit(solution)/shard_map/ppermute | solution.py:516
  86.3 31.3 %collective-permute-start.21 = (bf16[512,128]{1,0:T(8,128)(2,1)}, bf16[512,128]{1,0:T(8,128)(2,1)S(1)}, u32[]{:S(2)}, u32[]{:S(2)}) collective-permute-start(bf16[512,128]{1,0:T(8,128)(2,1)} %get-tuple-element.79), channel_id=1, source_target_pairs={{0,4},{4,0},{8,12},{12,8},{16,20},{20,16},{24,28},{28,24},{1,5},{5... | collective-permute-start | bytes 393224 | tf_op jit(solution)/shard_map/ppermute | solution.py:516
  93.3 26.0 %collective-permute-start.22 = (bf16[512,128]{1,0:T(8,128)(2,1)}, bf16[512,128]{1,0:T(8,128)(2,1)S(1)}, u32[]{:S(2)}, u32[]{:S(2)}) collective-permute-start(bf16[512,128]{1,0:T(8,128)(2,1)} %get-tuple-element.80), channel_id=1, source_target_pairs={{0,8},{4,12},{8,0},{12,4},{16,24},{20,28},{24,16},{28,20},{1,9},{5... | collective-permute-start | bytes 393224 | tf_op jit(solution)/shard_map/ppermute | solution.py:516
  100.6 20.1 %collective-permute-start.23 = (bf16[512,128]{1,0:T(8,128)(2,1)}, bf16[512,128]{1,0:T(8,128)(2,1)S(1)}, u32[]{:S(2)}, u32[]{:S(2)}) collective-permute-start(bf16[512,128]{1,0:T(8,128)(2,1)} %get-tuple-element.81), channel_id=1, source_target_pairs={{0,12},{4,8},{8,4},{12,0},{16,28},{20,24},{24,20},{28,16},{1,13},{... | collective-permute-start | bytes 393224 | tf_op jit(solution)/shard_map/ppermute | solution.py:516
  101.7 19.0 %collective-permute-start.24 = (bf16[512,128]{1,0:T(8,128)(2,1)}, bf16[512,128]{1,0:T(8,128)(2,1)S(1)}, u32[]{:S(2)}, u32[]{:S(2)}) collective-permute-start(bf16[512,128]{1,0:T(8,128)(2,1)} %get-tuple-element.82), channel_id=1, source_target_pairs={{0,16},{4,20},{8,24},{12,28},{16,0},{20,4},{24,8},{28,12},{1,17},{... | collective-permute-start | bytes 393224 | tf_op jit(solution)/shard_map/ppermute | solution.py:516
  102.2 15.0 %collective-permute-start.20 = (bf16[16,16,128]{2,1,0:T(8,128)(2,1)}, bf16[16,16,128]{2,1,0:T(8,128)(2,1)S(1)}, u32[]{:S(2)}, u32[]{:S(2)}) collective-permute-start(bf16[16,16,128]{2,1,0:T(8,128)(2,1)} %get-tuple-element.78), channel_id=1, source_target_pairs={{0,16},{4,20},{8,24},{12,28},{16,0},{20,4},{24,8},{28,12},{1,17},{... | collective-permute-start | bytes 196616 | tf_op jit(solution)/shard_map/ppermute | solution.py:516
  117.2 16.9 %copy-start.7 = (bf16[16,16,128]{2,1,0:T(8,128)(2,1)}, bf16[16,16,128]{2,1,0:T(8,128)(2,1)S(1)}, u32[]{:S(2)}) copy-start(bf16[16,16,128]{2,1,0:T(8,128)(2,1)S(1)} %collective-permute-done.20.other_ref) | copy-start | bytes 196612
  117.2 11.6 %collective-permute-start.25 = (bf16[512,128]{1,0:T(8,128)(2,1)}, bf16[512,128]{1,0:T(8,128)(2,1)S(1)}, u32[]{:S(2)}, u32[]{:S(2)}) collective-permute-start(bf16[512,128]{1,0:T(8,128)(2,1)} %get-tuple-element.83), channel_id=1, source_target_pairs={{0,20},{4,16},{8,28},{12,24},{16,4},{20,0},{24,12},{28,8},{1,21},{... | collective-permute-start | bytes 393224 | tf_op jit(solution)/shard_map/ppermute | solution.py:516
  117.7 22.8 %copy-start = (bf16[512,128]{1,0:T(8,128)(2,1)}, bf16[512,128]{1,0:T(8,128)(2,1)S(1)}, u32[]{:S(2)}) copy-start(bf16[512,128]{1,0:T(8,128)(2,1)S(1)} %collective-permute-done.21.refs_1_) | copy-start | bytes 393220
  117.7 12.1 %collective-permute-start.26 = (bf16[512,128]{1,0:T(8,128)(2,1)}, bf16[512,128]{1,0:T(8,128)(2,1)S(1)}, u32[]{:S(2)}, u32[]{:S(2)}) collective-permute-start(bf16[512,128]{1,0:T(8,128)(2,1)} %get-tuple-element.84), channel_id=1, source_target_pairs={{0,24},{4,28},{8,16},{12,20},{16,8},{20,12},{24,0},{28,4},{1,25},{... | collective-permute-start | bytes 393224 | tf_op jit(solution)/shard_map/ppermute | solution.py:516
  119.3 21.2 %copy-start.1 = (bf16[512,128]{1,0:T(8,128)(2,1)}, bf16[512,128]{1,0:T(8,128)(2,1)S(1)}, u32[]{:S(2)}) copy-start(bf16[512,128]{1,0:T(8,128)(2,1)S(1)} %collective-permute-done.22.refs_2_) | copy-start | bytes 393220
  119.3 11.4 %collective-permute-start.27 = (bf16[512,128]{1,0:T(8,128)(2,1)}, bf16[512,128]{1,0:T(8,128)(2,1)S(1)}, u32[]{:S(2)}, u32[]{:S(2)}) collective-permute-start(bf16[512,128]{1,0:T(8,128)(2,1)} %get-tuple-element.85), channel_id=1, source_target_pairs={{0,28},{4,24},{8,20},{12,16},{16,12},{20,8},{24,4},{28,0},{1,29},{... | collective-permute-start | bytes 393224 | tf_op jit(solution)/shard_map/ppermute | solution.py:516
  120.7 19.8 %copy-start.2 = (bf16[512,128]{1,0:T(8,128)(2,1)}, bf16[512,128]{1,0:T(8,128)(2,1)S(1)}, u32[]{:S(2)}) copy-start(bf16[512,128]{1,0:T(8,128)(2,1)S(1)} %collective-permute-done.23.refs_3_) | copy-start | bytes 393220
  120.7 10.8 %collective-permute-start.28 = (bf16[512,128]{1,0:T(8,128)(2,1)}, bf16[512,128]{1,0:T(8,128)(2,1)}, u32[]{:S(2)}, u32[]{:S(2)}) collective-permute-start(bf16[512,128]{1,0:T(8,128)(2,1)} %get-tuple-element.87), channel_id=1, source_target_pairs={{0,4},{4,0},{8,12},{12,8},{16,20},{20,16},{24,28},{28,24},{1,5},{5... | collective-permute-start | bytes 393224 | tf_op jit(solution)/shard_map/ppermute | solution.py:516
  120.7 19.8 %copy-start.3 = (bf16[512,128]{1,0:T(8,128)(2,1)}, bf16[512,128]{1,0:T(8,128)(2,1)S(1)}, u32[]{:S(2)}) copy-start(bf16[512,128]{1,0:T(8,128)(2,1)S(1)} %collective-permute-done.24.refs_4_) | copy-start | bytes 393220
  120.7 12.1 %collective-permute-start.29 = (bf16[512,128]{1,0:T(8,128)(2,1)}, bf16[512,128]{1,0:T(8,128)(2,1)}, u32[]{:S(2)}, u32[]{:S(2)}) collective-permute-start(bf16[512,128]{1,0:T(8,128)(2,1)} %get-tuple-element.88), channel_id=1, source_target_pairs={{0,8},{4,12},{8,0},{12,4},{16,24},{20,28},{24,16},{28,20},{1,9},{5... | collective-permute-start | bytes 393224 | tf_op jit(solution)/shard_map/ppermute | solution.py:516
  128.9 11.7 %copy-start.4 = (bf16[512,128]{1,0:T(8,128)(2,1)}, bf16[512,128]{1,0:T(8,128)(2,1)S(1)}, u32[]{:S(2)}) copy-start(bf16[512,128]{1,0:T(8,128)(2,1)S(1)} %collective-permute-done.25.refs_5_) | copy-start | bytes 393220
  128.9 11.7 %collective-permute-start.30 = (bf16[512,128]{1,0:T(8,128)(2,1)}, bf16[512,128]{1,0:T(8,128)(2,1)}, u32[]{:S(2)}, u32[]{:S(2)}) collective-permute-start(bf16[512,128]{1,0:T(8,128)(2,1)} %get-tuple-element.89), channel_id=1, source_target_pairs={{0,12},{4,8},{8,4},{12,0},{16,28},{20,24},{24,20},{28,16},{1,13},{... | collective-permute-start | bytes 393224 | tf_op jit(solution)/shard_map/ppermute | solution.py:516
  129.7 10.8 %copy-start.5 = (bf16[512,128]{1,0:T(8,128)(2,1)}, bf16[512,128]{1,0:T(8,128)(2,1)S(1)}, u32[]{:S(2)}) copy-start(bf16[512,128]{1,0:T(8,128)(2,1)S(1)} %collective-permute-done.26.refs_6_) | copy-start | bytes 393220
  129.7 12.3 %collective-permute-start.31 = (bf16[512,128]{1,0:T(8,128)(2,1)}, bf16[512,128]{1,0:T(8,128)(2,1)}, u32[]{:S(2)}, u32[]{:S(2)}) collective-permute-start(bf16[512,128]{1,0:T(8,128)(2,1)} %get-tuple-element.90), channel_id=1, source_target_pairs={{0,16},{4,20},{8,24},{12,28},{16,0},{20,4},{24,8},{28,12},{1,17},{... | collective-permute-start | bytes 393224 | tf_op jit(solution)/shard_map/ppermute | solution.py:516
  130.7 9.8 %copy-start.6 = (bf16[512,128]{1,0:T(8,128)(2,1)}, bf16[512,128]{1,0:T(8,128)(2,1)S(1)}, u32[]{:S(2)}) copy-start(bf16[512,128]{1,0:T(8,128)(2,1)S(1)} %collective-permute-done.27.refs_7_) | copy-start | bytes 393220
  130.7 13.0 %collective-permute-start.32 = (bf16[512,128]{1,0:T(8,128)(2,1)}, bf16[512,128]{1,0:T(8,128)(2,1)}, u32[]{:S(2)}, u32[]{:S(2)}) collective-permute-start(bf16[512,128]{1,0:T(8,128)(2,1)} %get-tuple-element.91), channel_id=1, source_target_pairs={{0,20},{4,16},{8,28},{12,24},{16,4},{20,0},{24,12},{28,8},{1,21},{... | collective-permute-start | bytes 393224 | tf_op jit(solution)/shard_map/ppermute | solution.py:516
  131.5 12.2 %collective-permute-start.33 = (bf16[512,128]{1,0:T(8,128)(2,1)}, bf16[512,128]{1,0:T(8,128)(2,1)}, u32[]{:S(2)}, u32[]{:S(2)}) collective-permute-start(bf16[512,128]{1,0:T(8,128)(2,1)} %get-tuple-element.92), channel_id=1, source_target_pairs={{0,24},{4,28},{8,16},{12,20},{16,8},{20,12},{24,0},{28,4},{1,25},{... | collective-permute-start | bytes 393224 | tf_op jit(solution)/shard_map/ppermute | solution.py:516
  132.8 10.9 %collective-permute-start.34 = (bf16[512,128]{1,0:T(8,128)(2,1)}, bf16[512,128]{1,0:T(8,128)(2,1)}, u32[]{:S(2)}, u32[]{:S(2)}) collective-permute-start(bf16[512,128]{1,0:T(8,128)(2,1)} %get-tuple-element.93), channel_id=1, source_target_pairs={{0,28},{4,24},{8,20},{12,16},{16,12},{20,8},{24,4},{28,0},{1,29},{... | collective-permute-start | bytes 393224 | tf_op jit(solution)/shard_map/ppermute | solution.py:516
  (5 other events, 21.5 us)

commit v3 on v2

--- a/solution.py
+++ b/solution.py
@@ -20,6 +20,7 @@
 
 floor_score = -1e30
 LOG2E = 1.4426950408889634
+TOO_SMALL = 2.0**-80
 
 
 F32 = jnp.float32
@@ -125,35 +126,37 @@
             out_ref[b * CHUNK : (b + 1) * CHUNK, lanes] = gate * convolved
 
 
-def gather_kernel(place_ref, rate_ref, *refs):
-    nears, (before_ref, total_ref) = refs[:SPAN], refs[SPAN:]
-    spot = place_ref[0] % SPAN
+def pair_kernel(place_ref, rate_ref, mine_ref, other_ref, total_ref):
+    mine, other = mine_ref[...].astype(F32), other_ref[...].astype(F32)
+    second = place_ref[0] % 2 == 1
+    lower, upper = jnp.where(second, other, mine), jnp.where(second, mine, other)
+    rows = place_ref[1].astype(F32)
+    total_ref[...] = (lower * jnp.exp(-rate_ref[...] * rows) + upper).astype(BF16)
+
+
+def gather_kernel(place_ref, rate_ref, other_ref, pair_ref, far_ref, before_ref, total_ref):
+    core, side = place_ref[0] % 2, (place_ref[0] // 2) % 2
     rows = place_ref[1].astype(F32)
     rate = rate_ref[...]
-    before = jnp.zeros(before_ref.shape, F32)
-    total = jnp.zeros(before_ref.shape, F32)
-    for r, near in enumerate(nears):
-        value = near[...].astype(F32)
-        j = spot ^ r
-        ahead = jnp.maximum(spot - 1 - j, 0).astype(F32) * rows
-        faded = value * jnp.exp(-rate * ahead)
-        before += jnp.where(j < spot, faded, 0.0)
-        total += value * jnp.exp(-rate * ((SPAN - 1 - j).astype(F32) * rows))
-    before_ref[...] = before
-    total_ref[...] = total.astype(BF16)
-
-
-def gather_states(where, rate, nears):
-    shape = nears[0].shape
+    pair, far = pair_ref[...].astype(F32), far_ref[...].astype(F32)
+    faded = far * jnp.exp(-rate * (core.astype(F32) * rows))
+    before_ref[...] = jnp.where(core == 1, other_ref[...].astype(F32), 0.0) + jnp.where(
+        side == 1, faded, 0.0
+    )
+    lower, upper = jnp.where(side == 1, far, pair), jnp.where(side == 1, pair, far)
+    total_ref[...] = (lower * jnp.exp(-rate * (2.0 * rows)) + upper).astype(BF16)
+
+
+def state_call(kernel, where, rate, states, kinds):
+    shape = states[0].shape
     return pl.pallas_call(
-        gather_kernel,
+        kernel,
         in_specs=[pl.BlockSpec(memory_space=pltpu.SMEM)]
-        + [pl.BlockSpec(memory_space=pltpu.VMEM)] * (1 + SPAN),
-        out_specs=[pl.BlockSpec(memory_space=pltpu.VMEM)] * 2,
-        out_shape=[jax.ShapeDtypeStruct(shape, F32), jax.ShapeDtypeStruct(shape, BF16)],
+        + [pl.BlockSpec(memory_space=pltpu.VMEM)] * (1 + len(states)),
+        out_specs=[pl.BlockSpec(memory_space=pltpu.VMEM)] * len(kinds),
+        out_shape=[jax.ShapeDtypeStruct(shape, kind) for kind in kinds],
         compiler_params=WHOLE_VMEM,
-        name="gather_states",
-    )(where, rate, *nears)
+    )(where, rate, *states)
 
 
 def remote_kernel(
@@ -290,7 +293,7 @@
 
 def pack_kernel(place_ref, q_ref, k_ref, v_ref, *refs, spots, heads, head):
     outs, (buf, sems, out_sems) = refs[: len(spots)], refs[len(spots) :]
-    place = place_ref[0]
+    place, rows = place_ref[0], q_ref.shape[0]
     reads = []
     for n, r in enumerate(spots):
         column = pl.multiple_of(((place ^ r) * heads + head) * HEAD_DIM, HEAD_DIM)
@@ -298,7 +301,7 @@
             reads.append(
                 pltpu.make_async_copy(
                     source.at[:, pl.ds(column, HEAD_DIM)],
-                    buf.at[n, :, pl.ds(j * HEAD_DIM, HEAD_DIM)],
+                    buf.at[n, pl.ds(j * rows, rows), :],
                     sems.at[n, j],
                 )
             )
@@ -315,7 +318,7 @@
 
 def pack(place, arrays, spots, heads, head):
     rows = arrays[0].shape[0]
-    shape = (rows, 3 * HEAD_DIM)
+    shape = (3 * rows, HEAD_DIM)
     return pl.pallas_call(
         functools.partial(pack_kernel, spots=spots, heads=heads, head=head),
         in_specs=[pl.BlockSpec(memory_space=pltpu.SMEM)]
@@ -337,15 +340,15 @@
 
 def flash_kernel(place_ref, *refs, blocks):
     sources, outs = refs[:blocks], refs[blocks : 2 * blocks]
-    q_buf, k_buf, v_buf, vt_buf, o_buf, s_buf, m_buf, l_buf, acc_buf, sems = refs[2 * blocks :]
-    rows = sources[0].shape[0]
+    q_buf, k_buf, v_buf, vt_buf, o_buf, l_buf, acc_buf, m_buf, sems = refs[2 * blocks :]
+    rows = sources[0].shape[0] // 3
     place = place_ref[0]
     targets = (q_buf, k_buf, v_buf)
 
     def fetch(r, block, j):
         spot = pl.ds(pl.multiple_of(block * rows, rows), rows)
         return pltpu.make_async_copy(
-            sources[r].at[:, pl.ds(j * HEAD_DIM, HEAD_DIM)], targets[j].at[spot], sems.at[block, j]
+            sources[r].at[pl.ds(j * rows, rows), :], targets[j].at[spot], sems.at[block, j]
         )
 
     for r in range(blocks):
@@ -360,58 +363,93 @@
 
     scale = LOG2E / math.sqrt(HEAD_DIM)
 
-    half = rows // 2
-
-    def score_part(i, keys, first, masked):
-        queries = slice(i * rows + first, (i + 1) * rows)
-        scores = mxu(k_buf[keys, :], q_buf[queries, :], LAST)
-        shape = scores.shape
-        if masked:
-            scores = jnp.where(iota(shape, 1) >= iota(shape, 0), scores, floor_score)
-        s_buf[i % 2, keys, first:] = scores
-        m_buf[i % 2, :, first:] = jnp.maximum(
-            m_buf[i % 2, :, first:], jnp.max(scores.reshape(shape[0] // 8, 8, shape[1]), axis=0)
-        )
-
-    def weigh_part(i, keys, first, top):
-        weights = jnp.exp2(s_buf[i % 2, keys, first:] * scale - top[:, first:])
-        shape = weights.shape
-        l_buf[:, first:] += jnp.sum(weights.reshape(shape[0] // 8, 8, shape[1]), axis=0)
-        acc_buf[:, first:] += mxu(vt_buf[:, keys], weights.astype(BF16), PLAIN)
-
-    def spans(i, j):
-        if i != j:
-            return [(slice(j * rows, (j + 1) * rows), 0)]
-        return [
-            (slice(j * rows, j * rows + half), 0),
-            (slice(j * rows + half, (j + 1) * rows), half),
-        ]
-
-    def score(i, j):
-        for keys, first in spans(i, j):
-            score_part(i, keys, first, i == j)
-
-    def weigh(i, j, top):
-        for keys, first in spans(i, j):
-            weigh_part(i, keys, first, top)
-
-    m_buf[...] = jnp.full(m_buf.shape, floor_score, F32)
-    ready(0)
-    score(0, 0)
-    for i in range(blocks):
-        if i + 1 < blocks:
-            ready(i + 1)
-        top = jnp.max(m_buf[i % 2], axis=0, keepdims=True) * scale
-        m_buf[(i + 1) % 2] = jnp.full((8, rows), floor_score, F32)
-        acc_buf[...] = jnp.zeros(acc_buf.shape, F32)
-        l_buf[...] = jnp.zeros(l_buf.shape, F32)
-        for j in range(i + 2):
-            if j <= i:
-                weigh(i, j, top)
-            if i + 1 < blocks:
-                score(i + 1, j)
-        total = jnp.sum(l_buf[...], axis=0, keepdims=True)
-        o_buf[i * rows : (i + 1) * rows, :] = (acc_buf[...] / total).T.astype(BF16)
+    half, wide = rows // 2, 2 * rows
+    ones = jnp.ones((8, HEAD_DIM), BF16)
+
+    def squares(a):
+        return mxu(ones, a * a, LAST)[:1]
+
+    def lower(a):
+        return jnp.where(iota(a.shape, 1) >= iota(a.shape, 0), a, floor_score)
+
+    def jobs_of(i):
+        jobs = [(j * rows, rows, 0, False) for j in range(2 * i)]
+        for n in range(4):
+            jobs.append((2 * i * rows + n * half, half, n * half, True))
+        return jobs
+
+    def score(i, job):
+        start, count, first, masked = job
+        scores = mxu(k_buf[start : start + count, :], q_buf[i * wide + first : (i + 1) * wide, :], LAST)
+        if not masked:
+            return scores
+        head = lower(scores[:, :count])
+        return head if first + count == wide else jnp.concatenate([head, scores[:, count:]], axis=1)
+
+    key_square = jnp.zeros((1, rows), F32)
+    smallest = jnp.full((1, wide), -floor_score, F32)
+    for i in range(blocks // 2):
+        for block in (2 * i, 2 * i + 1):
+            ready(block)
+            key_square = jnp.maximum(key_square, squares(k_buf[block * rows : (block + 1) * rows, :]))
+        most = jnp.max(key_square, axis=1, keepdims=True)
+        shift = jnp.sqrt(squares(q_buf[i * wide : (i + 1) * wide, :]) * most) * scale
+        jobs = jobs_of(i)
+        following = score(i, jobs[0])
+        for n, (start, count, first, _) in enumerate(jobs):
+            scores = following
+            if n + 1 < len(jobs):
+                following = score(i, jobs[n + 1])
+            weights = jnp.exp2(scores * scale - shift[:, first:])
+            total = jnp.sum(weights.reshape(count // 8, 8, wide - first), axis=0)
+            update = mxu(vt_buf[:, start : start + count], weights.astype(BF16), PLAIN)
+            if n == 0:
+                acc_buf[i % 2] = update
+                l_buf[i % 2] = total
+            else:
+                acc_buf[i % 2, :, first:] += update
+                l_buf[i % 2, :, first:] += total
+        total = jnp.sum(l_buf[i % 2], axis=0, keepdims=True)
+        smallest = jnp.minimum(smallest, total)
+        o_buf[i * wide : (i + 1) * wide, :] = (acc_buf[i % 2] / total).T.astype(BF16)
+
+    @pl.when(jnp.min(smallest) < TOO_SMALL)
+    def _():
+        def one_query(i, carry):
+            q_rows = pl.ds(pl.multiple_of(i * rows, rows), rows)
+            m_buf[...] = jnp.full(m_buf.shape, floor_score, F32)
+            l_buf[0, :, :rows] = jnp.zeros((8, rows), F32)
+            acc_buf[0, :, :rows] = jnp.zeros((HEAD_DIM, rows), F32)
+
+            def visit(j, masked):
+                k_rows = pl.ds(pl.multiple_of(j * rows, rows), rows)
+                scores = mxu(k_buf[k_rows, :], q_buf[q_rows, :], LAST)
+                if masked:
+                    scores = lower(scores)
+                old = m_buf[:1, :]
+                newest = jnp.maximum(old, jnp.max(scores, axis=0, keepdims=True) * scale)
+                weights = jnp.exp2(scores * scale - newest)
+                factor = jnp.exp2(old - newest)
+                m_buf[:1, :] = newest
+                l_buf[0, :, :rows] = l_buf[0, :, :rows] * factor + jnp.sum(
+                    weights.reshape(rows // 8, 8, rows), axis=0
+                )
+                acc_buf[0, :, :rows] = acc_buf[0, :, :rows] * factor + mxu(
+                    vt_buf[:, k_rows], weights.astype(BF16), PLAIN
+                )
+
+            def plain(j, inner):
+                visit(j, False)
+                return inner
+
+            lax.fori_loop(0, i, plain, 0)
+            visit(i, True)
+            total = jnp.sum(l_buf[0, :, :rows], axis=0, keepdims=True)
+            o_buf[q_rows, :] = (acc_buf[0, :, :rows] / total).T.astype(BF16)
+            return carry
+
+        lax.fori_loop(0, blocks, one_query, 0)
+
     writes = []
     for r in range(blocks):
         spot = pl.ds(pl.multiple_of((place ^ r) * rows, rows), rows)
@@ -422,7 +460,7 @@
 
 
 def flash(place, sources):
-    blocks, rows = len(sources), sources[0].shape[0]
+    blocks, rows = len(sources), sources[0].shape[0] // 3
     total = blocks * rows
     pairs = total * (total + rows) // 2
     return pl.pallas_call(
@@ -437,10 +475,9 @@
             pltpu.VMEM((total, HEAD_DIM), BF16),
             pltpu.VMEM((HEAD_DIM, total), BF16),
             pltpu.VMEM((total, HEAD_DIM), BF16),
-            pltpu.VMEM((2, total, rows), F32),
-            pltpu.VMEM((2, 8, rows), F32),
+            pltpu.VMEM((2, 8, 2 * rows), F32),
+            pltpu.VMEM((2, HEAD_DIM, 2 * rows), F32),
             pltpu.VMEM((8, rows), F32),
-            pltpu.VMEM((HEAD_DIM, rows), F32),
             pltpu.SemaphoreType.DMA((blocks, 3)),
         ],
         compiler_params=WHOLE_VMEM,
@@ -533,15 +570,15 @@
             )
         got.append(mine)
     part, state = local_part(gate_inner, gate_outer, hyena_value, rate, local_residue, skip_gain)
-    near = [state] + [swap(state, r) for r in range(1, SPAN)]
-
+    spot = jnp.stack([place.astype(jnp.int32), jnp.int32(row_count)])
+    partner = swap(state, 1)
+    (pair,) = state_call(pair_kernel, spot, rate, (state, partner), (BF16,))
+    far = swap(pair, 2)
     for h in range(heads):
         results = flash(where, got[h])
         if h == heads - 2:
-            near = lax.optimization_barrier(tuple(near) + (results[0],))[:-1]
-            before, total = gather_states(
-                jnp.stack([place.astype(jnp.int32), jnp.int32(row_count)]), rate, near
-            )
+            far = after(far, results[0])
+            before, total = state_call(gather_kernel, spot, rate, (partner, pair, far), (F32, BF16))
             other = swap(total, SPAN)
         back = list(results)
         for r in SENDS:

time: 147 us -> 181 us (1.23)
  Pallas kernels: 61.7 us -> 112 us
  waiting for transfers between devices: 46.9 us -> 29.7 us
    pallas_call x2, Pallas kernels: 27.2 us -> 75.9 us  [flash(): pl.pallas_call(functools.partial(flash_kernel, blocks=blocks), in_specs=[...]
    ppermute x32 -> x31, waiting for transfers between devices: 43.2 us -> 26 us  [swap(): return lax.ppermute(a, 'ctx', [(i, i ^ r) for i in range(ctx_size)])]
    ppermute x32 -> x31, starting transfers between devices: 28.7 us -> 29.4 us  [swap(): return lax.ppermute(a, 'ctx', [(i, i ^ r) for i in range(ctx_size)])]
  transfers between devices with their start and end apart: 35 -> 34, of which waited for: 13 -> 10; matrix products, arithmetic and copies ran while one was open for 2% -> 1% of each run, Pallas kernels for 39% -> 59%
where the time goes in v3:
time: 181 us
  Pallas kernels  112 us (62%)
  starting transfers between devices  34.1 us (19%)
  waiting for transfers between devices  29.7 us (16%)
  local copies, waits for them, and re-layouts  3.02 us (2%)
    pallas_call x2, Pallas kernels, flash(): pl.pallas_call(functools.partial(flash_kernel, blocks=blocks), in_specs=[...  75.9 us
    ppermute x31, starting transfers between devices, swap(): return lax.ppermute(a, 'ctx', [(i, i ^ r) for i in range(ctx_size)])  29.4 us
    ppermute x31, waiting for transfers between devices, swap(): return lax.ppermute(a, 'ctx', [(i, i ^ r) for i in range(ctx_size)])  26 us
    pallas_call x1, Pallas kernels, local_part(): pl.pallas_call(local_kernel, grid=grid, in_specs=[wide, wide, wide, row,...  15.9 us
    pallas_call x3, Pallas kernels, pack(): pl.pallas_call(functools.partial(pack_kernel, spots=spots, heads=heads, h...  8.06 us
    pallas_call x1, Pallas kernels, remote_part(): pl.pallas_call(remote_kernel, grid=grid, in_specs=[pl.BlockSpec(memory_sp...  6.37 us
    ppermute x3, starting transfers between devices, gathered_modes(): lax.ppermute(modes, 'tp', [(i, (i + shift) % tp_size) for i in range(tp_s...  4.67 us
    ppermute x3, waiting for transfers between devices, gathered_modes(): lax.ppermute(modes, 'tp', [(i, (i + shift) % tp_size) for i in range(tp_s...  3.7 us
  transfers between devices with their start and end apart: 34, of which 10 were waited for; matrix products, arithmetic and copies ran while one was open for 1% of the time, Pallas kernels for 59%

profile of v3, /device:TPU:0, one launch (start us, length us, event | category | flops | bytes accessed | tf_op | source)
XLA Modules:
  0.0 180.8 jit_solution(8443770081885302063)
XLA Ops:
  0.6 2.1 %pack.3 = (bf16[1536,128]{1,0:T(8,128)(2,1)}, bf16[1536,128]{1,0:T(8,128)(2,1)}) custom-call(s32[1]{0:T(128)} %bitcast.place_ref, bf16[512,2048]{1,0:T(8,128)(2,1)} %q_ref.2, bf16[512,2048]{1,0:T(8,128)(2,1)} %k_ref.5, bf16[512,2048]{1,0:T(8,128)(2,1)} %v_ref.5), custom_call_target="tpu_custom_call" | custom-call | bytes 1572864 | tf_op jit(solution)/shard_map/pack/pallas_call | solution.py:322
  2.7 4.0 %collective-permute-start.10 = (bf16[1536,128]{1,0:T(8,128)(2,1)}, bf16[1536,128]{1,0:T(8,128)(2,1)S(1)}, u32[]{:S(2)}, u32[]{:S(2)}) collective-permute-start(bf16[1536,128]{1,0:T(8,128)(2,1)} %get-tuple-element.46), channel_id=1, source_target_pairs={{0,24},{4,28},{8,16},{12,20},{16,8},{20,12},{24,0},{28,4},{1,25},{... | collective-permute-start | bytes 1179656 | tf_op jit(solution)/shard_map/ppermute | solution.py:553
  6.7 2.7 %pack.4 = (bf16[1536,128]{1,0:T(8,128)(2,1)}, bf16[1536,128]{1,0:T(8,128)(2,1)}, bf16[1536,128]{1,0:T(8,128)(2,1)}, bf16[1536,128]{1,0:T(8,128)(2,1)}, bf16[1536...) custom-call(s32[1]{0:T(128)} %bitcast.place_ref, bf16[512,2048]{1,0:T(8,128)(2,1)} %q_ref.2, bf16[512,2048]{1,0:T(8,128)(2,1)} %k_ref.5, ...), custom_call_target="tpu_custom_call" | custom-call | bytes 4718592 | tf_op jit(solution)/shard_map/pack/pallas_call | solution.py:322
  9.5 3.7 %collective-permute-start.2 = (f32[128,32]{0,1:T(8,128)S(1)}, f32[128,32]{0,1:T(8,128)S(1)}, u32[]{:S(2)}, u32[]{:S(2)}) collective-permute-start(f32[128,32]{0,1:T(8,128)S(1)} %pad_maximum_fusion), channel_id=1, source_target_pairs={{0,3},{1,0},{2,1},{3,2},{4,7},{5,4},{6,5},{7,6},{8,11},{9,8},{10,9... | collective-permute-start | bytes 49160 | tf_op jit(solution)/shard_map/ppermute | solution.py:198
  13.2 1.0 collective-permute-start
  14.2 0.4 collective-permute-done.2
  14.9 2.9 %collective-permute-done.1 = f32[128,32]{0,1:T(8,128)S(1)} collective-permute-done((f32[128,32]{0,1:T(8,128)S(1)}, f32[128,32]{0,1:T(8,128)S(1)}, u32[]{:S(2)}, u32[]{:S(2)}) %collective-permute-start.1) | collective-permute-done | bytes 16416 | tf_op jit(solution)/shard_map/ppermute | solution.py:198
  17.8 0.5 collective-permute-start.6
  18.3 0.4 collective-permute-done
  19.1 0.7 reshape.19
  19.9 0.7 reshape.18
  20.6 15.9 %local_part.1 = (f32[512,2048]{1,0:T(8,128)}, bf16[16,16,128]{2,1,0:T(8,128)(2,1)}) custom-call(bf16[512,2048]{1,0:T(8,128)(2,1)} %gate_ref.1, bf16[512,2048]{1,0:T(8,128)(2,1)} %outer_ref.3, bf16[512,2048]{1,0:T(8,128)(2,1)} %value_ref.1, f32[16,1,128]{2,1,0:T(1,128)} %bitcast.8, f32[16,1,128]{2,1,0:T(1,128)} %bitcast.12, f32[16,1,128]{2,1,0:T(1,128)} %bitcast.14), custom_call_target="tpu_custom_call" | custom-call | flops 4294967296 | bytes 10485760 | tf_op jit(solution)/shard_map/local_part/pallas_call | solution.py:230
  36.5 0.6 pad_add_fusion.place_ref
  37.1 0.8 collective-permute-done.3.other_ref
  37.9 0.6 copy-done
  38.5 1.6 shard_map.113.pair_ref
  40.1 1.1 collective-permute-start.4
  41.2 3.3 %collective-permute-done.4.far_ref = bf16[16,16,128]{2,1,0:T(8,128)(2,1)S(1)} collective-permute-done((bf16[16,16,128]{2,1,0:T(8,128)(2,1)}, bf16[16,16,128]{2,1,0:T(8,128)(2,1)S(1)}, u32[]{:S(2)}, u32[]{:S(2)}) %collective-permute-start.4) | collective-permute-done | bytes 65568 | tf_op jit(solution)/shard_map/ppermute | solution.py:553
  44.6 1.3 collective-permute-start.9
  45.9 3.3 %pack.5 = (bf16[1536,128]{1,0:T(8,128)(2,1)}, bf16[1536,128]{1,0:T(8,128)(2,1)}, bf16[1536,128]{1,0:T(8,128)(2,1)}, bf16[1536,128]{1,0:T(8,128)(2,1)}, bf16[1536...) custom-call(s32[1]{0:T(128)} %bitcast.place_ref, ...), custom_call_target="tpu_custom_call" | custom-call | bytes 6291456 | tf_op jit(solution)/shard_map/pack/pallas_call | solution.py:322
  49.2 1.6 collective-permute-start.8
  50.8 1.0 collective-permute-start.13
  51.8 4.5 %collective-permute-done.7.refs_3_ = bf16[1536,128]{1,0:T(8,128)(2,1)} collective-permute-done((bf16[1536,128]{1,0:T(8,128)(2,1)}, bf16[1536,128]{1,0:T(8,128)(2,1)}, u32[]{:S(2)}, u32[]{:S(2)}) %collective-permute-start.7) | collective-permute-done | bytes 393248 | tf_op jit(solution)/shard_map/ppermute | solution.py:553
  56.3 1.0 collective-permute-start.15
  57.3 8.8 %collective-permute-done.8.refs_4_ = bf16[1536,128]{1,0:T(8,128)(2,1)S(1)} collective-permute-done((bf16[1536,128]{1,0:T(8,128)(2,1)}, bf16[1536,128]{1,0:T(8,128)(2,1)S(1)}, u32[]{:S(2)}, u32[]{:S(2)}) %collective-permute-start.8) | collective-permute-done | bytes 393248 | tf_op jit(solution)/shard_map/ppermute | solution.py:553
  66.1 0.7 copy-done.15
  66.8 0.8 collective-permute-start.17
  67.6 1.4 collective-permute-start.18
  69.0 38.1 %flash.2 = (bf16[512,128]{1,0:T(8,128)(2,1)}, bf16[512,128]{1,0:T(8,128)(2,1)}, bf16[512,128]{1,0:T(8,128)(2,1)}, bf16[512,128]{1,0:T(8,128)(2,1)}, bf16[512,128...) custom-call(s32[1]{0:T(128)} %bitcast.place_ref, ...), custom_call_target="tpu_custom_call" | custom-call | flops 9663676416 | bytes 4194304 | tf_op jit(solution)/shard_map/flash/pallas_call | solution.py:466
  107.1 1.6 shard_map.114
  108.8 1.0 collective-permute-start.20
  109.8 1.1 collective-permute-start.21
  111.2 1.5 collective-permute-start.23
  112.7 0.6 collective-permute-start.19
  113.2 37.9 %flash.3 = (bf16[512,128]{1,0:T(8,128)(2,1)}, bf16[512,128]{1,0:T(8,128)(2,1)}, bf16[512,128]{1,0:T(8,128)(2,1)}, bf16[512,128]{1,0:T(8,128)(2,1)}, bf16[512,128...) custom-call(s32[1]{0:T(128)} %bitcast.place_ref, ...), custom_call_target="tpu_custom_call" | custom-call | flops 9663676416 | bytes 4194304 | tf_op jit(solution)/shard_map/flash/pallas_call | solution.py:466
  151.1 1.6 collective-permute-start.24
  152.7 1.4 collective-permute-start.25
  154.1 1.5 collective-permute-start.26
  155.8 1.4 collective-permute-start.28
  157.1 5.3 %collective-permute-done.24.refs_5_ = bf16[512,128]{1,0:T(8,128)(2,1)S(1)} collective-permute-done((bf16[512,128]{1,0:T(8,128)(2,1)}, bf16[512,128]{1,0:T(8,128)(2,1)S(1)}, u32[]{:S(2)}, u32[]{:S(2)}) %collective-permute-start.24) | collective-permute-done | bytes 131104 | tf_op jit(solution)/shard_map/ppermute | solution.py:553
  162.4 1.5 collective-permute-start.29
  163.9 2.1 %collective-permute-start.30 = (bf16[512,128]{1,0:T(8,128)(2,1)}, bf16[512,128]{1,0:T(8,128)(2,1)}, u32[]{:S(2)}, u32[]{:S(2)}) collective-permute-start(bf16[512,128]{1,0:T(8,128)(2,1)} %get-tuple-element.84), channel_id=1, source_target_pairs={{0,16},{4,20},{8,24},{12,28},{16,0},{20,4},{24,8},{28,12},{1,17},{... | collective-permute-start | bytes 393224 | tf_op jit(solution)/shard_map/ppermute | solution.py:553
  166.0 1.6 collective-permute-start.32
  167.6 0.8 collective-permute-start.33
  168.5 6.4 %remote_part.1 = bf16[512,2048]{1,0:T(8,128)(2,1)} custom-call(s32[1]{0:T(128)} %bitcast.place_ref, f32[512,2048]{1,0:T(8,128)} %get-tuple-element.50.part_ref, bf16[512,2048]{1,0:T(8,128)(2,1)} %outer_ref.3, f32[16,1,128]{2,1,0:T(1,128)} %bitcast.11, f32[16,1,128]{2,1,0:T(1,128)} %bitcast.13, f32[16,16,128]{2,1,0:T(8,128)} %get-tuple-element.71.before_ref, ...), custom_call_target="tpu_custom_call" | custom-call | flops 805306368 | bytes 8388608 | tf_op jit(solution)/shard_map/remote_part/pallas_call | solution.py:253
  174.9 1.4 collective-permute-done.30.refs_12_
  176.3 1.8 collective-permute-done.31.refs_13_
  178.1 2.6 %join.1 = bf16[512,2048]{1,0:T(8,128)(2,1)} custom-call(s32[1]{0:T(128)} %bitcast.place_ref, bf16[512,128]{1,0:T(8,128)(2,1)} %get-tuple-element.58.refs_0_, bf16[512,128]{1,0:T(8,128)(2,1)} %copy-done.1, bf16[512,128]{1,0:T(8,128)(2,1)} %copy-done.2, bf16[512,128]{1,0:T(8,128)(2,1)} %copy-done.3, bf16[512,128]{1,0:T(8,128)(2,1)} %copy-done.4, ...), custom_call_target="tpu_custom_call" | custom-call | bytes 4194304 | tf_op jit(solution)/shard_map/join/pallas_call | solution.py:514
  (73 shorter events, 1.4 us)
Async XLA Ops:
  2.7 6.8 %copy-start.10 = (f32[128,16]{0,1:T(8,128)S(1)}, f32[128,16]{0,1:T(8,128)}, u32[]{:S(2)}) copy-start(f32[128,16]{0,1:T(8,128)} %param.14) | copy-start | bytes 24580
  2.7 6.8 %copy-start.11 = (f32[128,16]{0,1:T(8,128)S(1)}, f32[128,16]{0,1:T(8,128)}, u32[]{:S(2)}) copy-start(f32[128,16]{0,1:T(8,128)} %param.13) | copy-start | bytes 24580
  2.7 11.5 %copy-start.16 = (s32[128]{0:T(128)S(1)}, s32[128]{0:T(128)}, u32[]{:S(2)}) copy-start(s32[128]{0:T(128)} %param.16) | copy-start | bytes 1540
  2.7 46.5 %collective-permute-start.10 = (bf16[1536,128]{1,0:T(8,128)(2,1)}, bf16[1536,128]{1,0:T(8,128)(2,1)S(1)}, u32[]{:S(2)}, u32[]{:S(2)}) collective-permute-start(bf16[1536,128]{1,0:T(8,128)(2,1)} %get-tuple-element.46), channel_id=1, source_target_pairs={{0,24},{4,28},{8,16},{12,20},{16,8},{20,12},{24,0},{28,4},{1,25},{... | collective-permute-start | bytes 1179656 | tf_op jit(solution)/shard_map/ppermute | solution.py:553
  9.5 5.1 %collective-permute-start.2 = (f32[128,32]{0,1:T(8,128)S(1)}, f32[128,32]{0,1:T(8,128)S(1)}, u32[]{:S(2)}, u32[]{:S(2)}) collective-permute-start(f32[128,32]{0,1:T(8,128)S(1)} %pad_maximum_fusion), channel_id=1, source_target_pairs={{0,3},{1,0},{2,1},{3,2},{4,7},{5,4},{6,5},{7,6},{8,11},{9,8},{10,9... | collective-permute-start | bytes 49160 | tf_op jit(solution)/shard_map/ppermute | solution.py:198
  13.2 4.6 %collective-permute-start.1 = (f32[128,32]{0,1:T(8,128)S(1)}, f32[128,32]{0,1:T(8,128)S(1)}, u32[]{:S(2)}, u32[]{:S(2)}) collective-permute-start(f32[128,32]{0,1:T(8,128)S(1)} %pad_maximum_fusion), channel_id=1, source_target_pairs={{0,2},{1,3},{2,0},{3,1},{4,6},{5,7},{6,4},{7,5},{8,10},{9,11},{10,... | collective-permute-start | bytes 49160 | tf_op jit(solution)/shard_map/ppermute | solution.py:198
  13.2 5.5 %collective-permute-start = (f32[128,32]{0,1:T(8,128)S(1)}, f32[128,32]{0,1:T(8,128)S(1)}, u32[]{:S(2)}, u32[]{:S(2)}) collective-permute-start(f32[128,32]{0,1:T(8,128)S(1)} %pad_maximum_fusion), channel_id=1, source_target_pairs={{0,1},{1,2},{2,3},{3,0},{4,5},{5,6},{6,7},{7,4},{8,9},{9,10},{10,1... | collective-permute-start | bytes 49160 | tf_op jit(solution)/shard_map/ppermute | solution.py:198
  14.2 30.4 %collective-permute-start.11 = (bf16[1536,128]{1,0:T(8,128)(2,1)}, bf16[1536,128]{1,0:T(8,128)(2,1)S(1)}, u32[]{:S(2)}, u32[]{:S(2)}) collective-permute-start(bf16[1536,128]{1,0:T(8,128)(2,1)} %get-tuple-element.57), channel_id=1, source_target_pairs={{0,28},{4,24},{8,20},{12,16},{16,12},{20,8},{24,4},{28,0},{1,29},{... | collective-permute-start | bytes 1179656 | tf_op jit(solution)/shard_map/ppermute | solution.py:553
  14.6 36.2 %collective-permute-start.5 = (bf16[1536,128]{1,0:T(8,128)(2,1)}, bf16[1536,128]{1,0:T(8,128)(2,1)}, u32[]{:S(2)}, u32[]{:S(2)}) collective-permute-start(bf16[1536,128]{1,0:T(8,128)(2,1)} %get-tuple-element.53), channel_id=1, source_target_pairs={{0,4},{4,0},{8,12},{12,8},{16,20},{20,16},{24,28},{28,24},{1,5},{5... | collective-permute-start | bytes 1179656 | tf_op jit(solution)/shard_map/ppermute | solution.py:553
  17.8 33.0 %collective-permute-start.6 = (bf16[1536,128]{1,0:T(8,128)(2,1)}, bf16[1536,128]{1,0:T(8,128)(2,1)}, u32[]{:S(2)}, u32[]{:S(2)}) collective-permute-start(bf16[1536,128]{1,0:T(8,128)(2,1)} %get-tuple-element.54), channel_id=1, source_target_pairs={{0,8},{4,12},{8,0},{12,4},{16,24},{20,28},{24,16},{28,20},{1,9},{5... | collective-permute-start | bytes 1179656 | tf_op jit(solution)/shard_map/ppermute | solution.py:553
  36.4 1.5 collective-permute-start.3
  40.1 4.5 %collective-permute-start.4 = (bf16[16,16,128]{2,1,0:T(8,128)(2,1)}, bf16[16,16,128]{2,1,0:T(8,128)(2,1)S(1)}, u32[]{:S(2)}, u32[]{:S(2)}) collective-permute-start(bf16[16,16,128]{2,1,0:T(8,128)(2,1)} %shard_map.113.pair_ref), channel_id=1, source_target_pairs={{0,8},{4,12},{8,0},{12,4},{16,24},{20,28},{24,16},{28,20},{1,9},{5... | collective-permute-start | bytes 196616 | tf_op jit(solution)/shard_map/ppermute | solution.py:553
  44.6 4.6 %copy-start.9 = (bf16[16,16,128]{2,1,0:T(8,128)(2,1)}, bf16[16,16,128]{2,1,0:T(8,128)(2,1)S(1)}, u32[]{:S(2)}) copy-start(bf16[16,16,128]{2,1,0:T(8,128)(2,1)S(1)} %collective-permute-done.4.far_ref) | copy-start | bytes 196612
  44.6 11.7 %collective-permute-start.7 = (bf16[1536,128]{1,0:T(8,128)(2,1)}, bf16[1536,128]{1,0:T(8,128)(2,1)}, u32[]{:S(2)}, u32[]{:S(2)}) collective-permute-start(bf16[1536,128]{1,0:T(8,128)(2,1)} %get-tuple-element.55), channel_id=1, source_target_pairs={{0,12},{4,8},{8,4},{12,0},{16,28},{20,24},{24,20},{28,16},{1,13},{... | collective-permute-start | bytes 1179656 | tf_op jit(solution)/shard_map/ppermute | solution.py:553
  44.6 11.7 %collective-permute-start.9 = (bf16[1536,128]{1,0:T(8,128)(2,1)}, bf16[1536,128]{1,0:T(8,128)(2,1)}, u32[]{:S(2)}, u32[]{:S(2)}) collective-permute-start(bf16[1536,128]{1,0:T(8,128)(2,1)} %get-tuple-element.56), channel_id=1, source_target_pairs={{0,20},{4,16},{8,28},{12,24},{16,4},{20,0},{24,12},{28,8},{1,21},{... | collective-permute-start | bytes 1179656 | tf_op jit(solution)/shard_map/ppermute | solution.py:553
  49.2 19.8 %copy-start.12 = (bf16[1536,128]{1,0:T(8,128)(2,1)}, bf16[1536,128]{1,0:T(8,128)(2,1)S(1)}, u32[]{:S(2)}) copy-start(bf16[1536,128]{1,0:T(8,128)(2,1)S(1)} %collective-permute-done.10.refs_6_) | copy-start | bytes 1179652
  49.2 16.8 %collective-permute-start.8 = (bf16[1536,128]{1,0:T(8,128)(2,1)}, bf16[1536,128]{1,0:T(8,128)(2,1)S(1)}, u32[]{:S(2)}, u32[]{:S(2)}) collective-permute-start(bf16[1536,128]{1,0:T(8,128)(2,1)} %get-tuple-element.48), channel_id=1, source_target_pairs={{0,16},{4,20},{8,24},{12,28},{16,0},{20,4},{24,8},{28,12},{1,17},{... | collective-permute-start | bytes 1179656 | tf_op jit(solution)/shard_map/ppermute | solution.py:553
  50.8 15.2 %collective-permute-start.12 = (bf16[1536,128]{1,0:T(8,128)(2,1)}, bf16[1536,128]{1,0:T(8,128)(2,1)S(1)}, u32[]{:S(2)}, u32[]{:S(2)}) collective-permute-start(bf16[1536,128]{1,0:T(8,128)(2,1)} %get-tuple-element.63), channel_id=1, source_target_pairs={{0,4},{4,0},{8,12},{12,8},{16,20},{20,16},{24,28},{28,24},{1,5},{5... | collective-permute-start | bytes 1179656 | tf_op jit(solution)/shard_map/ppermute | solution.py:553
  50.8 16.8 %collective-permute-start.13 = (bf16[1536,128]{1,0:T(8,128)(2,1)}, bf16[1536,128]{1,0:T(8,128)(2,1)}, u32[]{:S(2)}, u32[]{:S(2)}) collective-permute-start(bf16[1536,128]{1,0:T(8,128)(2,1)} %get-tuple-element.64), channel_id=1, source_target_pairs={{0,8},{4,12},{8,0},{12,4},{16,24},{20,28},{24,16},{28,20},{1,9},{5... | collective-permute-start | bytes 1179656 | tf_op jit(solution)/shard_map/ppermute | solution.py:553
  56.3 52.5 %collective-permute-start.14 = (bf16[1536,128]{1,0:T(8,128)(2,1)}, bf16[1536,128]{1,0:T(8,128)(2,1)}, u32[]{:S(2)}, u32[]{:S(2)}) collective-permute-start(bf16[1536,128]{1,0:T(8,128)(2,1)} %get-tuple-element.65), channel_id=1, source_target_pairs={{0,12},{4,8},{8,4},{12,0},{16,28},{20,24},{24,20},{28,16},{1,13},{... | collective-permute-start | bytes 1179656 | tf_op jit(solution)/shard_map/ppermute | solution.py:553
  56.3 53.5 %collective-permute-start.15 = (bf16[1536,128]{1,0:T(8,128)(2,1)}, bf16[1536,128]{1,0:T(8,128)(2,1)}, u32[]{:S(2)}, u32[]{:S(2)}) collective-permute-start(bf16[1536,128]{1,0:T(8,128)(2,1)} %get-tuple-element.66), channel_id=1, source_target_pairs={{0,16},{4,20},{8,24},{12,28},{16,0},{20,4},{24,8},{28,12},{1,17},{... | collective-permute-start | bytes 1179656 | tf_op jit(solution)/shard_map/ppermute | solution.py:553
  66.1 44.9 %collective-permute-start.16 = (bf16[1536,128]{1,0:T(8,128)(2,1)}, bf16[1536,128]{1,0:T(8,128)(2,1)}, u32[]{:S(2)}, u32[]{:S(2)}) collective-permute-start(bf16[1536,128]{1,0:T(8,128)(2,1)} %get-tuple-element.67), channel_id=1, source_target_pairs={{0,20},{4,16},{8,28},{12,24},{16,4},{20,0},{24,12},{28,8},{1,21},{... | collective-permute-start | bytes 1179656 | tf_op jit(solution)/shard_map/ppermute | solution.py:553
  66.8 40.3 %copy-start.14 = (bf16[1536,128]{1,0:T(8,128)(2,1)}, bf16[1536,128]{1,0:T(8,128)(2,1)S(1)}, u32[]{:S(2)}) copy-start(bf16[1536,128]{1,0:T(8,128)(2,1)S(1)} %collective-permute-done.12.refs_1_) | copy-start | bytes 1179652
  66.8 44.4 %collective-permute-start.17 = (bf16[1536,128]{1,0:T(8,128)(2,1)}, bf16[1536,128]{1,0:T(8,128)(2,1)}, u32[]{:S(2)}, u32[]{:S(2)}) collective-permute-start(bf16[1536,128]{1,0:T(8,128)(2,1)} %get-tuple-element.68), channel_id=1, source_target_pairs={{0,24},{4,28},{8,16},{12,20},{16,8},{20,12},{24,0},{28,4},{1,25},{... | collective-permute-start | bytes 1179656 | tf_op jit(solution)/shard_map/ppermute | solution.py:553
  67.6 45.0 %collective-permute-start.18 = (bf16[1536,128]{1,0:T(8,128)(2,1)}, bf16[1536,128]{1,0:T(8,128)(2,1)}, u32[]{:S(2)}, u32[]{:S(2)}) collective-permute-start(bf16[1536,128]{1,0:T(8,128)(2,1)} %get-tuple-element.69), channel_id=1, source_target_pairs={{0,28},{4,24},{8,20},{12,16},{16,12},{20,8},{24,4},{28,0},{1,29},{... | collective-permute-start | bytes 1179656 | tf_op jit(solution)/shard_map/ppermute | solution.py:553
  108.8 43.9 %collective-permute-start.20 = (bf16[512,128]{1,0:T(8,128)(2,1)}, bf16[512,128]{1,0:T(8,128)(2,1)S(1)}, u32[]{:S(2)}, u32[]{:S(2)}) collective-permute-start(bf16[512,128]{1,0:T(8,128)(2,1)} %get-tuple-element.73), channel_id=1, source_target_pairs={{0,4},{4,0},{8,12},{12,8},{16,20},{20,16},{24,28},{28,24},{1,5},{5... | collective-permute-start | bytes 393224 | tf_op jit(solution)/shard_map/ppermute | solution.py:553
  109.8 44.3 %collective-permute-start.21 = (bf16[512,128]{1,0:T(8,128)(2,1)}, bf16[512,128]{1,0:T(8,128)(2,1)S(1)}, u32[]{:S(2)}, u32[]{:S(2)}) collective-permute-start(bf16[512,128]{1,0:T(8,128)(2,1)} %get-tuple-element.74), channel_id=1, source_target_pairs={{0,8},{4,12},{8,0},{12,4},{16,24},{20,28},{24,16},{28,20},{1,9},{5... | collective-permute-start | bytes 393224 | tf_op jit(solution)/shard_map/ppermute | solution.py:553
  110.9 44.6 %collective-permute-start.22 = (bf16[512,128]{1,0:T(8,128)(2,1)}, bf16[512,128]{1,0:T(8,128)(2,1)S(1)}, u32[]{:S(2)}, u32[]{:S(2)}) collective-permute-start(bf16[512,128]{1,0:T(8,128)(2,1)} %get-tuple-element.75), channel_id=1, source_target_pairs={{0,12},{4,8},{8,4},{12,0},{16,28},{20,24},{24,20},{28,16},{1,13},{... | collective-permute-start | bytes 393224 | tf_op jit(solution)/shard_map/ppermute | solution.py:553
  111.2 44.5 %collective-permute-start.23 = (bf16[512,128]{1,0:T(8,128)(2,1)}, bf16[512,128]{1,0:T(8,128)(2,1)S(1)}, u32[]{:S(2)}, u32[]{:S(2)}) collective-permute-start(bf16[512,128]{1,0:T(8,128)(2,1)} %get-tuple-element.76), channel_id=1, source_target_pairs={{0,16},{4,20},{8,24},{12,28},{16,0},{20,4},{24,8},{28,12},{1,17},{... | collective-permute-start | bytes 393224 | tf_op jit(solution)/shard_map/ppermute | solution.py:553
  112.7 38.4 %collective-permute-start.19 = (bf16[16,16,128]{2,1,0:T(8,128)(2,1)}, bf16[16,16,128]{2,1,0:T(8,128)(2,1)S(1)}, u32[]{:S(2)}, u32[]{:S(2)}) collective-permute-start(bf16[16,16,128]{2,1,0:T(8,128)(2,1)} %get-tuple-element.72), channel_id=1, source_target_pairs={{0,16},{4,20},{8,24},{12,28},{16,0},{20,4},{24,8},{28,12},{1,17},{... | collective-permute-start | bytes 196616 | tf_op jit(solution)/shard_map/ppermute | solution.py:553
  151.1 17.3 %copy-start.8 = (bf16[16,16,128]{2,1,0:T(8,128)(2,1)}, bf16[16,16,128]{2,1,0:T(8,128)(2,1)S(1)}, u32[]{:S(2)}) copy-start(bf16[16,16,128]{2,1,0:T(8,128)(2,1)S(1)} %collective-permute-done.19.other_ref) | copy-start | bytes 196612
  151.1 11.3 %collective-permute-start.24 = (bf16[512,128]{1,0:T(8,128)(2,1)}, bf16[512,128]{1,0:T(8,128)(2,1)S(1)}, u32[]{:S(2)}, u32[]{:S(2)}) collective-permute-start(bf16[512,128]{1,0:T(8,128)(2,1)} %get-tuple-element.77), channel_id=1, source_target_pairs={{0,20},{4,16},{8,28},{12,24},{16,4},{20,0},{24,12},{28,8},{1,21},{... | collective-permute-start | bytes 393224 | tf_op jit(solution)/shard_map/ppermute | solution.py:553
  152.7 22.1 %copy-start.1 = (bf16[512,128]{1,0:T(8,128)(2,1)}, bf16[512,128]{1,0:T(8,128)(2,1)S(1)}, u32[]{:S(2)}) copy-start(bf16[512,128]{1,0:T(8,128)(2,1)S(1)} %collective-permute-done.20.refs_1_) | copy-start | bytes 393220
  152.7 11.2 %collective-permute-start.25 = (bf16[512,128]{1,0:T(8,128)(2,1)}, bf16[512,128]{1,0:T(8,128)(2,1)S(1)}, u32[]{:S(2)}, u32[]{:S(2)}) collective-permute-start(bf16[512,128]{1,0:T(8,128)(2,1)} %get-tuple-element.78), channel_id=1, source_target_pairs={{0,24},{4,28},{8,16},{12,20},{16,8},{20,12},{24,0},{28,4},{1,25},{... | collective-permute-start | bytes 393224 | tf_op jit(solution)/shard_map/ppermute | solution.py:553
  154.1 20.8 %copy-start.2 = (bf16[512,128]{1,0:T(8,128)(2,1)}, bf16[512,128]{1,0:T(8,128)(2,1)S(1)}, u32[]{:S(2)}) copy-start(bf16[512,128]{1,0:T(8,128)(2,1)S(1)} %collective-permute-done.21.refs_2_) | copy-start | bytes 393220
  154.1 11.9 %collective-permute-start.26 = (bf16[512,128]{1,0:T(8,128)(2,1)}, bf16[512,128]{1,0:T(8,128)(2,1)S(1)}, u32[]{:S(2)}, u32[]{:S(2)}) collective-permute-start(bf16[512,128]{1,0:T(8,128)(2,1)} %get-tuple-element.79), channel_id=1, source_target_pairs={{0,28},{4,24},{8,20},{12,16},{16,12},{20,8},{24,4},{28,0},{1,29},{... | collective-permute-start | bytes 393224 | tf_op jit(solution)/shard_map/ppermute | solution.py:553
  155.5 19.3 %copy-start.3 = (bf16[512,128]{1,0:T(8,128)(2,1)}, bf16[512,128]{1,0:T(8,128)(2,1)S(1)}, u32[]{:S(2)}) copy-start(bf16[512,128]{1,0:T(8,128)(2,1)S(1)} %collective-permute-done.22.refs_3_) | copy-start | bytes 393220
  155.5 10.5 %collective-permute-start.27 = (bf16[512,128]{1,0:T(8,128)(2,1)}, bf16[512,128]{1,0:T(8,128)(2,1)}, u32[]{:S(2)}, u32[]{:S(2)}) collective-permute-start(bf16[512,128]{1,0:T(8,128)(2,1)} %get-tuple-element.81), channel_id=1, source_target_pairs={{0,4},{4,0},{8,12},{12,8},{16,20},{20,16},{24,28},{28,24},{1,5},{5... | collective-permute-start | bytes 393224 | tf_op jit(solution)/shard_map/ppermute | solution.py:553
  155.8 19.1 %copy-start.4 = (bf16[512,128]{1,0:T(8,128)(2,1)}, bf16[512,128]{1,0:T(8,128)(2,1)S(1)}, u32[]{:S(2)}) copy-start(bf16[512,128]{1,0:T(8,128)(2,1)S(1)} %collective-permute-done.23.refs_4_) | copy-start | bytes 393220
  155.8 11.9 %collective-permute-start.28 = (bf16[512,128]{1,0:T(8,128)(2,1)}, bf16[512,128]{1,0:T(8,128)(2,1)}, u32[]{:S(2)}, u32[]{:S(2)}) collective-permute-start(bf16[512,128]{1,0:T(8,128)(2,1)} %get-tuple-element.82), channel_id=1, source_target_pairs={{0,8},{4,12},{8,0},{12,4},{16,24},{20,28},{24,16},{28,20},{1,9},{5... | collective-permute-start | bytes 393224 | tf_op jit(solution)/shard_map/ppermute | solution.py:553
  162.4 12.5 %copy-start.5 = (bf16[512,128]{1,0:T(8,128)(2,1)}, bf16[512,128]{1,0:T(8,128)(2,1)S(1)}, u32[]{:S(2)}) copy-start(bf16[512,128]{1,0:T(8,128)(2,1)S(1)} %collective-permute-done.24.refs_5_) | copy-start | bytes 393220
  162.4 12.5 %collective-permute-start.29 = (bf16[512,128]{1,0:T(8,128)(2,1)}, bf16[512,128]{1,0:T(8,128)(2,1)}, u32[]{:S(2)}, u32[]{:S(2)}) collective-permute-start(bf16[512,128]{1,0:T(8,128)(2,1)} %get-tuple-element.83), channel_id=1, source_target_pairs={{0,12},{4,8},{8,4},{12,0},{16,28},{20,24},{24,20},{28,16},{1,13},{... | collective-permute-start | bytes 393224 | tf_op jit(solution)/shard_map/ppermute | solution.py:553
  163.9 11.0 %copy-start.6 = (bf16[512,128]{1,0:T(8,128)(2,1)}, bf16[512,128]{1,0:T(8,128)(2,1)S(1)}, u32[]{:S(2)}) copy-start(bf16[512,128]{1,0:T(8,128)(2,1)S(1)} %collective-permute-done.25.refs_6_) | copy-start | bytes 393220
  163.9 12.4 %collective-permute-start.30 = (bf16[512,128]{1,0:T(8,128)(2,1)}, bf16[512,128]{1,0:T(8,128)(2,1)}, u32[]{:S(2)}, u32[]{:S(2)}) collective-permute-start(bf16[512,128]{1,0:T(8,128)(2,1)} %get-tuple-element.84), channel_id=1, source_target_pairs={{0,16},{4,20},{8,24},{12,28},{16,0},{20,4},{24,8},{28,12},{1,17},{... | collective-permute-start | bytes 393224 | tf_op jit(solution)/shard_map/ppermute | solution.py:553
  166.0 8.9 %copy-start.7 = (bf16[512,128]{1,0:T(8,128)(2,1)}, bf16[512,128]{1,0:T(8,128)(2,1)S(1)}, u32[]{:S(2)}) copy-start(bf16[512,128]{1,0:T(8,128)(2,1)S(1)} %collective-permute-done.26.refs_7_) | copy-start | bytes 393220
  166.0 12.1 %collective-permute-start.31 = (bf16[512,128]{1,0:T(8,128)(2,1)}, bf16[512,128]{1,0:T(8,128)(2,1)}, u32[]{:S(2)}, u32[]{:S(2)}) collective-permute-start(bf16[512,128]{1,0:T(8,128)(2,1)} %get-tuple-element.85), channel_id=1, source_target_pairs={{0,20},{4,16},{8,28},{12,24},{16,4},{20,0},{24,12},{28,8},{1,21},{... | collective-permute-start | bytes 393224 | tf_op jit(solution)/shard_map/ppermute | solution.py:553
  166.0 12.1 %collective-permute-start.32 = (bf16[512,128]{1,0:T(8,128)(2,1)}, bf16[512,128]{1,0:T(8,128)(2,1)}, u32[]{:S(2)}, u32[]{:S(2)}) collective-permute-start(bf16[512,128]{1,0:T(8,128)(2,1)} %get-tuple-element.86), channel_id=1, source_target_pairs={{0,24},{4,28},{8,16},{12,20},{16,8},{20,12},{24,0},{28,4},{1,25},{... | collective-permute-start | bytes 393224 | tf_op jit(solution)/shard_map/ppermute | solution.py:553
  167.6 10.4 %collective-permute-start.33 = (bf16[512,128]{1,0:T(8,128)(2,1)}, bf16[512,128]{1,0:T(8,128)(2,1)}, u32[]{:S(2)}, u32[]{:S(2)}) collective-permute-start(bf16[512,128]{1,0:T(8,128)(2,1)} %get-tuple-element.87), channel_id=1, source_target_pairs={{0,28},{4,24},{8,20},{12,16},{16,12},{20,8},{24,4},{28,0},{1,29},{... | collective-permute-start | bytes 393224 | tf_op jit(solution)/shard_map/ppermute | solution.py:553
  (3 other events, 6.0 us)

commit v4 on v3

--- a/solution.py
+++ b/solution.py
@@ -16,6 +16,7 @@
 STEP_TILES = 4
 SPAN = 4
 SENDS = (6, 7, 4, 2, 5, 3, 1)
+BACKS = (2, 4, 6, 7, 3, 5, 1)
 WHOLE_VMEM = pltpu.CompilerParams(vmem_limit_bytes=63 << 20)
 
 floor_score = -1e30
@@ -555,7 +556,7 @@
     order = list(SENDS) + [0]
     got, backs = [], []
     sent = query_rows
-    lead = 2
+    lead = 1
     for h in range(heads):
         mine = [None] * ctx_size
         pieces = [order[:lead], order[lead:]] if h == 0 else [order]
@@ -581,7 +582,7 @@
             before, total = state_call(gather_kernel, spot, rate, (partner, pair, far), (F32, BF16))
             other = swap(total, SPAN)
         back = list(results)
-        for r in SENDS:
+        for r in BACKS:
             back[r] = swap(results[r], r)
         backs.append(back)
     before = after(before, backs[-1][0])

time: 181 us -> 188 us (1.039)
  waiting for transfers between devices: 29.7 us -> 34.4 us
  starting transfers between devices: 34.1 us -> 36.4 us
    ppermute x31, waiting for transfers between devices: 26 us -> 30.5 us  [swap(): return lax.ppermute(a, 'ctx', [(i, i ^ r) for i in range(ctx_size)])]
    ppermute x31, starting transfers between devices: 29.4 us -> 31.7 us  [swap(): return lax.ppermute(a, 'ctx', [(i, i ^ r) for i in range(ctx_size)])]
  transfers between devices with their start and end apart: 34 -> 34, of which waited for: 10 -> 10; matrix products, arithmetic and copies ran while one was open for 1% -> 1% of each run, Pallas kernels for 59% -> 58%
where the time goes in v4:
time: 188 us; the launch traced here: 187 us
  Pallas kernels  112 us (60%)
  starting transfers between devices  36.4 us (19%)
  waiting for transfers between devices  34.4 us (18%)
  local copies, waits for them, and re-layouts  2.28 us (1%)
    pallas_call x2, Pallas kernels, flash(): pl.pallas_call(functools.partial(flash_kernel, blocks=blocks), in_specs=[...  75.9 us
    ppermute x31, starting transfers between devices, swap(): return lax.ppermute(a, 'ctx', [(i, i ^ r) for i in range(ctx_size)])  31.7 us
    ppermute x31, waiting for transfers between devices, swap(): return lax.ppermute(a, 'ctx', [(i, i ^ r) for i in range(ctx_size)])  30.5 us
    pallas_call x1, Pallas kernels, local_part(): pl.pallas_call(local_kernel, grid=grid, in_specs=[wide, wide, wide, row,...  15.9 us
    pallas_call x3, Pallas kernels, pack(): pl.pallas_call(functools.partial(pack_kernel, spots=spots, heads=heads, h...  8.11 us
    pallas_call x1, Pallas kernels, remote_part(): pl.pallas_call(remote_kernel, grid=grid, in_specs=[pl.BlockSpec(memory_sp...  6.37 us
    ppermute x3, starting transfers between devices, gathered_modes(): lax.ppermute(modes, 'tp', [(i, (i + shift) % tp_size) for i in range(tp_s...  4.67 us
    ppermute x3, waiting for transfers between devices, gathered_modes(): lax.ppermute(modes, 'tp', [(i, (i + shift) % tp_size) for i in range(tp_s...  3.96 us
  transfers between devices with their start and end apart: 34, of which 10 were waited for; matrix products, arithmetic and copies ran while one was open for 1% of the time, Pallas kernels for 58%

profile of v4, /device:TPU:0, one launch (start us, length us, event | category | flops | bytes accessed | tf_op | source)
XLA Modules:
  0.0 187.1 jit_solution(4626811633120715149)
XLA Ops:
  0.6 1.8 pack.3
  2.5 4.0 %collective-permute-start.10 = (bf16[1536,128]{1,0:T(8,128)(2,1)}, bf16[1536,128]{1,0:T(8,128)(2,1)S(1)}, u32[]{:S(2)}, u32[]{:S(2)}) collective-permute-start(bf16[1536,128]{1,0:T(8,128)(2,1)} %pack.3), channel_id=1, source_target_pairs={{0,24},{4,28},{8,16},{12,20},{16,8},{20,12},{24,0},{28,4},{1,25},{... | collective-permute-start | bytes 1179656 | tf_op jit(solution)/shard_map/ppermute | solution.py:554
  6.5 2.9 %pack.4 = (bf16[1536,128]{1,0:T(8,128)(2,1)}, bf16[1536,128]{1,0:T(8,128)(2,1)}, bf16[1536,128]{1,0:T(8,128)(2,1)}, bf16[1536,128]{1,0:T(8,128)(2,1)}, bf16[1536...) custom-call(s32[1]{0:T(128)} %bitcast.place_ref, bf16[512,2048]{1,0:T(8,128)(2,1)} %q_ref.2, ...), custom_call_target="tpu_custom_call" | custom-call | bytes 5505024 | tf_op jit(solution)/shard_map/pack/pallas_call | solution.py:323
  9.4 3.7 %collective-permute-start.2 = (f32[128,32]{0,1:T(8,128)S(1)}, f32[128,32]{0,1:T(8,128)S(1)}, u32[]{:S(2)}, u32[]{:S(2)}) collective-permute-start(f32[128,32]{0,1:T(8,128)S(1)} %pad_maximum_fusion), channel_id=1, source_target_pairs={{0,3},{1,0},{2,1},{3,2},{4,7},{5,4},{6,5},{7,6},{8,11},{9,8},{10,9... | collective-permute-start | bytes 49160 | tf_op jit(solution)/shard_map/ppermute | solution.py:199
  13.1 1.0 collective-permute-start
  14.1 0.4 collective-permute-done.2
  14.5 0.5 collective-permute-start.6
  15.1 2.7 %collective-permute-done.1 = f32[128,32]{0,1:T(8,128)S(1)} collective-permute-done((f32[128,32]{0,1:T(8,128)S(1)}, f32[128,32]{0,1:T(8,128)S(1)}, u32[]{:S(2)}, u32[]{:S(2)}) %collective-permute-start.1) | collective-permute-done | bytes 16416 | tf_op jit(solution)/shard_map/ppermute | solution.py:199
  17.7 0.9 collective-permute-done
  19.1 0.7 reshape.19
  19.8 0.7 reshape.18
  20.5 15.9 %local_part.1 = (f32[512,2048]{1,0:T(8,128)}, bf16[16,16,128]{2,1,0:T(8,128)(2,1)}) custom-call(bf16[512,2048]{1,0:T(8,128)(2,1)} %gate_ref.1, bf16[512,2048]{1,0:T(8,128)(2,1)} %outer_ref.3, bf16[512,2048]{1,0:T(8,128)(2,1)} %value_ref.1, f32[16,1,128]{2,1,0:T(1,128)} %bitcast.8, f32[16,1,128]{2,1,0:T(1,128)} %bitcast.12, f32[16,1,128]{2,1,0:T(1,128)} %bitcast.14), custom_call_target="tpu_custom_call" | custom-call | flops 4294967296 | bytes 10485760 | tf_op jit(solution)/shard_map/local_part/pallas_call | solution.py:231
  36.4 0.6 pad_add_fusion.place_ref
  37.0 0.9 collective-permute-done.3.other_ref
  37.9 0.6 copy-done
  38.5 1.6 shard_map.113.pair_ref
  40.1 0.9 collective-permute-start.4
  41.0 3.6 %collective-permute-done.4.far_ref = bf16[16,16,128]{2,1,0:T(8,128)(2,1)S(1)} collective-permute-done((bf16[16,16,128]{2,1,0:T(8,128)(2,1)}, bf16[16,16,128]{2,1,0:T(8,128)(2,1)S(1)}, u32[]{:S(2)}, u32[]{:S(2)}) %collective-permute-start.4) | collective-permute-done | bytes 65568 | tf_op jit(solution)/shard_map/ppermute | solution.py:554
  44.5 0.5 collective-permute-start.8
  45.1 3.4 %pack.5 = (bf16[1536,128]{1,0:T(8,128)(2,1)}, bf16[1536,128]{1,0:T(8,128)(2,1)}, bf16[1536,128]{1,0:T(8,128)(2,1)}, bf16[1536,128]{1,0:T(8,128)(2,1)}, bf16[1536...) custom-call(s32[1]{0:T(128)} %bitcast.place_ref, ...), custom_call_target="tpu_custom_call" | custom-call | bytes 6291456 | tf_op jit(solution)/shard_map/pack/pallas_call | solution.py:323
  48.5 2.1 %collective-permute-start.11 = (bf16[1536,128]{1,0:T(8,128)(2,1)}, bf16[1536,128]{1,0:T(8,128)(2,1)S(1)}, u32[]{:S(2)}, u32[]{:S(2)}) collective-permute-start(bf16[1536,128]{1,0:T(8,128)(2,1)} %get-tuple-element.46), channel_id=1, source_target_pairs={{0,28},{4,24},{8,20},{12,16},{16,12},{20,8},{24,4},{28,0},{1,29},{... | collective-permute-start | bytes 1179656 | tf_op jit(solution)/shard_map/ppermute | solution.py:554
  50.6 1.1 collective-permute-start.13
  51.7 13.5 %collective-permute-done.8.refs_4_ = bf16[1536,128]{1,0:T(8,128)(2,1)} collective-permute-done((bf16[1536,128]{1,0:T(8,128)(2,1)}, bf16[1536,128]{1,0:T(8,128)(2,1)}, u32[]{:S(2)}, u32[]{:S(2)}) %collective-permute-start.8) | collective-permute-done | bytes 393248 | tf_op jit(solution)/shard_map/ppermute | solution.py:554
  65.3 4.5 %collective-permute-done.9.refs_5_ = bf16[1536,128]{1,0:T(8,128)(2,1)} collective-permute-done((bf16[1536,128]{1,0:T(8,128)(2,1)}, bf16[1536,128]{1,0:T(8,128)(2,1)}, u32[]{:S(2)}, u32[]{:S(2)}) %collective-permute-start.9) | collective-permute-done | bytes 393248 | tf_op jit(solution)/shard_map/ppermute | solution.py:554
  69.8 1.5 collective-permute-start.15
  71.3 1.9 %collective-permute-start.16 = (bf16[1536,128]{1,0:T(8,128)(2,1)}, bf16[1536,128]{1,0:T(8,128)(2,1)}, u32[]{:S(2)}, u32[]{:S(2)}) collective-permute-start(bf16[1536,128]{1,0:T(8,128)(2,1)} %get-tuple-element.65), channel_id=1, source_target_pairs={{0,20},{4,16},{8,28},{12,24},{16,4},{20,0},{24,12},{28,8},{1,21},{... | collective-permute-start | bytes 1179656 | tf_op jit(solution)/shard_map/ppermute | solution.py:554
  73.2 1.5 collective-permute-start.17
  74.7 0.4 collective-permute-start.18
  75.1 38.1 %flash.2 = (bf16[512,128]{1,0:T(8,128)(2,1)}, bf16[512,128]{1,0:T(8,128)(2,1)}, bf16[512,128]{1,0:T(8,128)(2,1)}, bf16[512,128]{1,0:T(8,128)(2,1)}, bf16[512,128...) custom-call(s32[1]{0:T(128)} %bitcast.place_ref, ...), custom_call_target="tpu_custom_call" | custom-call | flops 9663676416 | bytes 4194304 | tf_op jit(solution)/shard_map/flash/pallas_call | solution.py:467
  113.2 1.6 shard_map.114
  114.9 1.4 collective-permute-start.20
  116.3 1.7 collective-permute-start.21
  118.0 1.0 collective-permute-start.23
  119.0 1.0 collective-permute-start.19
  120.1 37.8 %flash.3 = (bf16[512,128]{1,0:T(8,128)(2,1)}, bf16[512,128]{1,0:T(8,128)(2,1)}, bf16[512,128]{1,0:T(8,128)(2,1)}, bf16[512,128]{1,0:T(8,128)(2,1)}, bf16[512,128...) custom-call(s32[1]{0:T(128)} %bitcast.place_ref, ...), custom_call_target="tpu_custom_call" | custom-call | flops 9663676416 | bytes 4194304 | tf_op jit(solution)/shard_map/flash/pallas_call | solution.py:467
  157.9 1.1 collective-permute-start.24
  159.0 1.9 %collective-permute-start.25 = (bf16[512,128]{1,0:T(8,128)(2,1)}, bf16[512,128]{1,0:T(8,128)(2,1)S(1)}, u32[]{:S(2)}, u32[]{:S(2)}) collective-permute-start(bf16[512,128]{1,0:T(8,128)(2,1)} %get-tuple-element.76), channel_id=1, source_target_pairs={{0,24},{4,28},{8,16},{12,20},{16,8},{20,12},{24,0},{28,4},{1,25},{... | collective-permute-start | bytes 393224 | tf_op jit(solution)/shard_map/ppermute | solution.py:554
  161.0 0.9 collective-permute-start.26
  162.1 1.9 %collective-permute-start.28 = (bf16[512,128]{1,0:T(8,128)(2,1)}, bf16[512,128]{1,0:T(8,128)(2,1)}, u32[]{:S(2)}, u32[]{:S(2)}) collective-permute-start(bf16[512,128]{1,0:T(8,128)(2,1)} %get-tuple-element.80), channel_id=1, source_target_pairs={{0,8},{4,12},{8,0},{12,4},{16,24},{20,28},{24,16},{28,20},{1,9},{5... | collective-permute-start | bytes 393224 | tf_op jit(solution)/shard_map/ppermute | solution.py:554
  164.0 5.4 %collective-permute-done.24.refs_5_ = bf16[512,128]{1,0:T(8,128)(2,1)S(1)} collective-permute-done((bf16[512,128]{1,0:T(8,128)(2,1)}, bf16[512,128]{1,0:T(8,128)(2,1)S(1)}, u32[]{:S(2)}, u32[]{:S(2)}) %collective-permute-start.24) | collective-permute-done | bytes 131104 | tf_op jit(solution)/shard_map/ppermute | solution.py:554
  169.5 1.6 collective-permute-start.29
  171.1 1.6 collective-permute-start.30
  172.7 1.3 collective-permute-start.32
  174.0 1.5 collective-permute-start.33
  175.5 6.4 %remote_part.1 = bf16[512,2048]{1,0:T(8,128)(2,1)} custom-call(s32[1]{0:T(128)} %bitcast.place_ref, f32[512,2048]{1,0:T(8,128)} %get-tuple-element.48.part_ref, bf16[512,2048]{1,0:T(8,128)(2,1)} %outer_ref.3, f32[16,1,128]{2,1,0:T(1,128)} %bitcast.11, f32[16,1,128]{2,1,0:T(1,128)} %bitcast.13, f32[16,16,128]{2,1,0:T(8,128)} %get-tuple-element.69.before_ref, ...), custom_call_target="tpu_custom_call" | custom-call | flops 805306368 | bytes 8388608 | tf_op jit(solution)/shard_map/remote_part/pallas_call | solution.py:254
  181.9 0.8 collective-permute-done.30.refs_12_
  182.8 1.6 collective-permute-done.31.refs_13_
  184.4 2.6 %join.1 = bf16[512,2048]{1,0:T(8,128)(2,1)} custom-call(s32[1]{0:T(128)} %bitcast.place_ref, bf16[512,128]{1,0:T(8,128)(2,1)} %get-tuple-element.56.refs_0_, bf16[512,128]{1,0:T(8,128)(2,1)} %copy-done.1, bf16[512,128]{1,0:T(8,128)(2,1)} %copy-done.2, bf16[512,128]{1,0:T(8,128)(2,1)} %copy-done.3, bf16[512,128]{1,0:T(8,128)(2,1)} %copy-done.4, ...), custom_call_target="tpu_custom_call" | custom-call | bytes 4194304 | tf_op jit(solution)/shard_map/join/pallas_call | solution.py:515
  (73 shorter events, 0.9 us)
Async XLA Ops:
  2.5 6.9 %copy-start.10 = (f32[128,16]{0,1:T(8,128)S(1)}, f32[128,16]{0,1:T(8,128)}, u32[]{:S(2)}) copy-start(f32[128,16]{0,1:T(8,128)} %param.14) | copy-start | bytes 24580
  2.5 6.9 %copy-start.11 = (f32[128,16]{0,1:T(8,128)S(1)}, f32[128,16]{0,1:T(8,128)}, u32[]{:S(2)}) copy-start(f32[128,16]{0,1:T(8,128)} %param.13) | copy-start | bytes 24580
  2.5 11.6 %copy-start.16 = (s32[128]{0:T(128)S(1)}, s32[128]{0:T(128)}, u32[]{:S(2)}) copy-start(s32[128]{0:T(128)} %param.16) | copy-start | bytes 1540
  2.5 42.6 %collective-permute-start.10 = (bf16[1536,128]{1,0:T(8,128)(2,1)}, bf16[1536,128]{1,0:T(8,128)(2,1)S(1)}, u32[]{:S(2)}, u32[]{:S(2)}) collective-permute-start(bf16[1536,128]{1,0:T(8,128)(2,1)} %pack.3), channel_id=1, source_target_pairs={{0,24},{4,28},{8,16},{12,20},{16,8},{20,12},{24,0},{28,4},{1,25},{... | collective-permute-start | bytes 1179656 | tf_op jit(solution)/shard_map/ppermute | solution.py:554
  9.4 5.1 %collective-permute-start.2 = (f32[128,32]{0,1:T(8,128)S(1)}, f32[128,32]{0,1:T(8,128)S(1)}, u32[]{:S(2)}, u32[]{:S(2)}) collective-permute-start(f32[128,32]{0,1:T(8,128)S(1)} %pad_maximum_fusion), channel_id=1, source_target_pairs={{0,3},{1,0},{2,1},{3,2},{4,7},{5,4},{6,5},{7,6},{8,11},{9,8},{10,9... | collective-permute-start | bytes 49160 | tf_op jit(solution)/shard_map/ppermute | solution.py:199
  13.1 4.6 %collective-permute-start.1 = (f32[128,32]{0,1:T(8,128)S(1)}, f32[128,32]{0,1:T(8,128)S(1)}, u32[]{:S(2)}, u32[]{:S(2)}) collective-permute-start(f32[128,32]{0,1:T(8,128)S(1)} %pad_maximum_fusion), channel_id=1, source_target_pairs={{0,2},{1,3},{2,0},{3,1},{4,6},{5,7},{6,4},{7,5},{8,10},{9,11},{10,... | collective-permute-start | bytes 49160 | tf_op jit(solution)/shard_map/ppermute | solution.py:199
  13.1 5.5 %collective-permute-start = (f32[128,32]{0,1:T(8,128)S(1)}, f32[128,32]{0,1:T(8,128)S(1)}, u32[]{:S(2)}, u32[]{:S(2)}) collective-permute-start(f32[128,32]{0,1:T(8,128)S(1)} %pad_maximum_fusion), channel_id=1, source_target_pairs={{0,1},{1,2},{2,3},{3,0},{4,5},{5,6},{6,7},{7,4},{8,9},{9,10},{10,1... | collective-permute-start | bytes 49160 | tf_op jit(solution)/shard_map/ppermute | solution.py:199
  14.1 34.4 %collective-permute-start.5 = (bf16[1536,128]{1,0:T(8,128)(2,1)}, bf16[1536,128]{1,0:T(8,128)(2,1)S(1)}, u32[]{:S(2)}, u32[]{:S(2)}) collective-permute-start(bf16[1536,128]{1,0:T(8,128)(2,1)} %get-tuple-element.51), channel_id=1, source_target_pairs={{0,4},{4,0},{8,12},{12,8},{16,20},{20,16},{24,28},{28,24},{1,5},{5... | collective-permute-start | bytes 1179656 | tf_op jit(solution)/shard_map/ppermute | solution.py:554
  14.5 36.1 %collective-permute-start.6 = (bf16[1536,128]{1,0:T(8,128)(2,1)}, bf16[1536,128]{1,0:T(8,128)(2,1)}, u32[]{:S(2)}, u32[]{:S(2)}) collective-permute-start(bf16[1536,128]{1,0:T(8,128)(2,1)} %get-tuple-element.52), channel_id=1, source_target_pairs={{0,8},{4,12},{8,0},{12,4},{16,24},{20,28},{24,16},{28,20},{1,9},{5... | collective-permute-start | bytes 1179656 | tf_op jit(solution)/shard_map/ppermute | solution.py:554
  17.7 32.9 %collective-permute-start.7 = (bf16[1536,128]{1,0:T(8,128)(2,1)}, bf16[1536,128]{1,0:T(8,128)(2,1)}, u32[]{:S(2)}, u32[]{:S(2)}) collective-permute-start(bf16[1536,128]{1,0:T(8,128)(2,1)} %get-tuple-element.53), channel_id=1, source_target_pairs={{0,12},{4,8},{8,4},{12,0},{16,28},{20,24},{24,20},{28,16},{1,13},{... | collective-permute-start | bytes 1179656 | tf_op jit(solution)/shard_map/ppermute | solution.py:554
  36.4 1.5 collective-permute-start.3
  40.1 4.5 %collective-permute-start.4 = (bf16[16,16,128]{2,1,0:T(8,128)(2,1)}, bf16[16,16,128]{2,1,0:T(8,128)(2,1)S(1)}, u32[]{:S(2)}, u32[]{:S(2)}) collective-permute-start(bf16[16,16,128]{2,1,0:T(8,128)(2,1)} %shard_map.113.pair_ref), channel_id=1, source_target_pairs={{0,8},{4,12},{8,0},{12,4},{16,24},{20,28},{24,16},{28,20},{1,9},{5... | collective-permute-start | bytes 196616 | tf_op jit(solution)/shard_map/ppermute | solution.py:554
  44.5 3.9 %copy-start.9 = (bf16[16,16,128]{2,1,0:T(8,128)(2,1)}, bf16[16,16,128]{2,1,0:T(8,128)(2,1)S(1)}, u32[]{:S(2)}) copy-start(bf16[16,16,128]{2,1,0:T(8,128)(2,1)S(1)} %collective-permute-done.4.far_ref) | copy-start | bytes 196612
  44.5 20.7 %collective-permute-start.8 = (bf16[1536,128]{1,0:T(8,128)(2,1)}, bf16[1536,128]{1,0:T(8,128)(2,1)}, u32[]{:S(2)}, u32[]{:S(2)}) collective-permute-start(bf16[1536,128]{1,0:T(8,128)(2,1)} %get-tuple-element.54), channel_id=1, source_target_pairs={{0,16},{4,20},{8,24},{12,28},{16,0},{20,4},{24,8},{28,12},{1,17},{... | collective-permute-start | bytes 1179656 | tf_op jit(solution)/shard_map/ppermute | solution.py:554
  45.1 24.7 %collective-permute-start.9 = (bf16[1536,128]{1,0:T(8,128)(2,1)}, bf16[1536,128]{1,0:T(8,128)(2,1)}, u32[]{:S(2)}, u32[]{:S(2)}) collective-permute-start(bf16[1536,128]{1,0:T(8,128)(2,1)} %get-tuple-element.55), channel_id=1, source_target_pairs={{0,20},{4,16},{8,28},{12,24},{16,4},{20,0},{24,12},{28,8},{1,21},{... | collective-permute-start | bytes 1179656 | tf_op jit(solution)/shard_map/ppermute | solution.py:554
  48.5 26.6 %copy-start.13 = (bf16[1536,128]{1,0:T(8,128)(2,1)}, bf16[1536,128]{1,0:T(8,128)(2,1)S(1)}, u32[]{:S(2)}) copy-start(bf16[1536,128]{1,0:T(8,128)(2,1)S(1)} %collective-permute-done.5.refs_1_) | copy-start | bytes 1179652
  48.5 22.8 %collective-permute-start.11 = (bf16[1536,128]{1,0:T(8,128)(2,1)}, bf16[1536,128]{1,0:T(8,128)(2,1)S(1)}, u32[]{:S(2)}, u32[]{:S(2)}) collective-permute-start(bf16[1536,128]{1,0:T(8,128)(2,1)} %get-tuple-element.46), channel_id=1, source_target_pairs={{0,28},{4,24},{8,20},{12,16},{16,12},{20,8},{24,4},{28,0},{1,29},{... | collective-permute-start | bytes 1179656 | tf_op jit(solution)/shard_map/ppermute | solution.py:554
  50.6 22.6 %collective-permute-start.12 = (bf16[1536,128]{1,0:T(8,128)(2,1)}, bf16[1536,128]{1,0:T(8,128)(2,1)S(1)}, u32[]{:S(2)}, u32[]{:S(2)}) collective-permute-start(bf16[1536,128]{1,0:T(8,128)(2,1)} %get-tuple-element.61), channel_id=1, source_target_pairs={{0,4},{4,0},{8,12},{12,8},{16,20},{20,16},{24,28},{28,24},{1,5},{5... | collective-permute-start | bytes 1179656 | tf_op jit(solution)/shard_map/ppermute | solution.py:554
  50.6 24.1 %collective-permute-start.13 = (bf16[1536,128]{1,0:T(8,128)(2,1)}, bf16[1536,128]{1,0:T(8,128)(2,1)}, u32[]{:S(2)}, u32[]{:S(2)}) collective-permute-start(bf16[1536,128]{1,0:T(8,128)(2,1)} %get-tuple-element.62), channel_id=1, source_target_pairs={{0,8},{4,12},{8,0},{12,4},{16,24},{20,28},{24,16},{28,20},{1,9},{5... | collective-permute-start | bytes 1179656 | tf_op jit(solution)/shard_map/ppermute | solution.py:554
  65.3 49.6 %collective-permute-start.14 = (bf16[1536,128]{1,0:T(8,128)(2,1)}, bf16[1536,128]{1,0:T(8,128)(2,1)}, u32[]{:S(2)}, u32[]{:S(2)}) collective-permute-start(bf16[1536,128]{1,0:T(8,128)(2,1)} %get-tuple-element.63), channel_id=1, source_target_pairs={{0,12},{4,8},{8,4},{12,0},{16,28},{20,24},{24,20},{28,16},{1,13},{... | collective-permute-start | bytes 1179656 | tf_op jit(solution)/shard_map/ppermute | solution.py:554
  69.8 46.5 %collective-permute-start.15 = (bf16[1536,128]{1,0:T(8,128)(2,1)}, bf16[1536,128]{1,0:T(8,128)(2,1)}, u32[]{:S(2)}, u32[]{:S(2)}) collective-permute-start(bf16[1536,128]{1,0:T(8,128)(2,1)} %get-tuple-element.64), channel_id=1, source_target_pairs={{0,16},{4,20},{8,24},{12,28},{16,0},{20,4},{24,8},{28,12},{1,17},{... | collective-permute-start | bytes 1179656 | tf_op jit(solution)/shard_map/ppermute | solution.py:554
  71.3 46.7 %collective-permute-start.16 = (bf16[1536,128]{1,0:T(8,128)(2,1)}, bf16[1536,128]{1,0:T(8,128)(2,1)}, u32[]{:S(2)}, u32[]{:S(2)}) collective-permute-start(bf16[1536,128]{1,0:T(8,128)(2,1)} %get-tuple-element.65), channel_id=1, source_target_pairs={{0,20},{4,16},{8,28},{12,24},{16,4},{20,0},{24,12},{28,8},{1,21},{... | collective-permute-start | bytes 1179656 | tf_op jit(solution)/shard_map/ppermute | solution.py:554
  73.2 40.0 %copy-start.14 = (bf16[1536,128]{1,0:T(8,128)(2,1)}, bf16[1536,128]{1,0:T(8,128)(2,1)S(1)}, u32[]{:S(2)}) copy-start(bf16[1536,128]{1,0:T(8,128)(2,1)S(1)} %collective-permute-done.12.refs_1_) | copy-start | bytes 1179652
  73.2 44.7 %collective-permute-start.17 = (bf16[1536,128]{1,0:T(8,128)(2,1)}, bf16[1536,128]{1,0:T(8,128)(2,1)}, u32[]{:S(2)}, u32[]{:S(2)}) collective-permute-start(bf16[1536,128]{1,0:T(8,128)(2,1)} %get-tuple-element.66), channel_id=1, source_target_pairs={{0,24},{4,28},{8,16},{12,20},{16,8},{20,12},{24,0},{28,4},{1,25},{... | collective-permute-start | bytes 1179656 | tf_op jit(solution)/shard_map/ppermute | solution.py:554
  74.7 44.3 %collective-permute-start.18 = (bf16[1536,128]{1,0:T(8,128)(2,1)}, bf16[1536,128]{1,0:T(8,128)(2,1)}, u32[]{:S(2)}, u32[]{:S(2)}) collective-permute-start(bf16[1536,128]{1,0:T(8,128)(2,1)} %get-tuple-element.67), channel_id=1, source_target_pairs={{0,28},{4,24},{8,20},{12,16},{16,12},{20,8},{24,4},{28,0},{1,29},{... | collective-permute-start | bytes 1179656 | tf_op jit(solution)/shard_map/ppermute | solution.py:554
  114.9 44.2 %collective-permute-start.20 = (bf16[512,128]{1,0:T(8,128)(2,1)}, bf16[512,128]{1,0:T(8,128)(2,1)S(1)}, u32[]{:S(2)}, u32[]{:S(2)}) collective-permute-start(bf16[512,128]{1,0:T(8,128)(2,1)} %get-tuple-element.71), channel_id=1, source_target_pairs={{0,4},{4,0},{8,12},{12,8},{16,20},{20,16},{24,28},{28,24},{1,5},{5... | collective-permute-start | bytes 393224 | tf_op jit(solution)/shard_map/ppermute | solution.py:554
  116.3 44.7 %collective-permute-start.21 = (bf16[512,128]{1,0:T(8,128)(2,1)}, bf16[512,128]{1,0:T(8,128)(2,1)S(1)}, u32[]{:S(2)}, u32[]{:S(2)}) collective-permute-start(bf16[512,128]{1,0:T(8,128)(2,1)} %get-tuple-element.72), channel_id=1, source_target_pairs={{0,8},{4,12},{8,0},{12,4},{16,24},{20,28},{24,16},{28,20},{1,9},{5... | collective-permute-start | bytes 393224 | tf_op jit(solution)/shard_map/ppermute | solution.py:554
  118.0 43.9 %collective-permute-start.22 = (bf16[512,128]{1,0:T(8,128)(2,1)}, bf16[512,128]{1,0:T(8,128)(2,1)S(1)}, u32[]{:S(2)}, u32[]{:S(2)}) collective-permute-start(bf16[512,128]{1,0:T(8,128)(2,1)} %get-tuple-element.73), channel_id=1, source_target_pairs={{0,12},{4,8},{8,4},{12,0},{16,28},{20,24},{24,20},{28,16},{1,13},{... | collective-permute-start | bytes 393224 | tf_op jit(solution)/shard_map/ppermute | solution.py:554
  118.0 44.1 %collective-permute-start.23 = (bf16[512,128]{1,0:T(8,128)(2,1)}, bf16[512,128]{1,0:T(8,128)(2,1)S(1)}, u32[]{:S(2)}, u32[]{:S(2)}) collective-permute-start(bf16[512,128]{1,0:T(8,128)(2,1)} %get-tuple-element.74), channel_id=1, source_target_pairs={{0,16},{4,20},{8,24},{12,28},{16,0},{20,4},{24,8},{28,12},{1,17},{... | collective-permute-start | bytes 393224 | tf_op jit(solution)/shard_map/ppermute | solution.py:554
  119.0 38.9 %collective-permute-start.19 = (bf16[16,16,128]{2,1,0:T(8,128)(2,1)}, bf16[16,16,128]{2,1,0:T(8,128)(2,1)S(1)}, u32[]{:S(2)}, u32[]{:S(2)}) collective-permute-start(bf16[16,16,128]{2,1,0:T(8,128)(2,1)} %get-tuple-element.70), channel_id=1, source_target_pairs={{0,16},{4,20},{8,24},{12,28},{16,0},{20,4},{24,8},{28,12},{1,17},{... | collective-permute-start | bytes 196616 | tf_op jit(solution)/shard_map/ppermute | solution.py:554
  157.9 17.6 %copy-start.8 = (bf16[16,16,128]{2,1,0:T(8,128)(2,1)}, bf16[16,16,128]{2,1,0:T(8,128)(2,1)S(1)}, u32[]{:S(2)}) copy-start(bf16[16,16,128]{2,1,0:T(8,128)(2,1)S(1)} %collective-permute-done.19.other_ref) | copy-start | bytes 196612
  157.9 11.5 %collective-permute-start.24 = (bf16[512,128]{1,0:T(8,128)(2,1)}, bf16[512,128]{1,0:T(8,128)(2,1)S(1)}, u32[]{:S(2)}, u32[]{:S(2)}) collective-permute-start(bf16[512,128]{1,0:T(8,128)(2,1)} %get-tuple-element.75), channel_id=1, source_target_pairs={{0,20},{4,16},{8,28},{12,24},{16,4},{20,0},{24,12},{28,8},{1,21},{... | collective-permute-start | bytes 393224 | tf_op jit(solution)/shard_map/ppermute | solution.py:554
  159.0 22.8 %copy-start.1 = (bf16[512,128]{1,0:T(8,128)(2,1)}, bf16[512,128]{1,0:T(8,128)(2,1)S(1)}, u32[]{:S(2)}) copy-start(bf16[512,128]{1,0:T(8,128)(2,1)S(1)} %collective-permute-done.20.refs_1_) | copy-start | bytes 393220
  159.0 12.0 %collective-permute-start.25 = (bf16[512,128]{1,0:T(8,128)(2,1)}, bf16[512,128]{1,0:T(8,128)(2,1)S(1)}, u32[]{:S(2)}, u32[]{:S(2)}) collective-permute-start(bf16[512,128]{1,0:T(8,128)(2,1)} %get-tuple-element.76), channel_id=1, source_target_pairs={{0,24},{4,28},{8,16},{12,20},{16,8},{20,12},{24,0},{28,4},{1,25},{... | collective-permute-start | bytes 393224 | tf_op jit(solution)/shard_map/ppermute | solution.py:554
  161.0 20.9 %copy-start.2 = (bf16[512,128]{1,0:T(8,128)(2,1)}, bf16[512,128]{1,0:T(8,128)(2,1)S(1)}, u32[]{:S(2)}) copy-start(bf16[512,128]{1,0:T(8,128)(2,1)S(1)} %collective-permute-done.21.refs_2_) | copy-start | bytes 393220
  161.0 11.7 %collective-permute-start.26 = (bf16[512,128]{1,0:T(8,128)(2,1)}, bf16[512,128]{1,0:T(8,128)(2,1)S(1)}, u32[]{:S(2)}, u32[]{:S(2)}) collective-permute-start(bf16[512,128]{1,0:T(8,128)(2,1)} %get-tuple-element.77), channel_id=1, source_target_pairs={{0,28},{4,24},{8,20},{12,16},{16,12},{20,8},{24,4},{28,0},{1,29},{... | collective-permute-start | bytes 393224 | tf_op jit(solution)/shard_map/ppermute | solution.py:554
  161.9 20.0 %copy-start.3 = (bf16[512,128]{1,0:T(8,128)(2,1)}, bf16[512,128]{1,0:T(8,128)(2,1)S(1)}, u32[]{:S(2)}) copy-start(bf16[512,128]{1,0:T(8,128)(2,1)S(1)} %collective-permute-done.22.refs_3_) | copy-start | bytes 393220
  161.9 10.8 %collective-permute-start.27 = (bf16[512,128]{1,0:T(8,128)(2,1)}, bf16[512,128]{1,0:T(8,128)(2,1)}, u32[]{:S(2)}, u32[]{:S(2)}) collective-permute-start(bf16[512,128]{1,0:T(8,128)(2,1)} %get-tuple-element.79), channel_id=1, source_target_pairs={{0,4},{4,0},{8,12},{12,8},{16,20},{20,16},{24,28},{28,24},{1,5},{5... | collective-permute-start | bytes 393224 | tf_op jit(solution)/shard_map/ppermute | solution.py:554
  162.1 19.8 %copy-start.4 = (bf16[512,128]{1,0:T(8,128)(2,1)}, bf16[512,128]{1,0:T(8,128)(2,1)S(1)}, u32[]{:S(2)}) copy-start(bf16[512,128]{1,0:T(8,128)(2,1)S(1)} %collective-permute-done.23.refs_4_) | copy-start | bytes 393220
  162.1 11.9 %collective-permute-start.28 = (bf16[512,128]{1,0:T(8,128)(2,1)}, bf16[512,128]{1,0:T(8,128)(2,1)}, u32[]{:S(2)}, u32[]{:S(2)}) collective-permute-start(bf16[512,128]{1,0:T(8,128)(2,1)} %get-tuple-element.80), channel_id=1, source_target_pairs={{0,8},{4,12},{8,0},{12,4},{16,24},{20,28},{24,16},{28,20},{1,9},{5... | collective-permute-start | bytes 393224 | tf_op jit(solution)/shard_map/ppermute | solution.py:554
  169.5 12.4 %copy-start.5 = (bf16[512,128]{1,0:T(8,128)(2,1)}, bf16[512,128]{1,0:T(8,128)(2,1)S(1)}, u32[]{:S(2)}) copy-start(bf16[512,128]{1,0:T(8,128)(2,1)S(1)} %collective-permute-done.24.refs_5_) | copy-start | bytes 393220
  169.5 12.4 %collective-permute-start.29 = (bf16[512,128]{1,0:T(8,128)(2,1)}, bf16[512,128]{1,0:T(8,128)(2,1)}, u32[]{:S(2)}, u32[]{:S(2)}) collective-permute-start(bf16[512,128]{1,0:T(8,128)(2,1)} %get-tuple-element.81), channel_id=1, source_target_pairs={{0,12},{4,8},{8,4},{12,0},{16,28},{20,24},{24,20},{28,16},{1,13},{... | collective-permute-start | bytes 393224 | tf_op jit(solution)/shard_map/ppermute | solution.py:554
  171.1 10.8 %copy-start.6 = (bf16[512,128]{1,0:T(8,128)(2,1)}, bf16[512,128]{1,0:T(8,128)(2,1)S(1)}, u32[]{:S(2)}) copy-start(bf16[512,128]{1,0:T(8,128)(2,1)S(1)} %collective-permute-done.25.refs_6_) | copy-start | bytes 393220
  171.1 11.7 %collective-permute-start.30 = (bf16[512,128]{1,0:T(8,128)(2,1)}, bf16[512,128]{1,0:T(8,128)(2,1)}, u32[]{:S(2)}, u32[]{:S(2)}) collective-permute-start(bf16[512,128]{1,0:T(8,128)(2,1)} %get-tuple-element.82), channel_id=1, source_target_pairs={{0,16},{4,20},{8,24},{12,28},{16,0},{20,4},{24,8},{28,12},{1,17},{... | collective-permute-start | bytes 393224 | tf_op jit(solution)/shard_map/ppermute | solution.py:554
  172.7 9.3 %copy-start.7 = (bf16[512,128]{1,0:T(8,128)(2,1)}, bf16[512,128]{1,0:T(8,128)(2,1)S(1)}, u32[]{:S(2)}) copy-start(bf16[512,128]{1,0:T(8,128)(2,1)S(1)} %collective-permute-done.26.refs_7_) | copy-start | bytes 393220
  172.7 11.7 %collective-permute-start.31 = (bf16[512,128]{1,0:T(8,128)(2,1)}, bf16[512,128]{1,0:T(8,128)(2,1)}, u32[]{:S(2)}, u32[]{:S(2)}) collective-permute-start(bf16[512,128]{1,0:T(8,128)(2,1)} %get-tuple-element.83), channel_id=1, source_target_pairs={{0,20},{4,16},{8,28},{12,24},{16,4},{20,0},{24,12},{28,8},{1,21},{... | collective-permute-start | bytes 393224 | tf_op jit(solution)/shard_map/ppermute | solution.py:554
  172.7 11.7 %collective-permute-start.32 = (bf16[512,128]{1,0:T(8,128)(2,1)}, bf16[512,128]{1,0:T(8,128)(2,1)}, u32[]{:S(2)}, u32[]{:S(2)}) collective-permute-start(bf16[512,128]{1,0:T(8,128)(2,1)} %get-tuple-element.84), channel_id=1, source_target_pairs={{0,24},{4,28},{8,16},{12,20},{16,8},{20,12},{24,0},{28,4},{1,25},{... | collective-permute-start | bytes 393224 | tf_op jit(solution)/shard_map/ppermute | solution.py:554
  174.0 10.4 %collective-permute-start.33 = (bf16[512,128]{1,0:T(8,128)(2,1)}, bf16[512,128]{1,0:T(8,128)(2,1)}, u32[]{:S(2)}, u32[]{:S(2)}) collective-permute-start(bf16[512,128]{1,0:T(8,128)(2,1)} %get-tuple-element.85), channel_id=1, source_target_pairs={{0,28},{4,24},{8,20},{12,16},{16,12},{20,8},{24,4},{28,0},{1,29},{... | collective-permute-start | bytes 393224 | tf_op jit(solution)/shard_map/ppermute | solution.py:554
  (3 other events, 6.0 us)

commit v5 on v4

--- a/solution.py
+++ b/solution.py
@@ -22,6 +22,7 @@
 floor_score = -1e30
 LOG2E = 1.4426950408889634
 TOO_SMALL = 2.0**-80
+AHEAD = 2
 
 
 F32 = jnp.float32
@@ -396,11 +397,11 @@
         most = jnp.max(key_square, axis=1, keepdims=True)
         shift = jnp.sqrt(squares(q_buf[i * wide : (i + 1) * wide, :]) * most) * scale
         jobs = jobs_of(i)
-        following = score(i, jobs[0])
+        waiting = [score(i, job) for job in jobs[:AHEAD]]
         for n, (start, count, first, _) in enumerate(jobs):
-            scores = following
-            if n + 1 < len(jobs):
-                following = score(i, jobs[n + 1])
+            if n + AHEAD < len(jobs):
+                waiting.append(score(i, jobs[n + AHEAD]))
+            scores = waiting.pop(0)
             weights = jnp.exp2(scores * scale - shift[:, first:])
             total = jnp.sum(weights.reshape(count // 8, 8, wide - first), axis=0)
             update = mxu(vt_buf[:, start : start + count], weights.astype(BF16), PLAIN)

time: 188 us -> 187 us (level)
  transfers between devices with their start and end apart: 34 -> 34, of which waited for: 10 -> 10; matrix products, arithmetic and copies ran while one was open for 1% -> 1% of each run, Pallas kernels for 58% -> 57%
where the time goes in v5:
time: 187 us; the launch traced here: 186 us
  Pallas kernels  111 us (59%)
  starting transfers between devices  36.4 us (19%)
  waiting for transfers between devices  34.5 us (18%)
  local copies, waits for them, and re-layouts  2.28 us (1%)
    pallas_call x2, Pallas kernels, flash(): pl.pallas_call(functools.partial(flash_kernel, blocks=blocks), in_specs=[...  75.2 us
    ppermute x31, starting transfers between devices, swap(): return lax.ppermute(a, 'ctx', [(i, i ^ r) for i in range(ctx_size)])  31.7 us
    ppermute x31, waiting for transfers between devices, swap(): return lax.ppermute(a, 'ctx', [(i, i ^ r) for i in range(ctx_size)])  30.5 us
    pallas_call x1, Pallas kernels, local_part(): pl.pallas_call(local_kernel, grid=grid, in_specs=[wide, wide, wide, row,...  15.9 us
    pallas_call x3, Pallas kernels, pack(): pl.pallas_call(functools.partial(pack_kernel, spots=spots, heads=heads, h...  8.11 us
    pallas_call x1, Pallas kernels, remote_part(): pl.pallas_call(remote_kernel, grid=grid, in_specs=[pl.BlockSpec(memory_sp...  6.37 us
    ppermute x3, starting transfers between devices, gathered_modes(): lax.ppermute(modes, 'tp', [(i, (i + shift) % tp_size) for i in range(tp_s...  4.67 us
    ppermute x3, waiting for transfers between devices, gathered_modes(): lax.ppermute(modes, 'tp', [(i, (i + shift) % tp_size) for i in range(tp_s...  3.96 us
  transfers between devices with their start and end apart: 34, of which 10 were waited for; matrix products, arithmetic and copies ran while one was open for 1% of the time, Pallas kernels for 57%

profile of v5, /device:TPU:0, one launch (start us, length us, event | category | flops | bytes accessed | tf_op | source)
XLA Modules:
  0.0 186.4 jit_solution(339093922320184659)
XLA Ops:
  0.6 1.8 pack.3
  2.5 4.0 %collective-permute-start.10 = (bf16[1536,128]{1,0:T(8,128)(2,1)}, bf16[1536,128]{1,0:T(8,128)(2,1)S(1)}, u32[]{:S(2)}, u32[]{:S(2)}) collective-permute-start(bf16[1536,128]{1,0:T(8,128)(2,1)} %pack.3), channel_id=1, source_target_pairs={{0,24},{4,28},{8,16},{12,20},{16,8},{20,12},{24,0},{28,4},{1,25},{... | collective-permute-start | bytes 1179656 | tf_op jit(solution)/shard_map/ppermute | solution.py:555
  6.5 2.9 %pack.4 = (bf16[1536,128]{1,0:T(8,128)(2,1)}, bf16[1536,128]{1,0:T(8,128)(2,1)}, bf16[1536,128]{1,0:T(8,128)(2,1)}, bf16[1536,128]{1,0:T(8,128)(2,1)}, bf16[1536...) custom-call(s32[1]{0:T(128)} %bitcast.place_ref, bf16[512,2048]{1,0:T(8,128)(2,1)} %q_ref.2, ...), custom_call_target="tpu_custom_call" | custom-call | bytes 5505024 | tf_op jit(solution)/shard_map/pack/pallas_call | solution.py:324
  9.4 3.7 %collective-permute-start.2 = (f32[128,32]{0,1:T(8,128)S(1)}, f32[128,32]{0,1:T(8,128)S(1)}, u32[]{:S(2)}, u32[]{:S(2)}) collective-permute-start(f32[128,32]{0,1:T(8,128)S(1)} %pad_maximum_fusion), channel_id=1, source_target_pairs={{0,3},{1,0},{2,1},{3,2},{4,7},{5,4},{6,5},{7,6},{8,11},{9,8},{10,9... | collective-permute-start | bytes 49160 | tf_op jit(solution)/shard_map/ppermute | solution.py:200
  13.1 1.0 collective-permute-start
  14.1 0.4 collective-permute-done.2
  14.5 0.5 collective-permute-start.6
  15.1 2.7 %collective-permute-done.1 = f32[128,32]{0,1:T(8,128)S(1)} collective-permute-done((f32[128,32]{0,1:T(8,128)S(1)}, f32[128,32]{0,1:T(8,128)S(1)}, u32[]{:S(2)}, u32[]{:S(2)}) %collective-permute-start.1) | collective-permute-done | bytes 16416 | tf_op jit(solution)/shard_map/ppermute | solution.py:200
  17.7 0.9 collective-permute-done
  19.1 0.7 reshape.19
  19.8 0.7 reshape.18
  20.5 15.9 %local_part.1 = (f32[512,2048]{1,0:T(8,128)}, bf16[16,16,128]{2,1,0:T(8,128)(2,1)}) custom-call(bf16[512,2048]{1,0:T(8,128)(2,1)} %gate_ref.1, bf16[512,2048]{1,0:T(8,128)(2,1)} %outer_ref.3, bf16[512,2048]{1,0:T(8,128)(2,1)} %value_ref.1, f32[16,1,128]{2,1,0:T(1,128)} %bitcast.8, f32[16,1,128]{2,1,0:T(1,128)} %bitcast.12, f32[16,1,128]{2,1,0:T(1,128)} %bitcast.14), custom_call_target="tpu_custom_call" | custom-call | flops 4294967296 | bytes 10485760 | tf_op jit(solution)/shard_map/local_part/pallas_call | solution.py:232
  36.4 0.6 pad_add_fusion.place_ref
  37.0 0.9 collective-permute-done.3.other_ref
  37.9 0.6 copy-done
  38.5 1.6 shard_map.113.pair_ref
  40.1 0.9 collective-permute-start.4
  41.0 3.6 %collective-permute-done.4.far_ref = bf16[16,16,128]{2,1,0:T(8,128)(2,1)S(1)} collective-permute-done((bf16[16,16,128]{2,1,0:T(8,128)(2,1)}, bf16[16,16,128]{2,1,0:T(8,128)(2,1)S(1)}, u32[]{:S(2)}, u32[]{:S(2)}) %collective-permute-start.4) | collective-permute-done | bytes 65568 | tf_op jit(solution)/shard_map/ppermute | solution.py:555
  44.5 0.5 collective-permute-start.8
  45.1 3.4 %pack.5 = (bf16[1536,128]{1,0:T(8,128)(2,1)}, bf16[1536,128]{1,0:T(8,128)(2,1)}, bf16[1536,128]{1,0:T(8,128)(2,1)}, bf16[1536,128]{1,0:T(8,128)(2,1)}, bf16[1536...) custom-call(s32[1]{0:T(128)} %bitcast.place_ref, ...), custom_call_target="tpu_custom_call" | custom-call | bytes 6291456 | tf_op jit(solution)/shard_map/pack/pallas_call | solution.py:324
  48.5 2.1 %collective-permute-start.11 = (bf16[1536,128]{1,0:T(8,128)(2,1)}, bf16[1536,128]{1,0:T(8,128)(2,1)S(1)}, u32[]{:S(2)}, u32[]{:S(2)}) collective-permute-start(bf16[1536,128]{1,0:T(8,128)(2,1)} %get-tuple-element.46), channel_id=1, source_target_pairs={{0,28},{4,24},{8,20},{12,16},{16,12},{20,8},{24,4},{28,0},{1,29},{... | collective-permute-start | bytes 1179656 | tf_op jit(solution)/shard_map/ppermute | solution.py:555
  50.6 1.1 collective-permute-start.13
  51.7 13.5 %collective-permute-done.8.refs_4_ = bf16[1536,128]{1,0:T(8,128)(2,1)} collective-permute-done((bf16[1536,128]{1,0:T(8,128)(2,1)}, bf16[1536,128]{1,0:T(8,128)(2,1)}, u32[]{:S(2)}, u32[]{:S(2)}) %collective-permute-start.8) | collective-permute-done | bytes 393248 | tf_op jit(solution)/shard_map/ppermute | solution.py:555
  65.3 4.5 %collective-permute-done.9.refs_5_ = bf16[1536,128]{1,0:T(8,128)(2,1)} collective-permute-done((bf16[1536,128]{1,0:T(8,128)(2,1)}, bf16[1536,128]{1,0:T(8,128)(2,1)}, u32[]{:S(2)}, u32[]{:S(2)}) %collective-permute-start.9) | collective-permute-done | bytes 393248 | tf_op jit(solution)/shard_map/ppermute | solution.py:555
  69.8 1.5 collective-permute-start.15
  71.3 1.9 %collective-permute-start.16 = (bf16[1536,128]{1,0:T(8,128)(2,1)}, bf16[1536,128]{1,0:T(8,128)(2,1)}, u32[]{:S(2)}, u32[]{:S(2)}) collective-permute-start(bf16[1536,128]{1,0:T(8,128)(2,1)} %get-tuple-element.65), channel_id=1, source_target_pairs={{0,20},{4,16},{8,28},{12,24},{16,4},{20,0},{24,12},{28,8},{1,21},{... | collective-permute-start | bytes 1179656 | tf_op jit(solution)/shard_map/ppermute | solution.py:555
  73.2 1.5 collective-permute-start.17
  74.7 0.4 collective-permute-start.18
  75.1 37.7 %flash.2 = (bf16[512,128]{1,0:T(8,128)(2,1)}, bf16[512,128]{1,0:T(8,128)(2,1)}, bf16[512,128]{1,0:T(8,128)(2,1)}, bf16[512,128]{1,0:T(8,128)(2,1)}, bf16[512,128...) custom-call(s32[1]{0:T(128)} %bitcast.place_ref, ...), custom_call_target="tpu_custom_call" | custom-call | flops 9663676416 | bytes 4194304 | tf_op jit(solution)/shard_map/flash/pallas_call | solution.py:468
  112.8 1.6 shard_map.114
  114.5 1.4 collective-permute-start.20
  115.9 1.7 collective-permute-start.21
  117.6 1.0 collective-permute-start.23
  118.6 1.0 collective-permute-start.19
  119.7 37.5 %flash.3 = (bf16[512,128]{1,0:T(8,128)(2,1)}, bf16[512,128]{1,0:T(8,128)(2,1)}, bf16[512,128]{1,0:T(8,128)(2,1)}, bf16[512,128]{1,0:T(8,128)(2,1)}, bf16[512,128...) custom-call(s32[1]{0:T(128)} %bitcast.place_ref, ...), custom_call_target="tpu_custom_call" | custom-call | flops 9663676416 | bytes 4194304 | tf_op jit(solution)/shard_map/flash/pallas_call | solution.py:468
  157.2 1.1 collective-permute-start.24
  158.3 1.9 %collective-permute-start.25 = (bf16[512,128]{1,0:T(8,128)(2,1)}, bf16[512,128]{1,0:T(8,128)(2,1)S(1)}, u32[]{:S(2)}, u32[]{:S(2)}) collective-permute-start(bf16[512,128]{1,0:T(8,128)(2,1)} %get-tuple-element.76), channel_id=1, source_target_pairs={{0,24},{4,28},{8,16},{12,20},{16,8},{20,12},{24,0},{28,4},{1,25},{... | collective-permute-start | bytes 393224 | tf_op jit(solution)/shard_map/ppermute | solution.py:555
  160.2 0.9 collective-permute-start.26
  161.4 1.9 %collective-permute-start.28 = (bf16[512,128]{1,0:T(8,128)(2,1)}, bf16[512,128]{1,0:T(8,128)(2,1)}, u32[]{:S(2)}, u32[]{:S(2)}) collective-permute-start(bf16[512,128]{1,0:T(8,128)(2,1)} %get-tuple-element.80), channel_id=1, source_target_pairs={{0,8},{4,12},{8,0},{12,4},{16,24},{20,28},{24,16},{28,20},{1,9},{5... | collective-permute-start | bytes 393224 | tf_op jit(solution)/shard_map/ppermute | solution.py:555
  163.3 5.4 %collective-permute-done.24.refs_5_ = bf16[512,128]{1,0:T(8,128)(2,1)S(1)} collective-permute-done((bf16[512,128]{1,0:T(8,128)(2,1)}, bf16[512,128]{1,0:T(8,128)(2,1)S(1)}, u32[]{:S(2)}, u32[]{:S(2)}) %collective-permute-start.24) | collective-permute-done | bytes 131104 | tf_op jit(solution)/shard_map/ppermute | solution.py:555
  168.7 1.6 collective-permute-start.29
  170.3 1.6 collective-permute-start.30
  171.9 1.3 collective-permute-start.32
  173.2 1.5 collective-permute-start.33
  174.7 6.4 %remote_part.1 = bf16[512,2048]{1,0:T(8,128)(2,1)} custom-call(s32[1]{0:T(128)} %bitcast.place_ref, f32[512,2048]{1,0:T(8,128)} %get-tuple-element.48.part_ref, bf16[512,2048]{1,0:T(8,128)(2,1)} %outer_ref.3, f32[16,1,128]{2,1,0:T(1,128)} %bitcast.11, f32[16,1,128]{2,1,0:T(1,128)} %bitcast.13, f32[16,16,128]{2,1,0:T(8,128)} %get-tuple-element.69.before_ref, ...), custom_call_target="tpu_custom_call" | custom-call | flops 805306368 | bytes 8388608 | tf_op jit(solution)/shard_map/remote_part/pallas_call | solution.py:255
  181.2 0.9 collective-permute-done.30.refs_12_
  182.0 1.6 collective-permute-done.31.refs_13_
  183.6 2.6 %join.1 = bf16[512,2048]{1,0:T(8,128)(2,1)} custom-call(s32[1]{0:T(128)} %bitcast.place_ref, bf16[512,128]{1,0:T(8,128)(2,1)} %get-tuple-element.56.refs_0_, bf16[512,128]{1,0:T(8,128)(2,1)} %copy-done.1, bf16[512,128]{1,0:T(8,128)(2,1)} %copy-done.2, bf16[512,128]{1,0:T(8,128)(2,1)} %copy-done.3, bf16[512,128]{1,0:T(8,128)(2,1)} %copy-done.4, ...), custom_call_target="tpu_custom_call" | custom-call | bytes 4194304 | tf_op jit(solution)/shard_map/join/pallas_call | solution.py:516
  (73 shorter events, 0.9 us)
Async XLA Ops:
  2.5 6.9 %copy-start.10 = (f32[128,16]{0,1:T(8,128)S(1)}, f32[128,16]{0,1:T(8,128)}, u32[]{:S(2)}) copy-start(f32[128,16]{0,1:T(8,128)} %param.14) | copy-start | bytes 24580
  2.5 6.9 %copy-start.11 = (f32[128,16]{0,1:T(8,128)S(1)}, f32[128,16]{0,1:T(8,128)}, u32[]{:S(2)}) copy-start(f32[128,16]{0,1:T(8,128)} %param.13) | copy-start | bytes 24580
  2.5 11.6 %copy-start.16 = (s32[128]{0:T(128)S(1)}, s32[128]{0:T(128)}, u32[]{:S(2)}) copy-start(s32[128]{0:T(128)} %param.16) | copy-start | bytes 1540
  2.5 42.6 %collective-permute-start.10 = (bf16[1536,128]{1,0:T(8,128)(2,1)}, bf16[1536,128]{1,0:T(8,128)(2,1)S(1)}, u32[]{:S(2)}, u32[]{:S(2)}) collective-permute-start(bf16[1536,128]{1,0:T(8,128)(2,1)} %pack.3), channel_id=1, source_target_pairs={{0,24},{4,28},{8,16},{12,20},{16,8},{20,12},{24,0},{28,4},{1,25},{... | collective-permute-start | bytes 1179656 | tf_op jit(solution)/shard_map/ppermute | solution.py:555
  9.4 5.1 %collective-permute-start.2 = (f32[128,32]{0,1:T(8,128)S(1)}, f32[128,32]{0,1:T(8,128)S(1)}, u32[]{:S(2)}, u32[]{:S(2)}) collective-permute-start(f32[128,32]{0,1:T(8,128)S(1)} %pad_maximum_fusion), channel_id=1, source_target_pairs={{0,3},{1,0},{2,1},{3,2},{4,7},{5,4},{6,5},{7,6},{8,11},{9,8},{10,9... | collective-permute-start | bytes 49160 | tf_op jit(solution)/shard_map/ppermute | solution.py:200
  13.1 4.6 %collective-permute-start.1 = (f32[128,32]{0,1:T(8,128)S(1)}, f32[128,32]{0,1:T(8,128)S(1)}, u32[]{:S(2)}, u32[]{:S(2)}) collective-permute-start(f32[128,32]{0,1:T(8,128)S(1)} %pad_maximum_fusion), channel_id=1, source_target_pairs={{0,2},{1,3},{2,0},{3,1},{4,6},{5,7},{6,4},{7,5},{8,10},{9,11},{10,... | collective-permute-start | bytes 49160 | tf_op jit(solution)/shard_map/ppermute | solution.py:200
  13.1 5.5 %collective-permute-start = (f32[128,32]{0,1:T(8,128)S(1)}, f32[128,32]{0,1:T(8,128)S(1)}, u32[]{:S(2)}, u32[]{:S(2)}) collective-permute-start(f32[128,32]{0,1:T(8,128)S(1)} %pad_maximum_fusion), channel_id=1, source_target_pairs={{0,1},{1,2},{2,3},{3,0},{4,5},{5,6},{6,7},{7,4},{8,9},{9,10},{10,1... | collective-permute-start | bytes 49160 | tf_op jit(solution)/shard_map/ppermute | solution.py:200
  14.1 34.4 %collective-permute-start.5 = (bf16[1536,128]{1,0:T(8,128)(2,1)}, bf16[1536,128]{1,0:T(8,128)(2,1)S(1)}, u32[]{:S(2)}, u32[]{:S(2)}) collective-permute-start(bf16[1536,128]{1,0:T(8,128)(2,1)} %get-tuple-element.51), channel_id=1, source_target_pairs={{0,4},{4,0},{8,12},{12,8},{16,20},{20,16},{24,28},{28,24},{1,5},{5... | collective-permute-start | bytes 1179656 | tf_op jit(solution)/shard_map/ppermute | solution.py:555
  14.5 36.1 %collective-permute-start.6 = (bf16[1536,128]{1,0:T(8,128)(2,1)}, bf16[1536,128]{1,0:T(8,128)(2,1)}, u32[]{:S(2)}, u32[]{:S(2)}) collective-permute-start(bf16[1536,128]{1,0:T(8,128)(2,1)} %get-tuple-element.52), channel_id=1, source_target_pairs={{0,8},{4,12},{8,0},{12,4},{16,24},{20,28},{24,16},{28,20},{1,9},{5... | collective-permute-start | bytes 1179656 | tf_op jit(solution)/shard_map/ppermute | solution.py:555
  17.7 32.9 %collective-permute-start.7 = (bf16[1536,128]{1,0:T(8,128)(2,1)}, bf16[1536,128]{1,0:T(8,128)(2,1)}, u32[]{:S(2)}, u32[]{:S(2)}) collective-permute-start(bf16[1536,128]{1,0:T(8,128)(2,1)} %get-tuple-element.53), channel_id=1, source_target_pairs={{0,12},{4,8},{8,4},{12,0},{16,28},{20,24},{24,20},{28,16},{1,13},{... | collective-permute-start | bytes 1179656 | tf_op jit(solution)/shard_map/ppermute | solution.py:555
  36.4 1.5 collective-permute-start.3
  40.1 4.5 %collective-permute-start.4 = (bf16[16,16,128]{2,1,0:T(8,128)(2,1)}, bf16[16,16,128]{2,1,0:T(8,128)(2,1)S(1)}, u32[]{:S(2)}, u32[]{:S(2)}) collective-permute-start(bf16[16,16,128]{2,1,0:T(8,128)(2,1)} %shard_map.113.pair_ref), channel_id=1, source_target_pairs={{0,8},{4,12},{8,0},{12,4},{16,24},{20,28},{24,16},{28,20},{1,9},{5... | collective-permute-start | bytes 196616 | tf_op jit(solution)/shard_map/ppermute | solution.py:555
  44.5 3.9 %copy-start.9 = (bf16[16,16,128]{2,1,0:T(8,128)(2,1)}, bf16[16,16,128]{2,1,0:T(8,128)(2,1)S(1)}, u32[]{:S(2)}) copy-start(bf16[16,16,128]{2,1,0:T(8,128)(2,1)S(1)} %collective-permute-done.4.far_ref) | copy-start | bytes 196612
  44.5 20.7 %collective-permute-start.8 = (bf16[1536,128]{1,0:T(8,128)(2,1)}, bf16[1536,128]{1,0:T(8,128)(2,1)}, u32[]{:S(2)}, u32[]{:S(2)}) collective-permute-start(bf16[1536,128]{1,0:T(8,128)(2,1)} %get-tuple-element.54), channel_id=1, source_target_pairs={{0,16},{4,20},{8,24},{12,28},{16,0},{20,4},{24,8},{28,12},{1,17},{... | collective-permute-start | bytes 1179656 | tf_op jit(solution)/shard_map/ppermute | solution.py:555
  45.1 24.7 %collective-permute-start.9 = (bf16[1536,128]{1,0:T(8,128)(2,1)}, bf16[1536,128]{1,0:T(8,128)(2,1)}, u32[]{:S(2)}, u32[]{:S(2)}) collective-permute-start(bf16[1536,128]{1,0:T(8,128)(2,1)} %get-tuple-element.55), channel_id=1, source_target_pairs={{0,20},{4,16},{8,28},{12,24},{16,4},{20,0},{24,12},{28,8},{1,21},{... | collective-permute-start | bytes 1179656 | tf_op jit(solution)/shard_map/ppermute | solution.py:555
  48.5 26.6 %copy-start.13 = (bf16[1536,128]{1,0:T(8,128)(2,1)}, bf16[1536,128]{1,0:T(8,128)(2,1)S(1)}, u32[]{:S(2)}) copy-start(bf16[1536,128]{1,0:T(8,128)(2,1)S(1)} %collective-permute-done.5.refs_1_) | copy-start | bytes 1179652
  48.5 22.8 %collective-permute-start.11 = (bf16[1536,128]{1,0:T(8,128)(2,1)}, bf16[1536,128]{1,0:T(8,128)(2,1)S(1)}, u32[]{:S(2)}, u32[]{:S(2)}) collective-permute-start(bf16[1536,128]{1,0:T(8,128)(2,1)} %get-tuple-element.46), channel_id=1, source_target_pairs={{0,28},{4,24},{8,20},{12,16},{16,12},{20,8},{24,4},{28,0},{1,29},{... | collective-permute-start | bytes 1179656 | tf_op jit(solution)/shard_map/ppermute | solution.py:555
  50.6 22.6 %collective-permute-start.12 = (bf16[1536,128]{1,0:T(8,128)(2,1)}, bf16[1536,128]{1,0:T(8,128)(2,1)S(1)}, u32[]{:S(2)}, u32[]{:S(2)}) collective-permute-start(bf16[1536,128]{1,0:T(8,128)(2,1)} %get-tuple-element.61), channel_id=1, source_target_pairs={{0,4},{4,0},{8,12},{12,8},{16,20},{20,16},{24,28},{28,24},{1,5},{5... | collective-permute-start | bytes 1179656 | tf_op jit(solution)/shard_map/ppermute | solution.py:555
  50.6 24.1 %collective-permute-start.13 = (bf16[1536,128]{1,0:T(8,128)(2,1)}, bf16[1536,128]{1,0:T(8,128)(2,1)}, u32[]{:S(2)}, u32[]{:S(2)}) collective-permute-start(bf16[1536,128]{1,0:T(8,128)(2,1)} %get-tuple-element.62), channel_id=1, source_target_pairs={{0,8},{4,12},{8,0},{12,4},{16,24},{20,28},{24,16},{28,20},{1,9},{5... | collective-permute-start | bytes 1179656 | tf_op jit(solution)/shard_map/ppermute | solution.py:555
  65.3 49.2 %collective-permute-start.14 = (bf16[1536,128]{1,0:T(8,128)(2,1)}, bf16[1536,128]{1,0:T(8,128)(2,1)}, u32[]{:S(2)}, u32[]{:S(2)}) collective-permute-start(bf16[1536,128]{1,0:T(8,128)(2,1)} %get-tuple-element.63), channel_id=1, source_target_pairs={{0,12},{4,8},{8,4},{12,0},{16,28},{20,24},{24,20},{28,16},{1,13},{... | collective-permute-start | bytes 1179656 | tf_op jit(solution)/shard_map/ppermute | solution.py:555
  69.8 46.1 %collective-permute-start.15 = (bf16[1536,128]{1,0:T(8,128)(2,1)}, bf16[1536,128]{1,0:T(8,128)(2,1)}, u32[]{:S(2)}, u32[]{:S(2)}) collective-permute-start(bf16[1536,128]{1,0:T(8,128)(2,1)} %get-tuple-element.64), channel_id=1, source_target_pairs={{0,16},{4,20},{8,24},{12,28},{16,0},{20,4},{24,8},{28,12},{1,17},{... | collective-permute-start | bytes 1179656 | tf_op jit(solution)/shard_map/ppermute | solution.py:555
  71.3 46.3 %collective-permute-start.16 = (bf16[1536,128]{1,0:T(8,128)(2,1)}, bf16[1536,128]{1,0:T(8,128)(2,1)}, u32[]{:S(2)}, u32[]{:S(2)}) collective-permute-start(bf16[1536,128]{1,0:T(8,128)(2,1)} %get-tuple-element.65), channel_id=1, source_target_pairs={{0,20},{4,16},{8,28},{12,24},{16,4},{20,0},{24,12},{28,8},{1,21},{... | collective-permute-start | bytes 1179656 | tf_op jit(solution)/shard_map/ppermute | solution.py:555
  73.2 39.6 %copy-start.14 = (bf16[1536,128]{1,0:T(8,128)(2,1)}, bf16[1536,128]{1,0:T(8,128)(2,1)S(1)}, u32[]{:S(2)}) copy-start(bf16[1536,128]{1,0:T(8,128)(2,1)S(1)} %collective-permute-done.12.refs_1_) | copy-start | bytes 1179652
  73.2 44.4 %collective-permute-start.17 = (bf16[1536,128]{1,0:T(8,128)(2,1)}, bf16[1536,128]{1,0:T(8,128)(2,1)}, u32[]{:S(2)}, u32[]{:S(2)}) collective-permute-start(bf16[1536,128]{1,0:T(8,128)(2,1)} %get-tuple-element.66), channel_id=1, source_target_pairs={{0,24},{4,28},{8,16},{12,20},{16,8},{20,12},{24,0},{28,4},{1,25},{... | collective-permute-start | bytes 1179656 | tf_op jit(solution)/shard_map/ppermute | solution.py:555
  74.7 43.9 %collective-permute-start.18 = (bf16[1536,128]{1,0:T(8,128)(2,1)}, bf16[1536,128]{1,0:T(8,128)(2,1)}, u32[]{:S(2)}, u32[]{:S(2)}) collective-permute-start(bf16[1536,128]{1,0:T(8,128)(2,1)} %get-tuple-element.67), channel_id=1, source_target_pairs={{0,28},{4,24},{8,20},{12,16},{16,12},{20,8},{24,4},{28,0},{1,29},{... | collective-permute-start | bytes 1179656 | tf_op jit(solution)/shard_map/ppermute | solution.py:555
  114.5 43.8 %collective-permute-start.20 = (bf16[512,128]{1,0:T(8,128)(2,1)}, bf16[512,128]{1,0:T(8,128)(2,1)S(1)}, u32[]{:S(2)}, u32[]{:S(2)}) collective-permute-start(bf16[512,128]{1,0:T(8,128)(2,1)} %get-tuple-element.71), channel_id=1, source_target_pairs={{0,4},{4,0},{8,12},{12,8},{16,20},{20,16},{24,28},{28,24},{1,5},{5... | collective-permute-start | bytes 393224 | tf_op jit(solution)/shard_map/ppermute | solution.py:555
  115.9 44.4 %collective-permute-start.21 = (bf16[512,128]{1,0:T(8,128)(2,1)}, bf16[512,128]{1,0:T(8,128)(2,1)S(1)}, u32[]{:S(2)}, u32[]{:S(2)}) collective-permute-start(bf16[512,128]{1,0:T(8,128)(2,1)} %get-tuple-element.72), channel_id=1, source_target_pairs={{0,8},{4,12},{8,0},{12,4},{16,24},{20,28},{24,16},{28,20},{1,9},{5... | collective-permute-start | bytes 393224 | tf_op jit(solution)/shard_map/ppermute | solution.py:555
  117.6 43.5 %collective-permute-start.22 = (bf16[512,128]{1,0:T(8,128)(2,1)}, bf16[512,128]{1,0:T(8,128)(2,1)S(1)}, u32[]{:S(2)}, u32[]{:S(2)}) collective-permute-start(bf16[512,128]{1,0:T(8,128)(2,1)} %get-tuple-element.73), channel_id=1, source_target_pairs={{0,12},{4,8},{8,4},{12,0},{16,28},{20,24},{24,20},{28,16},{1,13},{... | collective-permute-start | bytes 393224 | tf_op jit(solution)/shard_map/ppermute | solution.py:555
  117.6 43.8 %collective-permute-start.23 = (bf16[512,128]{1,0:T(8,128)(2,1)}, bf16[512,128]{1,0:T(8,128)(2,1)S(1)}, u32[]{:S(2)}, u32[]{:S(2)}) collective-permute-start(bf16[512,128]{1,0:T(8,128)(2,1)} %get-tuple-element.74), channel_id=1, source_target_pairs={{0,16},{4,20},{8,24},{12,28},{16,0},{20,4},{24,8},{28,12},{1,17},{... | collective-permute-start | bytes 393224 | tf_op jit(solution)/shard_map/ppermute | solution.py:555
  118.6 38.5 %collective-permute-start.19 = (bf16[16,16,128]{2,1,0:T(8,128)(2,1)}, bf16[16,16,128]{2,1,0:T(8,128)(2,1)S(1)}, u32[]{:S(2)}, u32[]{:S(2)}) collective-permute-start(bf16[16,16,128]{2,1,0:T(8,128)(2,1)} %get-tuple-element.70), channel_id=1, source_target_pairs={{0,16},{4,20},{8,24},{12,28},{16,0},{20,4},{24,8},{28,12},{1,17},{... | collective-permute-start | bytes 196616 | tf_op jit(solution)/shard_map/ppermute | solution.py:555
  157.2 17.5 %copy-start.8 = (bf16[16,16,128]{2,1,0:T(8,128)(2,1)}, bf16[16,16,128]{2,1,0:T(8,128)(2,1)S(1)}, u32[]{:S(2)}) copy-start(bf16[16,16,128]{2,1,0:T(8,128)(2,1)S(1)} %collective-permute-done.19.other_ref) | copy-start | bytes 196612
  157.2 11.5 %collective-permute-start.24 = (bf16[512,128]{1,0:T(8,128)(2,1)}, bf16[512,128]{1,0:T(8,128)(2,1)S(1)}, u32[]{:S(2)}, u32[]{:S(2)}) collective-permute-start(bf16[512,128]{1,0:T(8,128)(2,1)} %get-tuple-element.75), channel_id=1, source_target_pairs={{0,20},{4,16},{8,28},{12,24},{16,4},{20,0},{24,12},{28,8},{1,21},{... | collective-permute-start | bytes 393224 | tf_op jit(solution)/shard_map/ppermute | solution.py:555
  158.3 22.8 %copy-start.1 = (bf16[512,128]{1,0:T(8,128)(2,1)}, bf16[512,128]{1,0:T(8,128)(2,1)S(1)}, u32[]{:S(2)}) copy-start(bf16[512,128]{1,0:T(8,128)(2,1)S(1)} %collective-permute-done.20.refs_1_) | copy-start | bytes 393220
  158.3 12.0 %collective-permute-start.25 = (bf16[512,128]{1,0:T(8,128)(2,1)}, bf16[512,128]{1,0:T(8,128)(2,1)S(1)}, u32[]{:S(2)}, u32[]{:S(2)}) collective-permute-start(bf16[512,128]{1,0:T(8,128)(2,1)} %get-tuple-element.76), channel_id=1, source_target_pairs={{0,24},{4,28},{8,16},{12,20},{16,8},{20,12},{24,0},{28,4},{1,25},{... | collective-permute-start | bytes 393224 | tf_op jit(solution)/shard_map/ppermute | solution.py:555
  160.2 20.9 %copy-start.2 = (bf16[512,128]{1,0:T(8,128)(2,1)}, bf16[512,128]{1,0:T(8,128)(2,1)S(1)}, u32[]{:S(2)}) copy-start(bf16[512,128]{1,0:T(8,128)(2,1)S(1)} %collective-permute-done.21.refs_2_) | copy-start | bytes 393220
  160.2 11.7 %collective-permute-start.26 = (bf16[512,128]{1,0:T(8,128)(2,1)}, bf16[512,128]{1,0:T(8,128)(2,1)S(1)}, u32[]{:S(2)}, u32[]{:S(2)}) collective-permute-start(bf16[512,128]{1,0:T(8,128)(2,1)} %get-tuple-element.77), channel_id=1, source_target_pairs={{0,28},{4,24},{8,20},{12,16},{16,12},{20,8},{24,4},{28,0},{1,29},{... | collective-permute-start | bytes 393224 | tf_op jit(solution)/shard_map/ppermute | solution.py:555
  161.1 20.0 %copy-start.3 = (bf16[512,128]{1,0:T(8,128)(2,1)}, bf16[512,128]{1,0:T(8,128)(2,1)S(1)}, u32[]{:S(2)}) copy-start(bf16[512,128]{1,0:T(8,128)(2,1)S(1)} %collective-permute-done.22.refs_3_) | copy-start | bytes 393220
  161.1 10.8 %collective-permute-start.27 = (bf16[512,128]{1,0:T(8,128)(2,1)}, bf16[512,128]{1,0:T(8,128)(2,1)}, u32[]{:S(2)}, u32[]{:S(2)}) collective-permute-start(bf16[512,128]{1,0:T(8,128)(2,1)} %get-tuple-element.79), channel_id=1, source_target_pairs={{0,4},{4,0},{8,12},{12,8},{16,20},{20,16},{24,28},{28,24},{1,5},{5... | collective-permute-start | bytes 393224 | tf_op jit(solution)/shard_map/ppermute | solution.py:555
  161.4 19.7 %copy-start.4 = (bf16[512,128]{1,0:T(8,128)(2,1)}, bf16[512,128]{1,0:T(8,128)(2,1)S(1)}, u32[]{:S(2)}) copy-start(bf16[512,128]{1,0:T(8,128)(2,1)S(1)} %collective-permute-done.23.refs_4_) | copy-start | bytes 393220
  161.4 11.8 %collective-permute-start.28 = (bf16[512,128]{1,0:T(8,128)(2,1)}, bf16[512,128]{1,0:T(8,128)(2,1)}, u32[]{:S(2)}, u32[]{:S(2)}) collective-permute-start(bf16[512,128]{1,0:T(8,128)(2,1)} %get-tuple-element.80), channel_id=1, source_target_pairs={{0,8},{4,12},{8,0},{12,4},{16,24},{20,28},{24,16},{28,20},{1,9},{5... | collective-permute-start | bytes 393224 | tf_op jit(solution)/shard_map/ppermute | solution.py:555
  168.7 12.4 %copy-start.5 = (bf16[512,128]{1,0:T(8,128)(2,1)}, bf16[512,128]{1,0:T(8,128)(2,1)S(1)}, u32[]{:S(2)}) copy-start(bf16[512,128]{1,0:T(8,128)(2,1)S(1)} %collective-permute-done.24.refs_5_) | copy-start | bytes 393220
  168.7 12.4 %collective-permute-start.29 = (bf16[512,128]{1,0:T(8,128)(2,1)}, bf16[512,128]{1,0:T(8,128)(2,1)}, u32[]{:S(2)}, u32[]{:S(2)}) collective-permute-start(bf16[512,128]{1,0:T(8,128)(2,1)} %get-tuple-element.81), channel_id=1, source_target_pairs={{0,12},{4,8},{8,4},{12,0},{16,28},{20,24},{24,20},{28,16},{1,13},{... | collective-permute-start | bytes 393224 | tf_op jit(solution)/shard_map/ppermute | solution.py:555
  170.3 10.8 %copy-start.6 = (bf16[512,128]{1,0:T(8,128)(2,1)}, bf16[512,128]{1,0:T(8,128)(2,1)S(1)}, u32[]{:S(2)}) copy-start(bf16[512,128]{1,0:T(8,128)(2,1)S(1)} %collective-permute-done.25.refs_6_) | copy-start | bytes 393220
  170.3 11.7 %collective-permute-start.30 = (bf16[512,128]{1,0:T(8,128)(2,1)}, bf16[512,128]{1,0:T(8,128)(2,1)}, u32[]{:S(2)}, u32[]{:S(2)}) collective-permute-start(bf16[512,128]{1,0:T(8,128)(2,1)} %get-tuple-element.82), channel_id=1, source_target_pairs={{0,16},{4,20},{8,24},{12,28},{16,0},{20,4},{24,8},{28,12},{1,17},{... | collective-permute-start | bytes 393224 | tf_op jit(solution)/shard_map/ppermute | solution.py:555
  171.9 9.2 %copy-start.7 = (bf16[512,128]{1,0:T(8,128)(2,1)}, bf16[512,128]{1,0:T(8,128)(2,1)S(1)}, u32[]{:S(2)}) copy-start(bf16[512,128]{1,0:T(8,128)(2,1)S(1)} %collective-permute-done.26.refs_7_) | copy-start | bytes 393220
  171.9 11.7 %collective-permute-start.31 = (bf16[512,128]{1,0:T(8,128)(2,1)}, bf16[512,128]{1,0:T(8,128)(2,1)}, u32[]{:S(2)}, u32[]{:S(2)}) collective-permute-start(bf16[512,128]{1,0:T(8,128)(2,1)} %get-tuple-element.83), channel_id=1, source_target_pairs={{0,20},{4,16},{8,28},{12,24},{16,4},{20,0},{24,12},{28,8},{1,21},{... | collective-permute-start | bytes 393224 | tf_op jit(solution)/shard_map/ppermute | solution.py:555
  171.9 11.7 %collective-permute-start.32 = (bf16[512,128]{1,0:T(8,128)(2,1)}, bf16[512,128]{1,0:T(8,128)(2,1)}, u32[]{:S(2)}, u32[]{:S(2)}) collective-permute-start(bf16[512,128]{1,0:T(8,128)(2,1)} %get-tuple-element.84), channel_id=1, source_target_pairs={{0,24},{4,28},{8,16},{12,20},{16,8},{20,12},{24,0},{28,4},{1,25},{... | collective-permute-start | bytes 393224 | tf_op jit(solution)/shard_map/ppermute | solution.py:555
  173.2 10.4 %collective-permute-start.33 = (bf16[512,128]{1,0:T(8,128)(2,1)}, bf16[512,128]{1,0:T(8,128)(2,1)}, u32[]{:S(2)}, u32[]{:S(2)}) collective-permute-start(bf16[512,128]{1,0:T(8,128)(2,1)} %get-tuple-element.85), channel_id=1, source_target_pairs={{0,28},{4,24},{8,20},{12,16},{16,12},{20,8},{24,4},{28,0},{1,29},{... | collective-permute-start | bytes 393224 | tf_op jit(solution)/shard_map/ppermute | solution.py:555
  (3 other events, 6.0 us)
